TPU v7x, 32 devices: a whole 2x2x4 slice. The times are simulated.
32 devices in a mesh: page: 8 (over y, x, core), blk: 4 (over z).
Axes of the slice: x: 2, y: 2, z: 4, core: 2. Of those that a mesh axis runs over, the one named last changes fastest.
Arguments:
- tokens: bfloat16 [8, 2048, 1024], P('page', 'blk'), may hold values from -6 to 6
- patches: bfloat16 [8, 1024, 1024], P('page', 'blk'), may hold values from -6 to 6
- patch_mask: int32 [8, 1024], P('page', 'blk'), may hold values from 0 to 1, as said below
- gain_one: float32 [1024], replicated, may hold values from 0.1 to 1.9
- qkv_self: bfloat16 [1024, 3072], replicated, may hold values from -0.1875 to 0.1875
- out_self: bfloat16 [1024, 1024], replicated, may hold values from -1.5 to 1.5
- gain_two: float32 [1024], replicated, may hold values from 0.1 to 1.9
- q_cross: bfloat16 [1024, 1024], replicated, may hold values from -0.1875 to 0.1875
- kv_cross: bfloat16 [1024, 2048], replicated, may hold values from -0.1875 to 0.1875
- out_cross: bfloat16 [1024, 1024], replicated, may hold values from -1.5 to 1.5
- gain_three: float32 [1024], replicated, may hold values from 0.1 to 1.9
- w_up: bfloat16 [1024, 4096], replicated, may hold values from -0.1875 to 0.1875
- w_down: bfloat16 [4096, 1024], replicated, may hold values from -0.09375 to 0.09375
- cotangent: bfloat16 [8, 2048, 1024], P('page', 'blk'), may hold values from -6 to 6
Outputs:
- output: bfloat16 [8, 2048, 1024], P('page', 'blk')
- grad_tokens: float32 [8, 2048, 1024], P('page', 'blk')
- grad_patches: float32 [8, 1024, 1024], P('page', 'blk')
- grad_gain_one: float32 [1024], replicated
- grad_qkv_self: float32 [1024, 3072], P('page', 'blk')
- grad_out_self: float32 [1024, 1024], P('page', 'blk')
- grad_gain_two: float32 [1024], replicated
- grad_q_cross: float32 [1024, 1024], P('page', 'blk')
- grad_kv_cross: float32 [1024, 2048], P('page', 'blk')
- grad_out_cross: float32 [1024, 1024], P('page', 'blk')
- grad_gain_three: float32 [1024], replicated
- grad_w_up: float32 [1024, 4096], P('page', 'blk')
- grad_w_down: float32 [4096, 1024], P('page', 'blk')
Inputs may be any that keep to these rules, and one draw needn't show every extreme that they name: `patch_mask`: 1 keeps a patch and 0 excludes it; the excluded patches of a page form one rectangle of its grid of 16 rows and 64 columns, of at most half of the rows and at most 32 columns.
All inputs are finite; a program needn't handle non-finite values.
Results may differ from a plain program's by a relative error of at most 0.025.
Values may be sent and summed in bfloat16 or wider, within the bound.
No kernel may reach another device: no remote copies, remote signals or barrier semaphores. Data moves between devices by JAX's collectives and lax.ppermute only.
A program may use at most 384 MiB of HBM per device.

v0:
```python
import jax
import jax.numpy as jnp
from jax import lax
from jax.sharding import PartitionSpec as P

HEADS = 16
HEAD_DIM = 64


norm_eps = 1e-05
masked_score = -1e30


def product(left, right):
    return jnp.dot(left, right, preferred_element_type=jnp.float32)


def inner_rows(left, right):
    return lax.dot_general(
        left, right, (((0,), (0,)), ((), ())), preferred_element_type=jnp.float32
    )


def times_transposed(left, right):
    return lax.dot_general(
        left, right, (((1,), (1,)), ((), ())), preferred_element_type=jnp.float32
    )


def layer_norm(values, gain_row):
    center = values - jnp.mean(values, axis=-1, keepdims=True)
    variance = jnp.mean(center * center, axis=-1, keepdims=True)
    return center * lax.rsqrt(variance + norm_eps) * gain_row


def exact_gelu(values):
    return jax.nn.gelu(values, approximate=False)


def head_split(matrix):
    return matrix.reshape(matrix.shape[0], HEADS, HEAD_DIM)


def attend_page(queries, key_rows, value_rows, allowed):
    score_scale = HEAD_DIM ** (-0.5)
    scores = (
        jnp.einsum(
            "qhd,khd->hqk",
            head_split(queries),
            head_split(key_rows),
            preferred_element_type=jnp.float32,
        )
        * score_scale
    )
    scores = jnp.where(allowed[None], scores, masked_score)
    largest = jnp.max(scores, axis=-1, keepdims=True)
    raised = jnp.exp(scores - largest)
    totals = jnp.sum(raised, axis=-1, keepdims=True)
    shares = (raised / totals).astype(jnp.bfloat16)
    blended = jnp.einsum(
        "hqk,khd->qhd", shares, head_split(value_rows), preferred_element_type=jnp.float32
    )
    log_totals = (largest + jnp.log(totals))[..., 0]
    return (blended.reshape(queries.shape[0], -1).astype(jnp.bfloat16), log_totals)


def shares_and_grads(queries, key_rows, value_rows, allowed, log_totals, d_blended):
    score_scale = HEAD_DIM ** (-0.5)
    scores = (
        jnp.einsum(
            "qhd,khd->hqk",
            head_split(queries),
            head_split(key_rows),
            preferred_element_type=jnp.float32,
        )
        * score_scale
    )
    scores = jnp.where(allowed[None], scores, masked_score)
    shares = jnp.exp(scores - log_totals[..., None])
    d_shares = jnp.einsum(
        "qhd,khd->hqk",
        head_split(d_blended),
        head_split(value_rows),
        preferred_element_type=jnp.float32,
    )
    return (shares, d_shares)


def key_side(queries, d_blended, shares, d_scores):
    score_scale = HEAD_DIM ** (-0.5)
    d_key = (
        jnp.einsum(
            "hqk,qhd->khd", d_scores, head_split(queries), preferred_element_type=jnp.float32
        )
        * score_scale
    )
    d_value = jnp.einsum(
        "hqk,qhd->khd",
        shares.astype(jnp.bfloat16),
        head_split(d_blended),
        preferred_element_type=jnp.float32,
    )
    key_count = d_key.shape[0]
    return jnp.concatenate([d_key.reshape(key_count, -1), d_value.reshape(key_count, -1)], axis=-1)


def query_side(key_rows, d_scores):
    score_scale = HEAD_DIM ** (-0.5)
    d_query = (
        jnp.einsum(
            "hqk,khd->qhd", d_scores, head_split(key_rows), preferred_element_type=jnp.float32
        )
        * score_scale
    )
    return d_query.reshape(d_query.shape[0], -1)


def attend_back(queries, key_rows, value_rows, allowed, log_totals, d_blended):
    shares, d_shares = shares_and_grads(
        queries, key_rows, value_rows, allowed, log_totals, d_blended
    )
    weighted = jnp.sum(shares * d_shares, axis=-1, keepdims=True)
    d_scores = (shares * (d_shares - weighted)).astype(jnp.bfloat16)
    return (query_side(key_rows, d_scores), key_side(queries, d_blended, shares, d_scores))


def on_device(
    tokens,
    patches,
    patch_mask,
    gain_one,
    qkv_self,
    out_self,
    gain_two,
    q_cross,
    kv_cross,
    out_cross,
    gain_three,
    w_up,
    w_down,
    cotangent,
):
    page_count, token_count, width = tokens.shape
    patch_count = patches.shape[1]
    cycle_size = lax.axis_size("blk")
    cycle_place = lax.axis_index("blk")
    flat_tokens = tokens.reshape(-1, width).astype(jnp.float32)
    normed_one, norm_back_one = jax.vjp(layer_norm, flat_tokens, gain_one)
    normed_one = normed_one.astype(jnp.bfloat16)
    packed = product(normed_one, qkv_self).astype(jnp.bfloat16)
    query_one = packed[:, :width].reshape(page_count, token_count, width)
    kv_one = packed[:, width:].reshape(page_count, token_count, 2 * width)
    flat_patches = patches.reshape(-1, width)
    pair_two = (
        product(flat_patches, kv_cross)
        .astype(jnp.bfloat16)
        .reshape(page_count, patch_count, 2 * width)
    )
    live_rows = patch_mask.astype(jnp.bfloat16)
    kept_self, kept_cross, kept_live = (
        lax.all_gather(kv_one, "blk", axis=1, tiled=True),
        lax.all_gather(pair_two, "blk", axis=1, tiled=True),
        lax.all_gather(live_rows, "blk", axis=1, tiled=True),
    )
    query_place = cycle_place * token_count + lax.iota(jnp.int32, token_count)
    key_place = lax.iota(jnp.int32, token_count * cycle_size)
    causal = query_place[:, None] >= key_place[None, :]

    def self_forward(inputs):
        page_query, page_pair = inputs
        return attend_page(page_query, page_pair[:, :width], page_pair[:, width:], causal)

    mixed_one, log_one = lax.map(self_forward, (query_one, kept_self))
    flat_mixed_one = mixed_one.reshape(-1, width)
    resid_one = flat_tokens + product(flat_mixed_one, out_self)
    normed_two, norm_back_two = jax.vjp(layer_norm, resid_one, gain_two)
    normed_two = normed_two.astype(jnp.bfloat16)
    query_two = (
        product(normed_two, q_cross).astype(jnp.bfloat16).reshape(page_count, token_count, width)
    )

    def cross_forward(inputs):
        page_query, page_pair, page_live = inputs
        return attend_page(
            page_query, page_pair[:, :width], page_pair[:, width:], page_live[None, :] > 0
        )

    mixed_two, log_two = lax.map(cross_forward, (query_two, kept_cross, kept_live))
    flat_mixed_two = mixed_two.reshape(-1, width)
    resid_two = resid_one + product(flat_mixed_two, out_cross)
    normed_three, norm_back_three = jax.vjp(layer_norm, resid_two, gain_three)
    normed_three = normed_three.astype(jnp.bfloat16)
    upward = product(normed_three, w_up)
    active, gelu_back = jax.vjp(exact_gelu, upward)
    active = active.astype(jnp.bfloat16)
    output = resid_two + product(active, w_down)
    pair_self, pair_cross, live_cross = (
        lax.all_gather(kv_one, "blk", axis=1, tiled=True),
        lax.all_gather(pair_two, "blk", axis=1, tiled=True),
        lax.all_gather(live_rows, "blk", axis=1, tiled=True),
    )
    flat_cotangent = cotangent.reshape(-1, width)
    grad_w_down = inner_rows(active, flat_cotangent)
    d_active = times_transposed(flat_cotangent, w_down)
    d_upward = gelu_back(d_active)[0].astype(jnp.bfloat16)
    grad_w_up = inner_rows(normed_three, d_upward)
    d_normed_three = times_transposed(d_upward, w_up)
    d_part_three, grad_gain_three = norm_back_three(d_normed_three)
    d_resid_two = flat_cotangent.astype(jnp.float32) + d_part_three
    branch_two = d_resid_two.astype(jnp.bfloat16)
    grad_out_cross = inner_rows(flat_mixed_two, branch_two)
    d_mixed_two = (
        times_transposed(branch_two, out_cross)
        .astype(jnp.bfloat16)
        .reshape(page_count, token_count, width)
    )

    def cross_backward(inputs):
        page_query, page_pair, page_live, page_log, page_grad = inputs
        return attend_back(
            page_query,
            page_pair[:, :width],
            page_pair[:, width:],
            page_live[None, :] > 0,
            page_log,
            page_grad,
        )

    d_query_two, cross_terms = lax.map(
        cross_backward, (query_two, pair_cross, live_cross, log_two, d_mixed_two)
    )
    d_pair_two = lax.psum_scatter(
        cross_terms.astype(jnp.bfloat16), "blk", scatter_dimension=1, tiled=True
    )
    flat_pair_grad = d_pair_two.reshape(-1, 2 * width)
    d_query_two = d_query_two.astype(jnp.bfloat16).reshape(-1, width)
    grad_q_cross = inner_rows(normed_two, d_query_two)
    grad_kv_cross = inner_rows(flat_patches, flat_pair_grad)
    grad_patches = times_transposed(flat_pair_grad, kv_cross).reshape(
        page_count, patch_count, width
    )
    d_normed_two = times_transposed(d_query_two, q_cross)
    d_part_two, grad_gain_two = norm_back_two(d_normed_two)
    d_resid_one = d_resid_two + d_part_two
    branch_one = d_resid_one.astype(jnp.bfloat16)
    grad_out_self = inner_rows(flat_mixed_one, branch_one)
    d_mixed_one = (
        times_transposed(branch_one, out_self)
        .astype(jnp.bfloat16)
        .reshape(page_count, token_count, width)
    )

    def self_backward(inputs):
        page_query, page_pair, page_log, page_grad = inputs
        return attend_back(
            page_query, page_pair[:, :width], page_pair[:, width:], causal, page_log, page_grad
        )

    d_query_one, self_terms = lax.map(self_backward, (query_one, pair_self, log_one, d_mixed_one))
    d_kv_one = lax.psum_scatter(
        self_terms.astype(jnp.bfloat16), "blk", scatter_dimension=1, tiled=True
    )
    d_packed = jnp.concatenate([d_query_one.astype(jnp.bfloat16), d_kv_one], axis=-1).reshape(
        -1, 3 * width
    )
    grad_qkv_self = inner_rows(normed_one, d_packed)
    d_normed_one = times_transposed(d_packed, qkv_self)
    d_part_one, grad_gain_one = norm_back_one(d_normed_one)
    grad_tokens = d_resid_one + d_part_one
    matrices = (
        grad_qkv_self,
        grad_out_self,
        grad_q_cross,
        grad_kv_cross,
        grad_out_cross,
        grad_w_up,
        grad_w_down,
    )
    halfway = (
        lax.psum_scatter(
            matrices[0].astype(jnp.bfloat16), "page", scatter_dimension=0, tiled=True
        ).astype(jnp.float32),
        lax.psum_scatter(
            matrices[1].astype(jnp.bfloat16), "page", scatter_dimension=0, tiled=True
        ).astype(jnp.float32),
        lax.psum_scatter(
            matrices[2].astype(jnp.bfloat16), "page", scatter_dimension=0, tiled=True
        ).astype(jnp.float32),
        lax.psum_scatter(
            matrices[3].astype(jnp.bfloat16), "page", scatter_dimension=0, tiled=True
        ).astype(jnp.float32),
        lax.psum_scatter(
            matrices[4].astype(jnp.bfloat16), "page", scatter_dimension=0, tiled=True
        ).astype(jnp.float32),
        lax.psum_scatter(
            matrices[5].astype(jnp.bfloat16), "page", scatter_dimension=0, tiled=True
        ).astype(jnp.float32),
        lax.psum_scatter(
            matrices[6].astype(jnp.bfloat16), "page", scatter_dimension=0, tiled=True
        ).astype(jnp.float32),
    )
    reduced = (
        lax.psum_scatter(
            halfway[0].astype(jnp.bfloat16), "blk", scatter_dimension=1, tiled=True
        ).astype(jnp.float32),
        lax.psum_scatter(
            halfway[1].astype(jnp.bfloat16), "blk", scatter_dimension=1, tiled=True
        ).astype(jnp.float32),
        lax.psum_scatter(
            halfway[2].astype(jnp.bfloat16), "blk", scatter_dimension=1, tiled=True
        ).astype(jnp.float32),
        lax.psum_scatter(
            halfway[3].astype(jnp.bfloat16), "blk", scatter_dimension=1, tiled=True
        ).astype(jnp.float32),
        lax.psum_scatter(
            halfway[4].astype(jnp.bfloat16), "blk", scatter_dimension=1, tiled=True
        ).astype(jnp.float32),
        lax.psum_scatter(
            halfway[5].astype(jnp.bfloat16), "blk", scatter_dimension=1, tiled=True
        ).astype(jnp.float32),
        lax.psum_scatter(
            halfway[6].astype(jnp.bfloat16), "blk", scatter_dimension=1, tiled=True
        ).astype(jnp.float32),
    )
    gain_sums = lax.psum((grad_gain_one, grad_gain_two, grad_gain_three), ("page", "blk"))
    return (
        output.astype(jnp.bfloat16).reshape(page_count, token_count, width),
        grad_tokens.reshape(page_count, token_count, width),
        grad_patches,
        gain_sums[0],
        reduced[0],
        reduced[1],
        gain_sums[1],
        reduced[2],
        reduced[3],
        reduced[4],
        gain_sums[2],
        reduced[5],
        reduced[6],
    )


def solution(mesh):
    placed = (
        P("page", "blk", None),
        P("page", "blk", None),
        P("page", "blk"),
        P(),
        P(),
        P(),
        P(),
        P(),
        P(),
        P(),
        P(),
        P(),
        P(),
        P("page", "blk", None),
    )
    return jax.shard_map(
        on_device,
        mesh=mesh,
        in_specs=placed,
        out_specs=(
            P("page", "blk", None),
            P("page", "blk", None),
            P("page", "blk", None),
            P(),
            P("page", "blk"),
            P("page", "blk"),
            P(),
            P("page", "blk"),
            P("page", "blk"),
            P("page", "blk"),
            P(),
            P("page", "blk"),
            P("page", "blk"),
        ),
        check_vma=False,
    )
```

profile of v0, /device:TPU:15, one launch (start us, length us, event | category | flops | bytes accessed | tf_op | source)
XLA Modules:
  0.0 1356.0 jit_solution(17000029020617859254)
XLA Ops:
  36.4 55.3 %all-gather.7.cloned.1.call-done = bf16[1024,2048]{1,0:T(8,128)(2,1)} async-done(((bf16[256,2048]{1,0:T(8,128)(2,1)}), bf16[1024,2048]{1,0:T(8,128)(2,1)}) %all-gather.7.cloned.1.call-update) | async-done | bytes 4194320 | tf_op jit(solution)/shard_map/all_gather | solution.py:162
  104.4 137.3 %all-gather.5.cloned.1.call-done = bf16[2048,2048]{1,0:T(8,128)(2,1)} async-done(((bf16[512,2048]{1,0:T(8,128)(2,1)}), bf16[2048,2048]{1,0:T(8,128)(2,1)}) %all-gather.5.cloned.1.call-update) | async-done | bytes 8388624 | tf_op jit(solution)/shard_map/all_gather | solution.py:161
  260.7 26.5 %fusion.81 = (f32[16,512]{1,0:T(8,128)S(1)}, f32[16,512,2048]{2,1,0:T(8,128)}) fusion(bf16[512,16,64]{0,2,1:T(8,128)(2,1)} %bitcast.161, bf16[2048,16,64]{0,2,1:T(8,128)(2,1)} %bitcast.148, pred[512,2048]{1,0:T(8,128)(4,1)} %iota_compare_fusion), kind=kOutput, calls=%fused_computation.149 | convolution fusion | flops 2197807104 | bytes 73433088 | tf_op jit(solution)/shard_map/while/body/eval_jaxpr/qhd,khd->hqk/dot_general | solution.py:47
  287.2 21.1 %fusion = f32[16,512]{1,0:T(8,128)S(1)} fusion(f32[16,512,2048]{2,1,0:T(8,128)} %get-tuple-element.156, f32[16,512]{1,0:T(8,128)S(1)} %get-tuple-element.155), kind=kLoop, calls=%fused_computation.6 | loop fusion | flops 33546240 | bytes 67174400 | tf_op jit(solution)/shard_map/while/body/eval_jaxpr/reduce_sum | solution.py:58
  308.3 25.7 %fusion.42 = bf16[16,64,512]{2,1,0:T(8,128)(2,1)} fusion(bf16[2048,16,64]{0,2,1:T(8,128)(2,1)} %bitcast.154, f32[16,512,2048]{2,1,0:T(8,128)} %get-tuple-element.156, f32[16,512]{1,0:T(8,128)S(1)} %fusion, f32[16,512]{1,0:T(8,128)S(1)} %get-tuple-element.155), kind=kOutput, calls=%fused_computation.98 | convolution fusion | flops 2198339584 | bytes 72417280 | tf_op jit(solution)/shard_map/while/body/eval_jaxpr/hqk,khd->qhd/dot_general | solution.py:60
  389.7 27.8 %multiply_convert_fusion.3 = (bf16[512,4096]{1,0:T(8,128)(2,1)}, f32[512,4096]{1,0:T(8,128)}, f32[512,4096]{1,0:T(8,128)}) fusion(bf16[1024,4096]{1,0:T(8,128)(2,1)} %param.25, f32[512,1024]{1,0:T(8,128)S(1)} %get-tuple-element.162, f32[1024]{0:T(1024)S(1)} %copy-done.47, f32[512]{0:T(512)S(1)} %fusion.67, f32[512]{0:T(512)S(1)} %broadcast_multiply_fusion), kind=kOutput, calls=%fused_computation.28 | convolution fusion | flops 4433379328 | bytes 31465472 | tf_op jit(solution)/shard_map/dot_general | solution.py:15
  462.4 24.6 %multiply_reduce_fusion.1 = (f32[16,512]{1,0:T(8,128)S(1)}, f32[16,512,1024]{2,1,0:T(8,128)}) fusion(f32[16,512]{1,0:T(8,128)S(1)} %copy-done.24, f32[16,512,1024]{2,1,0:T(8,128)} %get-tuple-element.160, pred[1024]{0:T(1024)(128)(4,1)S(1)} %compare_reduce_fusion, bf16[512,16,64]{0,2,1:T(8,128)(2,1)} %bitcast.166, bf16[1024,16,64]{0,2,1:T(8,128)(2,1)S(1)} %bitcast.159), kind=kOutput, calls=%fused_computation.11 | convolution fusion | flops 1115676672 | bytes 70321152 | tf_op jit(solution)/shard_map/while/body/eval_jaxpr/qhd,khd->hqk/dot_general | solution.py:80
  486.9 28.2 %multiply_convert_fusion.1 = bf16[16,512,1024]{2,1,0:T(8,128)(2,1)} fusion(f32[16,512,1024]{2,1,0:T(8,128)} %get-tuple-element.166, f32[16,512]{1,0:T(8,128)S(1)} %get-tuple-element.165, f32[16,512]{1,0:T(8,128)S(1)} %copy-done.24, f32[16,512,1024]{2,1,0:T(8,128)} %get-tuple-element.160, pred[1024]{0:T(1024)(128)(4,1)S(1)} %compare_reduce_fusion), kind=kLoop, calls=%fused_computation.10 | loop fusion | flops 50331648 | bytes 83952640 | tf_op jit(solution)/shard_map/while/body/eval_jaxpr/convert_element_type | solution.py:123
  585.9 46.9 %multiply_reduce_fusion = (f32[16,512]{1,0:T(8,128)S(1)}, f32[16,512,2048]{2,1,0:T(8,128)}) fusion(f32[16,512,2048]{2,1,0:T(8,128)} %get-tuple-element.156, f32[16,512]{1,0:T(8,128)S(1)} %log_add_fusion, bf16[512,16,64]{0,2,1:T(8,128)(2,1)S(1)} %bitcast.163, bf16[2048,16,64]{0,2,1:T(8,128)(2,1)} %bitcast.155), kind=kOutput, calls=%fused_computation.1 | convolution fusion | flops 2197807104 | bytes 139526144 | tf_op jit(solution)/shard_map/while/body/eval_jaxpr/qhd,khd->hqk/dot_general | solution.py:80
  643.9 54.5 %multiply_convert_fusion = bf16[16,512,2048]{2,1,0:T(8,128)(2,1)} fusion(f32[16,512,2048]{2,1,0:T(8,128)} %get-tuple-element.169, f32[16,512,2048]{2,1,0:T(8,128)} %get-tuple-element.156, f32[16,512]{1,0:T(8,128)S(1)} %get-tuple-element.168, f32[16,512]{1,0:T(8,128)S(1)} %log_add_fusion), kind=kLoop, calls=%fused_computation | loop fusion | flops 67108864 | bytes 167837696 | tf_op jit(solution)/shard_map/while/body/eval_jaxpr/convert_element_type | solution.py:123
  698.5 19.3 %multiply_convert_fusion.2 = bf16[16,64,2048]{2,1,0:T(8,128)(2,1)} fusion(bf16[512,16,64]{0,2,1:T(8,128)(2,1)S(1)} %bitcast.162, bf16[16,512,2048]{2,1,0:T(8,128)(2,1)} %multiply_convert_fusion), kind=kOutput, calls=%fused_computation.26 | convolution fusion | flops 2151677952 | bytes 38797312 | tf_op jit(solution)/shard_map/while/body/eval_jaxpr/hqk,qhd->khd/dot_general | solution.py:92
  717.8 26.4 %fusion.19 = bf16[16,64,2048]{2,1,0:T(8,128)(2,1)} fusion(bf16[512,16,64]{0,2,1:T(8,128)(2,1)} %bitcast.164, f32[16,512,2048]{2,1,0:T(8,128)} %get-tuple-element.156, f32[16,512]{1,0:T(8,128)S(1)} %log_add_fusion), kind=kOutput, calls=%fused_computation.50 | convolution fusion | flops 2183135232 | bytes 72384512 | tf_op jit(solution)/shard_map/while/body/eval_jaxpr/hqk,qhd->khd/dot_general | solution.py:97
  755.9 56.8 %reduce-scatter.41.cloned.1.call-done = bf16[128,4096]{1,0:T(8,128)(2,1)} async-done(((bf16[1024,4096]{1,0:T(8,128)(2,1)}), bf16[128,4096]{1,0:T(8,128)(2,1)}) %reduce-scatter.41.cloned.1.call-update) | async-done | bytes 1048592 | tf_op jit(solution)/shard_map/reduce_scatter | solution.py:295
  812.7 75.1 %reduce-scatter.45.cloned.1.call-done = bf16[512,1024]{1,0:T(8,128)(2,1)} async-done(((bf16[4096,1024]{1,0:T(8,128)(2,1)}), bf16[512,1024]{1,0:T(8,128)(2,1)}) %reduce-scatter.45.cloned.1.call-update) | async-done | bytes 1048592 | tf_op jit(solution)/shard_map/reduce_scatter | solution.py:298
  887.9 54.6 %reduce-scatter.49.cloned.1.call-done = bf16[128,2048]{1,0:T(8,128)(2,1)} async-done(((bf16[1024,2048]{1,0:T(8,128)(2,1)}), bf16[128,2048]{1,0:T(8,128)(2,1)}) %reduce-scatter.49.cloned.1.call-update) | async-done | bytes 524304
  944.9 18.8 %multiply_convert_fusion.5 = bf16[16,64,512]{2,1,0:T(8,128)(2,1)} fusion(bf16[2048,16,64]{0,2,1:T(8,128)(2,1)} %bitcast.149, bf16[16,512,2048]{2,1,0:T(8,128)(2,1)} %multiply_convert_fusion), kind=kOutput, calls=%fused_computation.77 | convolution fusion | flops 2148532224 | bytes 38797312 | tf_op jit(solution)/shard_map/while/body/eval_jaxpr/hqk,khd->qhd/dot_general | solution.py:110
  963.7 126.3 %reduce-scatter.19.cloned.1.call-done = bf16[1,512,2048]{1,2,0:T(8,128)(2,1)} async-done(((bf16[1,2048,2048]{1,2,0:T(8,128)(2,1)}), bf16[1,512,2048]{1,2,0:T(8,128)(2,1)}) %reduce-scatter.19.cloned.1.call-update) | async-done | bytes 2097168 | tf_op jit(solution)/shard_map/reduce_scatter | solution.py:260
  1110.8 18.1 %reduce-scatter.33.cloned.1.call-done = bf16[128,256]{1,0:T(8,128)(2,1)} async-done(((bf16[128,1024]{1,0:T(8,128)(2,1)}), bf16[128,256]{1,0:T(8,128)(2,1)}) %reduce-scatter.33.cloned.1.call-update) | async-done | bytes 65552 | tf_op jit(solution)/shard_map/reduce_scatter | solution.py:309
  1130.4 18.7 %reduce-scatter.29.cloned.1.call-done = bf16[128,256]{1,0:T(8,128)(2,1)} async-done(((bf16[128,1024]{1,0:T(8,128)(2,1)}), bf16[128,256]{1,0:T(8,128)(2,1)}) %reduce-scatter.29.cloned.1.call-update) | async-done | bytes 65552 | tf_op jit(solution)/shard_map/reduce_scatter | solution.py:306
  1155.4 23.5 %reduce-scatter.43.cloned.1.call-done = bf16[128,1024]{1,0:T(8,128)(2,1)} async-done(((bf16[128,4096]{1,0:T(8,128)(2,1)}), bf16[128,1024]{1,0:T(8,128)(2,1)}) %reduce-scatter.43.cloned.1.call-update) | async-done | bytes 262160 | tf_op jit(solution)/shard_map/reduce_scatter | solution.py:318
  1180.7 26.3 %reduce-scatter.47.cloned.1.call-done = bf16[512,256]{1,0:T(8,128)(2,1)} async-done(((bf16[512,1024]{1,0:T(8,128)(2,1)}), bf16[512,256]{1,0:T(8,128)(2,1)}) %reduce-scatter.47.cloned.1.call-update) | async-done | bytes 262160 | tf_op jit(solution)/shard_map/reduce_scatter | solution.py:321
  1208.8 18.8 %reduce-scatter.35.cloned.1.call-done = bf16[128,512]{0,1:T(8,128)(2,1)} async-done(((bf16[128,2048]{0,1:T(8,128)(2,1)}), bf16[128,512]{0,1:T(8,128)(2,1)}) %reduce-scatter.35.cloned.1.call-update) | async-done | bytes 131088 | tf_op jit(solution)/shard_map/reduce_scatter | solution.py:312
  1229.2 64.6 %reduce-scatter.23.cloned.1.call-done = bf16[128,3072]{1,0:T(8,128)(2,1)} async-done(((bf16[1024,3072]{1,0:T(8,128)(2,1)}), bf16[128,3072]{1,0:T(8,128)(2,1)}) %reduce-scatter.23.cloned.1.call-update) | async-done | bytes 786448 | tf_op jit(solution)/shard_map/reduce_scatter | solution.py:280
  1303.0 40.0 %all-reduce = (f32[1024]{0:T(1024)}, f32[1024]{0:T(1024)}, f32[1024]{0:T(1024)}) all-reduce(f32[1024]{0:T(1024)S(1)} %get-tuple-element.140, f32[1024]{0:T(1024)S(1)} %copy-done.44, f32[1024]{0:T(1024)S(1)} %copy-done.43), channel_id=1, replica_groups=mesh['page'=8,'blk'=4] {'page','blk'}, use_global_device_ids=true, to_apply=%region_21.22 | all-reduce | flops 3072 | bytes 24576 | tf_op jit(solution)/shard_map/psum | solution.py:325
  (224 shorter events, 305.6 us)
Async XLA Ops:
  7.2 332.1 %copy-start = (bf16[1024,1024]{1,0:T(8,128)(2,1)S(1)}, bf16[1024,1024]{1,0:T(8,128)(2,1)}, u32[]{:S(2)}) copy-start(bf16[1024,1024]{1,0:T(8,128)(2,1)} %param.21) | copy-start | bytes 6291460
  7.2 84.4 %all-gather.7.cloned.1.call-start = ((), (), s32[]{:S(2)}) async-start(), calls=%async_computation.32 | async-start | bytes 5242880 | tf_op jit(solution)/shard_map/all_gather | solution.py:162
  12.0 229.6 %all-gather.5.cloned.1.call-start = ((), (), s32[]{:S(2)}) async-start(), calls=%async_computation.31 | async-start | bytes 10485760 | tf_op jit(solution)/shard_map/all_gather | solution.py:161
  23.2 609.6 %reduce-scatter.21.cloned.1.call-start = ((), (), s32[]{:S(2)}) async-start(), calls=%async_computation.17 | async-start | bytes 5242880 | tf_op jit(solution)/shard_map/reduce_scatter | solution.py:232
  526.5 227.3 %reduce-scatter.37.cloned.1.call-start = ((), (), s32[]{:S(2)}) async-start(), calls=%async_computation.25 | async-start | bytes 2359296 | tf_op jit(solution)/shard_map/reduce_scatter | solution.py:292
  531.6 223.0 %reduce-scatter.31.cloned.1.call-start = ((), (), s32[]{:S(2)}) async-start(), calls=%async_computation.22 | async-start | bytes 2359296 | tf_op jit(solution)/shard_map/reduce_scatter | solution.py:286
  548.5 206.6 %reduce-scatter.27.cloned.1.call-start = ((), (), s32[]{:S(2)}) async-start(), calls=%async_computation.20 | async-start | bytes 2359296 | tf_op jit(solution)/shard_map/reduce_scatter | solution.py:283
  559.6 253.1 %reduce-scatter.41.cloned.1.call-start = ((), (), s32[]{:S(2)}) async-start(), calls=%async_computation.27 | async-start | bytes 9437184 | tf_op jit(solution)/shard_map/reduce_scatter | solution.py:295
  570.4 317.4 %reduce-scatter.45.cloned.1.call-start = ((), (), s32[]{:S(2)}) async-start(), calls=%async_computation.29 | async-start | bytes 9437184 | tf_op jit(solution)/shard_map/reduce_scatter | solution.py:298
  579.6 362.9 %reduce-scatter.49.cloned.1.call-start = ((), (), s32[]{:S(2)}) async-start(), calls=%async_computation.33 | async-start | bytes 4718592
  643.9 446.1 %reduce-scatter.19.cloned.1.call-start = ((), (), s32[]{:S(2)}) async-start(), calls=%async_computation.16 | async-start | bytes 10485760 | tf_op jit(solution)/shard_map/reduce_scatter | solution.py:260
  643.9 54.5 %copy-start.12 = (bf16[512,1024]{0,1:T(8,128)(2,1)S(1)}, bf16[512,1024]{0,1:T(8,128)(2,1)}, u32[]{:S(2)}) copy-start(bf16[512,1024]{0,1:T(8,128)(2,1)} %copy.54) | copy-start | bytes 3145732
  753.8 355.5 %reduce-scatter.39.cloned.1.call-start = ((), (), s32[]{:S(2)}) async-start(), calls=%async_computation.26 | async-start | bytes 327680 | tf_op jit(solution)/shard_map/reduce_scatter | solution.py:315
  754.5 374.4 %reduce-scatter.33.cloned.1.call-start = ((), (), s32[]{:S(2)}) async-start(), calls=%async_computation.23 | async-start | bytes 327680 | tf_op jit(solution)/shard_map/reduce_scatter | solution.py:309
  755.1 394.0 %reduce-scatter.29.cloned.1.call-start = ((), (), s32[]{:S(2)}) async-start(), calls=%async_computation.21 | async-start | bytes 327680 | tf_op jit(solution)/shard_map/reduce_scatter | solution.py:306
  755.9 423.0 %reduce-scatter.43.cloned.1.call-start = ((), (), s32[]{:S(2)}) async-start(), calls=%async_computation.28 | async-start | bytes 1310720 | tf_op jit(solution)/shard_map/reduce_scatter | solution.py:318
  812.7 394.3 %reduce-scatter.47.cloned.1.call-start = ((), (), s32[]{:S(2)}) async-start(), calls=%async_computation.30 | async-start | bytes 1310720 | tf_op jit(solution)/shard_map/reduce_scatter | solution.py:321
  887.8 339.7 %reduce-scatter.35.cloned.1.call-start = ((), (), s32[]{:S(2)}) async-start(), calls=%async_computation.24 | async-start | bytes 655360 | tf_op jit(solution)/shard_map/reduce_scatter | solution.py:312
  944.6 145.4 %copy-start.2 = (bf16[1,512,1024]{2,1,0:T(8,128)(2,1)S(1)}, bf16[1,512,1024]{2,1,0:T(8,128)(2,1)}, u32[]{:S(2)}) copy-start(bf16[1,512,1024]{2,1,0:T(8,128)(2,1)} %param.14) | copy-start | bytes 3145732
  944.6 145.4 %copy-start.30 = (f32[512]{0:T(512)S(1)}, f32[512]{0:T(512)}, u32[]{:S(2)}) copy-start(f32[512]{0:T(512)} %copy-done.29) | copy-start | bytes 6148
  944.6 145.4 %copy-start.38 = (f32[512]{0:T(512)S(1)}, f32[512]{0:T(512)}, u32[]{:S(2)}) copy-start(f32[512]{0:T(512)} %copy-done.37) | copy-start | bytes 6148
  944.6 145.4 %copy-start.40 = (f32[1024]{0:T(1024)S(1)}, f32[1024]{0:T(1024)}, u32[]{:S(2)}) copy-start(f32[1024]{0:T(1024)} %param.17) | copy-start | bytes 12292
  944.7 349.2 %reduce-scatter.23.cloned.1.call-start = ((), (), s32[]{:S(2)}) async-start(), calls=%async_computation.18 | async-start | bytes 7077888 | tf_op jit(solution)/shard_map/reduce_scatter | solution.py:280
  1098.3 248.9 %reduce-scatter.25.cloned.1.call-start = ((), (), s32[]{:S(2)}) async-start(), calls=%async_computation.19 | async-start | bytes 983040 | tf_op jit(solution)/shard_map/reduce_scatter | solution.py:303
  (46 other events, 438.1 us)
Sparse Core Ops, SparseCore 0:
  12.1 79.4 all-gather.6
  93.8 147.7 all-gather.4
  526.7 77.7 reduce-scatter.20
  608.0 40.7 reduce-scatter.36
  651.9 41.1 reduce-scatter.30
  696.6 41.2 reduce-scatter.26
  741.3 71.2 reduce-scatter.40
  816.5 71.2 reduce-scatter.44
  891.2 51.3 reduce-scatter.48
  944.8 145.1 reduce-scatter.18
  1092.4 16.4 reduce-scatter.38
  1111.0 17.8 reduce-scatter.32
  1131.3 17.8 reduce-scatter.28
  1151.3 27.5 reduce-scatter.42
  1181.1 25.8 reduce-scatter.46
  1209.1 18.3 reduce-scatter.34
  1230.8 63.0 reduce-scatter.22
  1296.1 22.0 reduce-scatter.24
where the time goes:
time: 1360 us
  waiting for transfers between devices  677 us (50%)
  matrix products  400 us (29%)
  other arithmetic  151 us (11%)
  local copies, waits for them, and re-layouts  63.6 us (5%)
  blocking collectives  46.8 us (3%)
  between operations  15.3 us (1%)
    all_gather x1, waiting for transfers between devices, on_device(): lax.all_gather(kv_one, 'blk', axis=1, tiled=True)  137 us
    reduce_scatter x1, waiting for transfers between devices, on_device(): lax.psum_scatter(self_terms.astype(jnp.bfloat16), 'blk', scatter_dimensio...  126 us
    convert_element_type x2, other arithmetic, attend_back(): d_scores = (shares * (d_shares - weighted)).astype(jnp.bfloat16)  82.7 us
    reduce_scatter x1, waiting for transfers between devices, on_device(): lax.psum_scatter(matrices[6].astype(jnp.bfloat16), 'page', scatter_dimens...  75.1 us
    dot_general x2, matrix products, shares_and_grads(): jnp.einsum('qhd,khd->hqk', head_split(d_blended), head_split(value_rows),...  71.5 us
    reduce_scatter x1, waiting for transfers between devices, on_device(): lax.psum_scatter(matrices[0].astype(jnp.bfloat16), 'page', scatter_dimens...  64.6 us
    dot_general x7, matrix products, product(): return jnp.dot(left, right, preferred_element_type=jnp.float32)  56.9 us
    reduce_scatter x1, waiting for transfers between devices, on_device(): lax.psum_scatter(matrices[5].astype(jnp.bfloat16), 'page', scatter_dimens...  56.8 us
  transfers between devices with their start and end apart: 18, of which 12 were waited for; matrix products, arithmetic and copies ran while one was open for 23% of the time, Pallas kernels for 0%

commit v1 on v0

v1 whole, which is shorter than its diff:
```python
import functools

import jax
import jax.numpy as jnp
from jax import lax
from jax.experimental import pallas as pl
from jax.experimental.pallas import tpu as pltpu
from jax.sharding import PartitionSpec as P

HEADS = 16
HEAD_DIM = 64
LANES = 128

norm_eps = 1e-05
masked_score = -1e30


def nt(left, right):
    return lax.dot_general(
        left, right, (((1,), (1,)), ((), ())), preferred_element_type=jnp.float32
    )


def nn(left, right):
    return lax.dot_general(
        left, right, (((1,), (0,)), ((), ())), preferred_element_type=jnp.float32
    )


def tn(left, right):
    return lax.dot_general(
        left, right, (((0,), (0,)), ((), ())), preferred_element_type=jnp.float32
    )


def lane_of(shape):
    return lax.broadcasted_iota(jnp.int32, shape, len(shape) - 1)


def own_lanes(shape, head):
    lane = lane_of(shape)
    return lane < HEAD_DIM if head == 0 else lane >= HEAD_DIM


def spare_lane(shape, head):
    return lane_of(shape) - (HEAD_DIM if head == 0 else 0)


def three_parts(column):
    high = column.astype(jnp.bfloat16)
    rest = column - high.astype(jnp.float32)
    middle = rest.astype(jnp.bfloat16)
    low = (rest - middle.astype(jnp.float32)).astype(jnp.bfloat16)
    return high, middle, low


def forward_kernel(heads, causal, tq, tk, q_ref, k_ref, v_ref, *rest):
    if causal:
        bias_ref = None
        mixed_ref, qx_ref, kx, vx = rest
    else:
        bias_ref, mixed_ref, qx_ref, kx, vx = rest
    step = pl.program_id(2)
    keys = k_ref.shape[0]
    scale = HEAD_DIM ** (-0.5)

    @pl.when(step == 0)
    def _():
        turned = v_ref[...].astype(jnp.float32).T.astype(jnp.bfloat16)
        ones = jnp.ones((16, keys), jnp.bfloat16)
        for h in range(heads):
            vx[h, :HEAD_DIM] = turned[h * HEAD_DIM : (h + 1) * HEAD_DIM]
            vx[h, HEAD_DIM:] = ones
            k = k_ref[...]
            filler = jnp.zeros_like(k) if causal else bias_ref[...]
            kx[h] = jnp.where(own_lanes(k.shape, h), k, filler)

    q = q_ref[...] * jnp.bfloat16(scale)
    q_heads = []
    for h in range(heads):
        one = (spare_lane(q.shape, h) == 0).astype(jnp.float32).astype(jnp.bfloat16)
        q_heads.append(jnp.where(own_lanes(q.shape, h), q, one))

    def tile(j, carry, masked):
        out = []
        start = pl.multiple_of(j * tk, tk)
        for h in range(heads):
            largest, total = carry[h]
            scores = nt(kx[h, pl.ds(start, tk), :], q_heads[h])
            if masked:
                key_at = start + lax.broadcasted_iota(jnp.int32, scores.shape, 0)
                query_at = step * tq + lax.broadcasted_iota(jnp.int32, scores.shape, 1)
                scores = jnp.where(key_at <= query_at, scores, masked_score)
            new_largest = jnp.maximum(largest, jnp.max(scores, axis=0, keepdims=True))
            raised = jnp.exp(scores - new_largest).astype(jnp.bfloat16)
            part = nn(vx[h, :, pl.ds(start, tk)], raised)
            out.append((new_largest, total * jnp.exp(largest - new_largest) + part))
        return tuple(out)

    carry = tuple(
        (
            jnp.full((1, tq), masked_score, jnp.float32),
            jnp.zeros((HEAD_DIM + 16, tq), jnp.float32),
        )
        for _ in range(heads)
    )
    if causal:
        full = step * tq // tk
        carry = lax.fori_loop(0, full, lambda j, c: tile(j, c, False), carry)
        for extra in range(max(tq // tk, 1)):
            carry = tile(full + extra, carry, True)
    else:
        for j in range(keys // tk):
            carry = tile(j, carry, False)
    blended, columns = [], []
    for h in range(heads):
        largest, total = carry[h]
        sums = total[HEAD_DIM : HEAD_DIM + 1]
        blended.append(total[:HEAD_DIM] / sums)
        columns.append(-(largest + jnp.log(sums)))
    if heads == 1:
        blended.append(jnp.zeros_like(blended[0]))
    mixed_ref[...] = jnp.concatenate(blended, 0).T.astype(mixed_ref.dtype)
    for h in range(heads):
        turned = jnp.broadcast_to(columns[h], (LANES, tq)).T
        high, middle, low = three_parts(turned)
        place = spare_lane(q.shape, h)
        qx = jnp.where(own_lanes(q.shape, h), q, jnp.zeros_like(q))
        qx = jnp.where(place == 0, jnp.ones_like(q), qx)
        qx = jnp.where(place == 1, high, qx)
        qx = jnp.where(place == 2, middle, qx)
        qx_ref[:, h * LANES : (h + 1) * LANES] = jnp.where(place == 3, low, qx)


def backward_kernel(heads, causal, tq, tk, qx_ref, k_ref, v_ref, o_ref, do_ref, *rest):
    bias_ref = None
    if causal:
        packed_ref, kx, kt, vx, dx, dqt = rest
    else:
        bias_ref, dq_ref, packed_ref, kx, kt, vx, dx, dqt = rest
    queries, keys = qx_ref.shape[0], k_ref.shape[0]
    scale = HEAD_DIM ** (-0.5)
    at = LANES if causal else 0

    k = k_ref[...]
    v = v_ref[...]
    kt[...] = (k.astype(jnp.float32) * scale).T.astype(jnp.bfloat16)
    do = do_ref[...]
    product = do.astype(jnp.float32) * o_ref[...].astype(jnp.float32)
    for h in range(heads):
        own = own_lanes(k.shape, h)
        place = spare_lane(k.shape, h)
        ones = jnp.ones_like(k)
        bias = jnp.zeros_like(k) if causal else bias_ref[...]
        kx[h] = jnp.where(own, k, jnp.where(place == 0, bias, ones))
        vx[h] = jnp.where(own, v, ones)
        own = own_lanes(do.shape, h)
        place = spare_lane(do.shape, h)
        delta = jnp.sum(jnp.where(own, product, 0.0), axis=1, keepdims=True)
        high, middle, low = three_parts(jnp.broadcast_to(-delta, do.shape))
        value = jnp.where(own, do, jnp.zeros_like(do))
        value = jnp.where(place == 0, high, value)
        value = jnp.where(place == 1, middle, value)
        dx[h] = jnp.where(place == 2, low, value)

    dqt[...] = jnp.zeros_like(dqt)

    def tile(i, j, masked, sums):
        q_at = pl.multiple_of(i * tq, tq)
        k_at = pl.multiple_of(j * tk, tk)
        out = []
        for h in range(heads):
            qx = qx_ref[pl.ds(q_at, tq), h * LANES : (h + 1) * LANES]
            shares = jnp.exp(nt(kx[h, pl.ds(k_at, tk), :], qx))
            if masked:
                key_at = k_at + lax.broadcasted_iota(jnp.int32, shares.shape, 0)
                query_at = q_at + lax.broadcasted_iota(jnp.int32, shares.shape, 1)
                shares = jnp.where(key_at <= query_at, shares, 0.0)
            grad = dx[h, pl.ds(q_at, tq), :]
            d_shares = nt(vx[h, pl.ds(k_at, tk), :], grad)
            d_scores = (shares * d_shares).astype(jnp.bfloat16)
            dv = nn(shares.astype(jnp.bfloat16), grad)
            dk = nn(d_scores, qx)
            rows = pl.ds(h * HEAD_DIM, HEAD_DIM)
            dqt[rows, pl.ds(q_at, tq)] += nn(kt[rows, pl.ds(k_at, tk)], d_scores)
            if sums is not None:
                dk, dv = sums[h][0] + dk, sums[h][1] + dv
            out.append((dk, dv))
        return tuple(out)

    def finish(j, sums):
        k_at = pl.multiple_of(j * tk, tk)
        dk, dv = sums[0]
        if heads == 2:
            own = own_lanes(dk.shape, 0)
            dk, dv = jnp.where(own, dk, sums[1][0]), jnp.where(own, dv, sums[1][1])
        packed_ref[pl.ds(k_at, tk), at : at + LANES] = dk.astype(packed_ref.dtype)
        packed_ref[pl.ds(k_at, tk), at + LANES : at + 2 * LANES] = dv.astype(packed_ref.dtype)

    if causal:

        @pl.loop(0, keys // tk)
        def _(j):
            sums = tile(j, j, True, None)
            sums = lax.fori_loop(
                j + 1, queries // tq, lambda i, s: tile(i, j, False, s), sums
            )
            finish(j, sums)

        packed_ref[:, :LANES] = dqt[...].T.astype(packed_ref.dtype)
    else:
        for j in range(keys // tk):
            sums = None
            for i in range(queries // tq):
                sums = tile(i, j, False, sums)
            finish(j, sums)
        dq_ref[...] = dqt[...].T.astype(dq_ref.dtype)


def tile_of(rows, largest):
    return rows if rows < largest else largest


def attend(q, kv, bias, heads, blocks, tq, tk):
    pages, queries = q.shape[:2]
    keys = kv.shape[1]
    causal = bias is None
    tq, tk = tile_of(queries, tq), tile_of(keys, tk)
    wide, skip = (3, 1) if causal else (2, 0)
    q_wide = 3 if causal else 1
    in_specs = [
        pl.BlockSpec((None, tq, LANES), lambda p, b, i: (p, i, q_wide * b)),
        pl.BlockSpec((None, keys, LANES), lambda p, b, i: (p, 0, wide * b + skip)),
        pl.BlockSpec((None, keys, LANES), lambda p, b, i: (p, 0, wide * b + skip + 1)),
    ]
    args = [q, kv, kv]
    if not causal:
        in_specs.append(pl.BlockSpec((None, keys, LANES), lambda p, b, i: (p, 0, 0)))
        args.append(bias)
    elements = pages * blocks * heads * queries * keys // (2 if causal else 1)
    return pl.pallas_call(
        functools.partial(forward_kernel, heads, causal, tq, tk),
        grid=(pages, blocks, queries // tq),
        in_specs=in_specs,
        out_specs=[
            pl.BlockSpec((None, tq, LANES), lambda p, b, i: (p, i, b)),
            pl.BlockSpec((None, tq, heads * LANES), lambda p, b, i: (p, i, b)),
        ],
        out_shape=[
            jax.ShapeDtypeStruct((pages, queries, blocks * LANES), jnp.bfloat16),
            jax.ShapeDtypeStruct((pages, queries, blocks * heads * LANES), jnp.bfloat16),
        ],
        scratch_shapes=[
            pltpu.VMEM((heads, keys, LANES), jnp.bfloat16),
            pltpu.VMEM((heads, HEAD_DIM + 16, keys), jnp.bfloat16),
        ],
        compiler_params=pltpu.CompilerParams(vmem_limit_bytes=40 << 20),
        cost_estimate=pl.CostEstimate(
            flops=elements * 2048, bytes_accessed=4 << 20, transcendentals=elements
        ),
        name="attend",
    )(*args)


def attend_back(qx, kv, mixed, d_mixed, bias, heads, blocks, tq, tk):
    pages, queries = qx.shape[:2]
    keys = kv.shape[1]
    causal = bias is None
    tq, tk = tile_of(queries, tq), tile_of(keys, tk)
    wide, skip = (3, 1) if causal else (2, 0)
    whole = lambda rows, lanes: pl.BlockSpec((None, rows, lanes), lambda p, b: (p, 0, b))
    in_specs = [
        whole(queries, heads * LANES),
        pl.BlockSpec((None, keys, LANES), lambda p, b: (p, 0, wide * b + skip)),
        pl.BlockSpec((None, keys, LANES), lambda p, b: (p, 0, wide * b + skip + 1)),
        whole(queries, LANES),
        whole(queries, LANES),
    ]
    args = [qx, kv, kv, mixed, d_mixed]
    out_specs = [whole(keys, wide * LANES)]
    out_shape = [jax.ShapeDtypeStruct((pages, keys, blocks * wide * LANES), jnp.bfloat16)]
    if not causal:
        in_specs.append(pl.BlockSpec((None, keys, LANES), lambda p, b: (p, 0, 0)))
        args.append(bias)
        out_specs.insert(0, whole(queries, LANES))
        out_shape.insert(0, jax.ShapeDtypeStruct((pages, queries, blocks * LANES), jnp.bfloat16))
    elements = pages * blocks * heads * queries * keys // (2 if causal else 1)
    return pl.pallas_call(
        functools.partial(backward_kernel, heads, causal, tq, tk),
        grid=(pages, blocks),
        in_specs=in_specs,
        out_specs=out_specs,
        out_shape=out_shape,
        scratch_shapes=[
            pltpu.VMEM((heads, keys, LANES), jnp.bfloat16),
            pltpu.VMEM((LANES, keys), jnp.bfloat16),
            pltpu.VMEM((heads, keys, LANES), jnp.bfloat16),
            pltpu.VMEM((heads, queries, LANES), jnp.bfloat16),
            pltpu.VMEM((LANES, queries), jnp.float32),
        ],
        compiler_params=pltpu.CompilerParams(vmem_limit_bytes=40 << 20),
        cost_estimate=pl.CostEstimate(
            flops=elements * 2560, bytes_accessed=8 << 20, transcendentals=elements
        ),
        name="attend_back",
    )(*args)


def expand_kernel(normed_ref, grad_ref, up_ref, down_ref, active_ref, d_upward_ref):
    upward = nn(normed_ref[...], up_ref[...])
    d_active = nt(grad_ref[...], down_ref[...])
    share = 0.5 * (1.0 + lax.erf(upward * (0.5**0.5)))
    active_ref[...] = (upward * share).astype(active_ref.dtype)
    density = jnp.exp(-0.5 * upward * upward) * 0.3989422804014327
    d_upward_ref[...] = (d_active * (share + upward * density)).astype(d_upward_ref.dtype)


def expand(normed, grad, w_up, w_down):
    rows, width = normed.shape
    wide = w_up.shape[1]
    step = 512
    return pl.pallas_call(
        expand_kernel,
        grid=(wide // step,),
        in_specs=[
            pl.BlockSpec((rows, width), lambda f: (0, 0)),
            pl.BlockSpec((rows, width), lambda f: (0, 0)),
            pl.BlockSpec((width, step), lambda f: (0, f)),
            pl.BlockSpec((step, width), lambda f: (f, 0)),
        ],
        out_specs=[
            pl.BlockSpec((rows, step), lambda f: (0, f)),
            pl.BlockSpec((rows, step), lambda f: (0, f)),
        ],
        out_shape=[jax.ShapeDtypeStruct((rows, wide), jnp.bfloat16)] * 2,
        compiler_params=pltpu.CompilerParams(vmem_limit_bytes=40 << 20),
        cost_estimate=pl.CostEstimate(
            flops=4 * rows * width * wide, bytes_accessed=26 << 20, transcendentals=2 * rows * wide
        ),
        name="expand",
    )(normed, grad, w_up, w_down)


def norm_of(values):
    center = values - jnp.mean(values, axis=-1, keepdims=True)
    rstd = lax.rsqrt(jnp.mean(center * center, axis=-1, keepdims=True) + norm_eps)
    return center * rstd, rstd


def norm_back(values, gain, d_normed):
    xhat, rstd = norm_of(values)
    e = d_normed * gain
    d_values = rstd * (
        e
        - jnp.mean(e, axis=-1, keepdims=True)
        - xhat * jnp.mean(e * xhat, axis=-1, keepdims=True)
    )
    return d_values, jnp.sum(d_normed * xhat, axis=0)


def shifted(value, shift):
    count = lax.axis_size("blk")
    return lax.ppermute(value, "blk", [(i, (i + shift) % count) for i in range(count)])


def ring_pieces(value):
    count = lax.axis_size("blk")
    pieces = [(value, 0)]
    right = left = value
    for hop in range(1, (count - 1) // 2 + 1):
        right, left = shifted(right, 1), shifted(left, -1)
        pieces += [(right, -hop), (left, hop)]
    if count % 2 == 0:
        half = value.shape[1] // 2
        if count > 1:
            top, low = shifted(right[:, :half], 1), shifted(left[:, half:], -1)
            pieces.append((jnp.concatenate([top, low], 1), count // 2))
    return pieces


def gathered(pieces, axis):
    count = lax.axis_size("blk")
    place = lax.axis_index("blk")
    size = pieces[0][0].shape[axis]
    shape = list(pieces[0][0].shape)
    shape[axis] = size * count
    whole = jnp.zeros(shape, pieces[0][0].dtype)
    for piece, far in pieces:
        whole = lax.dynamic_update_slice_in_dim(
            whole, piece, (place + far) % count * size, axis
        )
    return whole


def exchanged(value, split, join):
    count = lax.axis_size("blk")
    place = lax.axis_index("blk")
    size = value.shape[split] // count
    take = lambda far: lax.dynamic_slice_in_dim(
        value, (place + far) % count * size, size, split
    )
    pieces = [(take(0), 0)]
    order = sorted(range(1, count), key=lambda far: -min(far, count - far))
    for far in order:
        pieces.append((shifted(take(far), far), -far))
    return gathered(pieces, join)


def on_device(
    tokens,
    patches,
    patch_mask,
    gain_one,
    qkv_self,
    out_self,
    gain_two,
    q_cross,
    kv_cross,
    out_cross,
    gain_three,
    w_up,
    w_down,
    cotangent,
):
    pages, token_count, width = tokens.shape
    patch_count = patches.shape[1]
    count = lax.axis_size("blk")
    place = lax.axis_index("blk")
    rows = pages * token_count
    here = HEADS // count
    heads = 2 if here % 2 == 0 else 1
    blocks = here // heads
    lanes = heads * HEAD_DIM

    def padded(value):
        if lanes == LANES:
            return value
        split = value.reshape(value.shape[:-1] + (-1, lanes))
        split = jnp.pad(split, [(0, 0)] * (split.ndim - 1) + [(0, LANES - lanes)])
        return split.reshape(value.shape[:-1] + (-1,))

    def cut(value):
        if lanes == LANES:
            return value
        split = value.reshape(value.shape[:-1] + (-1, LANES))[..., :lanes]
        return split.reshape(value.shape[:-1] + (-1,))

    qkv_blocks = (
        qkv_self.reshape(width, 3, width // lanes, lanes)
        .transpose(0, 2, 1, 3)
        .reshape(width, 3 * width)
    )
    qkv_here = lax.dynamic_slice_in_dim(
        qkv_blocks, place * (3 * width // count), 3 * width // count, 1
    )
    kv_blocks = (
        kv_cross.reshape(width, 2, width // LANES, LANES)
        .transpose(0, 2, 1, 3)
        .reshape(width, 2 * width)
    )

    normed_pieces, packed_pieces = [], []
    for piece, far in ring_pieces(tokens):
        flat = piece.reshape(rows, width).astype(jnp.float32)
        normed = (norm_of(flat)[0] * gain_one).astype(jnp.bfloat16)
        packed = padded(nn(normed, qkv_here).astype(jnp.bfloat16))
        normed_pieces.append((normed.reshape(pages, token_count, width), far))
        packed_pieces.append((packed.reshape(pages, token_count, -1), far))
    normed_one = gathered(normed_pieces, 1)
    packed = gathered(packed_pieces, 1)
    mixed_here, qx_one = attend(packed, packed, None, heads, blocks, 512, 512)
    mixed_one = exchanged(cut(mixed_here), 1, 2).reshape(rows, width)

    patches_all = gathered(ring_pieces(patches), 1)
    dead = jnp.where(patch_mask > 0, 0.0, masked_score).astype(jnp.bfloat16)
    dead_pieces = [(dead, 0)] + [(shifted(dead, far), -far) for far in range(1, count)]
    bias = gathered(dead_pieces, 1)
    bias = jnp.broadcast_to(bias[:, :, None], bias.shape + (LANES,))
    page_patches = patches_all.reshape(-1, width)
    kv_two = nn(page_patches, kv_blocks).astype(jnp.bfloat16)
    kv_two = kv_two.reshape(pages, -1, 2 * width)

    flat_tokens = tokens.reshape(rows, width).astype(jnp.float32)
    resid_one = flat_tokens + nn(mixed_one, out_self)
    normed_two = (norm_of(resid_one)[0] * gain_two).astype(jnp.bfloat16)
    query_two = nn(normed_two, q_cross).astype(jnp.bfloat16).reshape(pages, token_count, width)
    mixed_two, qx_two = attend(query_two, kv_two, bias, 2, width // LANES, 512, 1024)
    flat_mixed_two = mixed_two.reshape(rows, width)
    resid_two = resid_one + nn(flat_mixed_two, out_cross)
    normed_three = (norm_of(resid_two)[0] * gain_three).astype(jnp.bfloat16)

    flat_cotangent = cotangent.reshape(rows, width)
    active, d_upward = expand(normed_three, flat_cotangent, w_up, w_down)
    output = (resid_two + nn(active, w_down)).astype(jnp.bfloat16)
    grad_w_down = tn(active, flat_cotangent)
    grad_w_up = tn(normed_three, d_upward)

    d_part, grad_gain_three = norm_back(resid_two, gain_three, nt(d_upward, w_up))
    d_resid_two = flat_cotangent.astype(jnp.float32) + d_part
    branch_two = d_resid_two.astype(jnp.bfloat16)
    grad_out_cross = tn(flat_mixed_two, branch_two)
    d_mixed_two = nt(branch_two, out_cross).astype(jnp.bfloat16)
    d_query_two, d_kv_two = attend_back(
        qx_two,
        kv_two,
        mixed_two,
        d_mixed_two.reshape(pages, token_count, width),
        bias,
        2,
        width // LANES,
        512,
        1024,
    )
    d_query_two = d_query_two.reshape(rows, width)
    d_kv_two = d_kv_two.reshape(-1, 2 * width)
    grad_q_cross = tn(normed_two, d_query_two)
    grad_kv_cross = tn(page_patches, d_kv_two)
    grad_kv_cross = (
        grad_kv_cross.reshape(width, width // LANES, 2, LANES)
        .transpose(0, 2, 1, 3)
        .reshape(width, 2 * width)
    )
    grad_patches = nt(d_kv_two, kv_blocks).astype(jnp.bfloat16).reshape(pages, -1, width)
    grad_patches = exchanged(grad_patches[None], 2, 0)
    grad_patches = jnp.sum(grad_patches.astype(jnp.float32), axis=0)

    d_part, grad_gain_two = norm_back(resid_one, gain_two, nt(d_query_two, q_cross))
    d_resid_one = d_resid_two + d_part
    branch_one = d_resid_one.astype(jnp.bfloat16)
    grad_out_self = tn(mixed_one, branch_one)
    d_mixed_one = nt(branch_one, out_self).astype(jnp.bfloat16)
    d_mixed_here = exchanged(d_mixed_one.reshape(pages, token_count, width), 2, 1)
    (d_packed_here,) = attend_back(
        qx_one, packed, mixed_here, padded(d_mixed_here), None, heads, blocks, 512, 512
    )
    d_packed_here = cut(d_packed_here)
    d_packed = exchanged(d_packed_here, 1, 2).reshape(rows, 3 * width)
    grad_qkv_here = tn(
        normed_one.reshape(-1, width), d_packed_here.reshape(-1, 3 * width // count)
    )
    d_part, grad_gain_one = norm_back(flat_tokens, gain_one, nt(d_packed, qkv_blocks))
    grad_tokens = d_resid_one + d_part

    def over_page(matrix):
        return lax.psum_scatter(
            matrix.astype(jnp.bfloat16), "page", scatter_dimension=0, tiled=True
        )

    def over_both(matrix):
        return lax.psum_scatter(
            over_page(matrix), "blk", scatter_dimension=1, tiled=True
        ).astype(jnp.float32)

    qkv_part = over_page(grad_qkv_here)
    qkv_pieces = [(qkv_part, 0)] + [(shifted(qkv_part, far), -far) for far in range(1, count)]
    qkv_rows = gathered(qkv_pieces, 1)
    qkv_rows = (
        qkv_rows.reshape(-1, width // lanes, 3, lanes).transpose(0, 2, 1, 3).reshape(-1, 3 * width)
    )
    size = 3 * width // count
    grad_qkv_self = lax.dynamic_slice_in_dim(qkv_rows, place * size, size, 1).astype(jnp.float32)

    gain_sums = lax.psum((grad_gain_one, grad_gain_two, grad_gain_three), ("page", "blk"))
    return (
        output.reshape(pages, token_count, width),
        grad_tokens.reshape(pages, token_count, width),
        grad_patches,
        gain_sums[0],
        grad_qkv_self,
        over_both(grad_out_self),
        gain_sums[1],
        over_both(grad_q_cross),
        over_both(grad_kv_cross),
        over_both(grad_out_cross),
        gain_sums[2],
        over_both(grad_w_up),
        over_both(grad_w_down),
    )


def solution(mesh):
    whole = P()
    cut = P("page", "blk", None)
    matrix = P("page", "blk")
    placed = (cut, cut, matrix) + (whole,) * 10 + (cut,)
    return jax.shard_map(
        on_device,
        mesh=mesh,
        in_specs=placed,
        out_specs=(
            cut,
            cut,
            cut,
            whole,
            matrix,
            matrix,
            whole,
            matrix,
            matrix,
            matrix,
            whole,
            matrix,
            matrix,
        ),
        check_vma=False,
    )
```

time: 1360 us -> 810 us (0.60)
  waiting for transfers between devices: 677 us -> 358 us
  matrix products: 400 us -> 112 us
  Pallas kernels: 0 us -> 123 us
  other arithmetic: 151 us -> 34.2 us
  starting transfers between devices: 1.77 us -> 30.5 us
  local copies, waits for them, and re-layouts: 63.6 us -> 83.7 us
    dot_general x33 -> x22, matrix products: 400 us -> 112 us  [the longest x7 40.3 us: tn(): lax.dot_general(left, right, (((0,), (0,)), ((), ())), preferred_element_...]
    reduce_scatter x15 -> x12, waiting for transfers between devices: 428 us -> 146 us  [the longest x6 84.3 us: over_both(): lax.psum_scatter(over_page(matrix), 'blk', scatter_dimension=1, tiled=True)]
    all_gather x2 -> x0, waiting for transfers between devices: 193 us -> none  [the longest x1 137 us: on_device(): lax.all_gather(kv_one, 'blk', axis=1, tiled=True)]
    ppermute x0 -> x26, waiting for transfers between devices: none -> 160 us  [shifted(): lax.ppermute(value, 'blk', [(i, (i + shift) % count) for i in range(count)])]
    pallas_call x0 -> x5, Pallas kernels: none -> 123 us  [the longest x2 62.7 us: attend_back(): pl.pallas_call(functools.partial(backward_kernel, heads, causal, tq, tk),...]
    convert_element_type x10 -> x9, other arithmetic: 92.8 us -> 9.14 us  [the longest x5 8.08 us: over_both(): return lax.psum_scatter(over_page(matrix), 'blk', scatter_dimension=1, ti...]
    slice x9 -> x4, local copies, waits for them, and re-layouts: 37.9 us -> 4.24 us  [ring_pieces(): top, low = (shifted(right[:, :half], 1), shifted(left[:, half:], -1))]
    ppermute x0 -> x26, starting transfers between devices: none -> 29.6 us  [shifted(): lax.ppermute(value, 'blk', [(i, (i + shift) % count) for i in range(count)])]
  transfers between devices with their start and end apart: 18 -> 39, of which waited for: 12 -> 22; matrix products, arithmetic and copies ran while one was open for 23% -> 23% of each run, Pallas kernels for 0% -> 5%
where the time goes in v1:
time: 810 us; the launch traced here: 799 us
  waiting for transfers between devices  358 us (44%)
  Pallas kernels  123 us (15%)
  matrix products  112 us (14%)
  local copies, waits for them, and re-layouts  83.7 us (10%)
  blocking collectives  41 us (5%)
  other arithmetic  34.2 us (4%)
  starting transfers between devices  30.5 us (4%)
  between operations  15.6 us (2%)
    ppermute x26, waiting for transfers between devices, shifted(): lax.ppermute(value, 'blk', [(i, (i + shift) % count) for i in range(count)])  160 us
    reduce_scatter x6, waiting for transfers between devices, over_both(): lax.psum_scatter(over_page(matrix), 'blk', scatter_dimension=1, tiled=True)  84.3 us
    pallas_call x2, Pallas kernels, attend_back(): pl.pallas_call(functools.partial(backward_kernel, heads, causal, tq, tk),...  62.7 us
    reduce_scatter x6, waiting for transfers between devices, over_page(): lax.psum_scatter(matrix.astype(jnp.bfloat16), 'page', scatter_dimension=0...  61.5 us
    unnamed x14, waiting for transfers between devices  51.8 us
    pallas_call x2, Pallas kernels, attend(): pl.pallas_call(functools.partial(forward_kernel, heads, causal, tq, tk),...  47.3 us
    psum x1, blocking collectives, on_device(): lax.psum((grad_gain_one, grad_gain_two, grad_gain_three), ('page', 'blk'))  41 us
    dot_general x7, matrix products, tn(): lax.dot_general(left, right, (((0,), (0,)), ((), ())), preferred_element_...  40.3 us
  transfers between devices with their start and end apart: 39, of which 22 were waited for; matrix products, arithmetic and copies ran while one was open for 23% of the time, Pallas kernels for 5%

profile of v1, /device:TPU:15, one launch (start us, length us, event | category | flops | bytes accessed | tf_op | source)
XLA Modules:
  0.0 798.7 jit_solution(642378035644293193)
XLA Ops:
  61.5 22.6 %collective-permute-done.10 = bf16[1,128,1024]{2,1,0:T(8,128)(2,1)S(1)} collective-permute-done((bf16[1,128,1024]{2,1,0:T(8,128)(2,1)S(1)}, bf16[1,128,1024]{2,1,0:T(8,128)(2,1)S(1)}, u32[]{:S(2)}, u32[]{:S(2)}) %collective-permute-start.10) | collective-permute-done | bytes 262176 | tf_op jit(solution)/shard_map/ppermute | solution.py:363
  108.6 13.7 %collective-permute-done.3 = bf16[1,256,1024]{2,1,0:T(8,128)(2,1)S(1)} collective-permute-done((bf16[1,256,1024]{2,1,0:T(8,128)(2,1)S(1)}, bf16[1,256,1024]{2,1,0:T(8,128)(2,1)S(1)}, u32[]{:S(2)}, u32[]{:S(2)}) %collective-permute-start.3) | collective-permute-done | bytes 524320 | tf_op jit(solution)/shard_map/ppermute | solution.py:363
  125.6 27.4 %attend.2 = (bf16[1,2048,256]{2,1,0:T(8,128)(2,1)S(1)}, bf16[1,2048,512]{2,1,0:T(8,128)(2,1)S(1)}) custom-call(bf16[1,2048,768]{2,1,0:T(8,128)(2,1)} %fusion.64.q_ref.k_ref.v_ref, bf16[1,2048,768]{2,1,0:T(8,128)(2,1)} %fusion.64.q_ref.k_ref.v_ref, bf16[1,2048,768]{2,1,0:T(8,128)(2,1)} %fusion.64.q_ref.k_ref.v_ref), custom_call_target="tpu_custom_call" | custom-call | flops 17179869184 | bytes 4194304 | tf_op jit(solution)/shard_map/attend/pallas_call | solution.py:241
  164.1 11.2 %collective-permute-done.5 = bf16[1,512,256]{2,1,0:T(8,128)(2,1)S(1)} collective-permute-done((bf16[1,512,256]{2,1,0:T(8,128)(2,1)S(1)}, bf16[1,512,256]{2,1,0:T(8,128)(2,1)S(1)}, u32[]{:S(2)}, u32[]{:S(2)}) %collective-permute-start.5) | collective-permute-done | bytes 262176 | tf_op jit(solution)/shard_map/ppermute | solution.py:363
  182.5 20.0 %attend.3 = (bf16[1,512,1024]{2,1,0:T(8,128)(2,1)S(1)}, bf16[1,512,2048]{2,1,0:T(8,128)(2,1)S(1)}) custom-call(bf16[1,512,1024]{2,1,0:T(8,128)(2,1)S(1)} %fusion.54.q_ref, bf16[1,1024,2048]{2,1,0:T(8,128)(2,1)S(1)} %convert_bitcast_fusion.1.k_ref.v_ref, bf16[1,1024,2048]{2,1,0:T(8,128)(2,1)S(1)} %convert_bitcast_fusion.1.k_ref.v_ref, ...), custom_call_target="tpu_custom_call" | custom-call | flops 17179869184 | bytes 4194304 | tf_op jit(solution)/shard_map/attend/pallas_call | solution.py:241
  205.8 13.3 %expand.1 = (bf16[512,4096]{1,0:T(8,128)(2,1)S(1)}, bf16[512,4096]{1,0:T(8,128)(2,1)S(1)}) custom-call(bf16[512,1024]{1,0:T(8,128)(2,1)S(1)} %multiply_convert_fusion.1.normed_ref, bf16[512,1024]{1,0:T(8,128)(2,1)S(1)} %bitcast.238, bf16[1024,4096]{1,0:T(8,128)(2,1)} %up_ref.1, bf16[4096,1024]{1,0:T(8,128)(2,1)} %down_ref.1), custom_call_target="tpu_custom_call" | custom-call | flops 8589934592 | bytes 27262976 | tf_op jit(solution)/shard_map/expand/pallas_call | solution.py:322
  219.2 13.4 %multiply_reduce_fusion = (f32[1024]{0:T(1024)}, f32[512]{0:T(512)S(1)}, f32[512]{0:T(512)S(1)}, f32[512,1024]{1,0:T(8,128)}) fusion(f32[512,1024]{1,0:T(8,128)} %copy-done.17, f32[512]{0:T(512)S(1)} %add_rsqrt_fusion, f32[512]{0:T(512)S(1)} %broadcast_multiply_fusion.6, f32[1024]{0:T(1024)S(1)} %copy-done.54, bf16[512,4096]{1,0:T(8,128)(2,1)S(1)} %get-tuple-element.24, ...), kind=kOutput, calls=%fused_computation.64 | convolution fusion | flops 4299159552 | bytes 16793600 | tf_op jit(solution)/shard_map/dot_general | solution.py:19
  238.1 26.1 %attend_back.2 = (bf16[1,512,1024]{2,1,0:T(8,128)(2,1)S(1)}, bf16[1,1024,2048]{2,1,0:T(8,128)(2,1)S(1)}) custom-call(bf16[1,512,2048]{2,1,0:T(8,128)(2,1)S(1)} %copy-done.14, bf16[1,1024,2048]{2,1,0:T(8,128)(2,1)S(1)} %convert_bitcast_fusion.1.k_ref.v_ref, bf16[1,1024,2048]{2,1,0:T(8,128)(2,1)S(1)} %convert_bitcast_fusion.1.k_ref.v_ref, ...), custom_call_target="tpu_custom_call" | custom-call | flops 21474836480 | bytes 8388608 | tf_op jit(solution)/shard_map/attend_back/pallas_call | solution.py:288
  306.3 9.0 %convolution_convert_fusion.1 = bf16[1024,4096]{1,0:T(8,128)(2,1)} fusion(bf16[512,1024]{1,0:T(8,128)(2,1)S(1)} %multiply_convert_fusion.1.normed_ref, bf16[512,4096]{1,0:T(8,128)(2,1)} %copy-done.12), kind=kOutput, calls=%fused_computation.1 | convolution fusion | flops 4299161600 | bytes 13631488 | tf_op jit(solution)/shard_map/dot_general | solution.py:31
  316.5 9.1 %convolution_convert_fusion = bf16[4096,1024]{1,0:T(8,128)(2,1)} fusion(bf16[512,4096]{1,0:T(8,128)(2,1)} %copy-done.11, bf16[1,512,1024]{2,1,0:T(8,128)(2,1)S(1)} %copy-done.8), kind=kOutput, calls=%fused_computation | convolution fusion | flops 4299161600 | bytes 13631488 | tf_op jit(solution)/shard_map/dot_general | solution.py:31
  344.2 11.2 %collective-permute-done.15 = bf16[1,512,256]{2,1,0:T(8,128)(2,1)S(1)} collective-permute-done((bf16[1,512,256]{2,1,0:T(8,128)(2,1)S(1)}, bf16[1,512,256]{2,1,0:T(8,128)(2,1)S(1)}, u32[]{:S(2)}, u32[]{:S(2)}) %collective-permute-start.15) | collective-permute-done | bytes 262176 | tf_op jit(solution)/shard_map/ppermute | solution.py:363
  358.8 36.7 %attend_back.3 = bf16[1,2048,768]{2,1,0:T(8,128)(2,1)S(1)} custom-call(bf16[1,2048,512]{2,1,0:T(8,128)(2,1)S(1)} %copy-done.16, bf16[1,2048,768]{2,1,0:T(8,128)(2,1)} %fusion.64.q_ref.k_ref.v_ref, bf16[1,2048,768]{2,1,0:T(8,128)(2,1)} %fusion.64.q_ref.k_ref.v_ref, bf16[1,2048,256]{2,1,0:T(8,128)(2,1)S(1)} %copy-done.6, ...), custom_call_target="tpu_custom_call" | custom-call | flops 21474836480 | bytes 8388608 | tf_op jit(solution)/shard_map/attend_back/pallas_call | solution.py:288
  404.0 49.8 %reduce-scatter.40.cloned.1.call-done = bf16[128,2048]{1,0:T(8,128)(2,1)} async-done(((bf16[1024,2048]{1,0:T(8,128)(2,1)}), bf16[128,2048]{1,0:T(8,128)(2,1)}) %reduce-scatter.40.cloned.1.call-update) | async-done | bytes 524304
  468.8 59.6 %reduce-scatter.32.cloned.1.call-done = bf16[128,4096]{1,0:T(8,128)(2,1)} async-done(((bf16[1024,4096]{1,0:T(8,128)(2,1)}), bf16[128,4096]{1,0:T(8,128)(2,1)}) %reduce-scatter.32.cloned.1.call-update) | async-done | bytes 1048592 | tf_op jit(solution)/shard_map/reduce_scatter | solution.py:545
  528.6 10.3 %fusion.56 = bf16[1,512,1024]{2,1,0:T(8,128)(2,1)} fusion(f32[512,1024]{1,0:T(8,128)S(1)} %copy-done.18, bf16[512,4096]{1,0:T(8,128)(2,1)} %copy-done.11, bf16[4096,1024]{1,0:T(8,128)(2,1)} %down_ref.1), kind=kOutput, calls=%fused_computation.96 | convolution fusion | flops 4296015872 | bytes 15728640 | tf_op jit(solution)/shard_map/dot_general | solution.py:25
  551.7 14.2 %collective-permute-done.22 = bf16[1,1,256,1024]{3,2,1,0:T(8,128)(2,1)S(1)} collective-permute-done((bf16[1,1,256,1024]{3,2,1,0:T(8,128)(2,1)S(1)}, bf16[1,1,256,1024]{3,2,1,0:T(8,128)(2,1)S(1)}, u32[]{:S(2)}, u32[]{:S(2)}) %collective-permute-start.22) | collective-permute-done | bytes 524320 | tf_op jit(solution)/shard_map/ppermute | solution.py:363
  567.2 28.3 %collective-permute-done.17 = bf16[1,512,768]{2,1,0:T(8,128)(2,1)S(1)} collective-permute-done((bf16[1,512,768]{2,1,0:T(8,128)(2,1)S(1)}, bf16[1,512,768]{2,1,0:T(8,128)(2,1)S(1)}, u32[]{:S(2)}, u32[]{:S(2)}) %collective-permute-start.17) | collective-permute-done | bytes 786464 | tf_op jit(solution)/shard_map/ppermute | solution.py:363
  596.5 32.7 %collective-permute-done.18 = bf16[1,512,768]{2,1,0:T(8,128)(2,1)S(1)} collective-permute-done((bf16[1,512,768]{2,1,0:T(8,128)(2,1)S(1)}, bf16[1,512,768]{2,1,0:T(8,128)(2,1)S(1)}, u32[]{:S(2)}, u32[]{:S(2)}) %collective-permute-start.18) | collective-permute-done | bytes 786464 | tf_op jit(solution)/shard_map/ppermute | solution.py:363
  633.3 9.5 %fusion.18 = (f32[1024]{0:T(1024)}, f32[512]{0:T(512)S(1)}, f32[512]{0:T(512)S(1)}, f32[512,1024]{1,0:T(8,128)}) fusion(bf16[1,512,1024]{2,1,0:T(8,128)(2,1)S(1)} %copy-done.21, f32[512]{0:T(512)S(1)} %copy-done.53, f32[512]{0:T(512)S(1)} %copy-done.45, f32[1024]{0:T(1024)S(1)} %copy-done.43, bf16[512,3072]{1,0:T(8,128)(2,1)} %bitcast_dynamic-update-slice_fusion, ...), kind=kOutput, calls=%fused_computation.34 | convolution fusion | flops 3225942016 | bytes 12599296 | tf_op jit(solution)/shard_map/dot_general | solution.py:19
  652.7 41.0 %all-reduce = (f32[1024]{0:T(1024)}, f32[1024]{0:T(1024)}, f32[1024]{0:T(1024)}) all-reduce(f32[1024]{0:T(1024)} %get-tuple-element.72, f32[1024]{0:T(1024)} %get-tuple-element.70, f32[1024]{0:T(1024)} %get-tuple-element.68), channel_id=1, replica_groups=mesh['page'=8,'blk'=4] {'page','blk'}, use_global_device_ids=true, to_apply=%region_20.21 | all-reduce | flops 3072 | bytes 24576 | tf_op jit(solution)/shard_map/psum | solution.py:563
  700.6 9.0 %reduce-scatter.20.cloned.1.call-done = bf16[128,256]{1,0:T(8,128)(2,1)} async-done(((bf16[128,1024]{1,0:T(8,128)(2,1)}), bf16[128,256]{1,0:T(8,128)(2,1)}) %reduce-scatter.20.cloned.1.call-update) | async-done | bytes 65552 | tf_op jit(solution)/shard_map/reduce_scatter | solution.py:550
  711.1 21.0 %reduce-scatter.26.cloned.1.call-done = bf16[128,512]{0,1:T(8,128)(2,1)} async-done(((bf16[128,2048]{0,1:T(8,128)(2,1)}), bf16[128,512]{0,1:T(8,128)(2,1)}) %reduce-scatter.26.cloned.1.call-update) | async-done | bytes 131088 | tf_op jit(solution)/shard_map/reduce_scatter | solution.py:550
  733.8 27.9 %reduce-scatter.34.cloned.1.call-done = bf16[128,1024]{1,0:T(8,128)(2,1)} async-done(((bf16[128,4096]{1,0:T(8,128)(2,1)}), bf16[128,1024]{1,0:T(8,128)(2,1)}) %reduce-scatter.34.cloned.1.call-update) | async-done | bytes 262160 | tf_op jit(solution)/shard_map/reduce_scatter | solution.py:550
  763.6 26.3 %reduce-scatter.38.cloned.1.call-done = bf16[512,256]{1,0:T(8,128)(2,1)} async-done(((bf16[512,1024]{1,0:T(8,128)(2,1)}), bf16[512,256]{1,0:T(8,128)(2,1)}) %reduce-scatter.38.cloned.1.call-update) | async-done | bytes 262160 | tf_op jit(solution)/shard_map/reduce_scatter | solution.py:550
  (342 shorter events, 239.9 us)
Async XLA Ops:
  7.2 394.7 %reduce-scatter.22.cloned.1.call-start = ((), (), s32[]{:S(2)}) async-start(), calls=%async_computation.16 | async-start | bytes 2359296 | tf_op jit(solution)/shard_map/reduce_scatter | solution.py:545
  7.2 47.5 %collective-permute-start.7 = (bf16[1,256,1024]{2,1,0:T(8,128)(2,1)}, bf16[1,256,1024]{2,1,0:T(8,128)(2,1)}, u32[]{:S(2)}, u32[]{:S(2)}) collective-permute-start(bf16[1,256,1024]{2,1,0:T(8,128)(2,1)} %param.15), channel_id=1, source_target_pairs={{0,1},{1,2},{2,3},{3,0},{4,5},{5,6},{6,7},{7,4},{8,9},{9,10},{10,1... | collective-permute-start | bytes 1572872 | tf_op jit(solution)/shard_map/ppermute | solution.py:363
  8.6 44.0 %collective-permute-start.8 = (bf16[1,256,1024]{2,1,0:T(8,128)(2,1)}, bf16[1,256,1024]{2,1,0:T(8,128)(2,1)}, u32[]{:S(2)}, u32[]{:S(2)}) collective-permute-start(bf16[1,256,1024]{2,1,0:T(8,128)(2,1)} %param.15), channel_id=1, source_target_pairs={{0,3},{1,0},{2,1},{3,2},{4,7},{5,4},{6,5},{7,6},{8,11},{9,8},{10,9... | collective-permute-start | bytes 1572872 | tf_op jit(solution)/shard_map/ppermute | solution.py:363
  13.6 75.2 %collective-permute-start = (bf16[1,512,1024]{2,1,0:T(8,128)(2,1)}, bf16[1,512,1024]{2,1,0:T(8,128)(2,1)}, u32[]{:S(2)}, u32[]{:S(2)}) collective-permute-start(bf16[1,512,1024]{2,1,0:T(8,128)(2,1)} %param.14), channel_id=1, source_target_pairs={{0,1},{1,2},{2,3},{3,0},{4,5},{5,6},{6,7},{7,4},{8,9},{9,10},{10,1... | collective-permute-start | bytes 3145736 | tf_op jit(solution)/shard_map/ppermute | solution.py:363
  50.6 41.4 %collective-permute-start.1 = (bf16[1,512,1024]{2,1,0:T(8,128)(2,1)S(1)}, bf16[1,512,1024]{2,1,0:T(8,128)(2,1)}, u32[]{:S(2)}, u32[]{:S(2)}) collective-permute-start(bf16[1,512,1024]{2,1,0:T(8,128)(2,1)S(1)} %copy-done.20), channel_id=1, source_target_pairs={{0,3},{1,0},{2,1},{3,2},{4,7},{5,4},{6,5},{7,6},{8,11},{9,8},{10,9... | collective-permute-start | bytes 3145736 | tf_op jit(solution)/shard_map/ppermute | solution.py:363
  269.9 132.8 %reduce-scatter.28.cloned.1.call-start = ((), (), s32[]{:S(2)}) async-start(), calls=%async_computation.19 | async-start | bytes 2359296 | tf_op jit(solution)/shard_map/reduce_scatter | solution.py:545
  274.5 128.9 %reduce-scatter.18.cloned.1.call-start = ((), (), s32[]{:S(2)}) async-start(), calls=%async_computation.14 | async-start | bytes 2359296 | tf_op jit(solution)/shard_map/reduce_scatter | solution.py:545
  282.8 171.0 %reduce-scatter.40.cloned.1.call-start = ((), (), s32[]{:S(2)}) async-start(), calls=%async_computation.25 | async-start | bytes 4718592
  306.2 222.2 %reduce-scatter.32.cloned.1.call-start = ((), (), s32[]{:S(2)}) async-start(), calls=%async_computation.21 | async-start | bytes 9437184 | tf_op jit(solution)/shard_map/reduce_scatter | solution.py:545
  315.3 317.9 %reduce-scatter.36.cloned.1.call-start = ((), (), s32[]{:S(2)}) async-start(), calls=%async_computation.23 | async-start | bytes 9437184 | tf_op jit(solution)/shard_map/reduce_scatter | solution.py:545
  325.6 319.6 %reduce-scatter.16.cloned.1.call-start = ((), (), s32[]{:S(2)}) async-start(), calls=%async_computation.13 | async-start | bytes 1769472 | tf_op jit(solution)/shard_map/reduce_scatter | solution.py:545
  401.9 295.7 %reduce-scatter.24.cloned.1.call-start = ((), (), s32[]{:S(2)}) async-start(), calls=%async_computation.17 | async-start | bytes 327680 | tf_op jit(solution)/shard_map/reduce_scatter | solution.py:550
  402.6 296.5 %reduce-scatter.30.cloned.1.call-start = ((), (), s32[]{:S(2)}) async-start(), calls=%async_computation.20 | async-start | bytes 327680 | tf_op jit(solution)/shard_map/reduce_scatter | solution.py:550
  403.4 306.2 %reduce-scatter.20.cloned.1.call-start = ((), (), s32[]{:S(2)}) async-start(), calls=%async_computation.15 | async-start | bytes 327680 | tf_op jit(solution)/shard_map/reduce_scatter | solution.py:550
  403.9 328.2 %reduce-scatter.26.cloned.1.call-start = ((), (), s32[]{:S(2)}) async-start(), calls=%async_computation.18 | async-start | bytes 655360 | tf_op jit(solution)/shard_map/reduce_scatter | solution.py:550
  455.9 305.9 %reduce-scatter.34.cloned.1.call-start = ((), (), s32[]{:S(2)}) async-start(), calls=%async_computation.22 | async-start | bytes 1310720 | tf_op jit(solution)/shard_map/reduce_scatter | solution.py:550
  466.7 81.7 %collective-permute-start.20 = (bf16[1,1,256,1024]{3,2,1,0:T(8,128)(2,1)}, bf16[1,1,256,1024]{3,2,1,0:T(8,128)(2,1)}, u32[]{:S(2)}, u32[]{:S(2)}) collective-permute-start(bf16[1,1,256,1024]{3,2,1,0:T(8,128)(2,1)} %get-tuple-element.85), channel_id=1, source_target_pairs={{0,2},{1,3},{2,0},{3,1},{4,6},{5,7},{6,4},{7,5},{8,10},{9,11},{10,... | collective-permute-start | bytes 1572872 | tf_op jit(solution)/shard_map/ppermute | solution.py:363
  528.5 261.4 %reduce-scatter.38.cloned.1.call-start = ((), (), s32[]{:S(2)}) async-start(), calls=%async_computation.24 | async-start | bytes 1310720 | tf_op jit(solution)/shard_map/reduce_scatter | solution.py:550
  540.4 55.1 %collective-permute-start.17 = (bf16[1,512,768]{2,1,0:T(8,128)(2,1)S(1)}, bf16[1,512,768]{2,1,0:T(8,128)(2,1)S(1)}, u32[]{:S(2)}, u32[]{:S(2)}) collective-permute-start(bf16[1,512,768]{2,1,0:T(8,128)(2,1)S(1)} %get-tuple-element.82), channel_id=1, source_target_pairs={{0,2},{1,3},{2,0},{3,1},{4,6},{5,7},{6,4},{7,5},{8,10},{9,11},{10,... | collective-permute-start | bytes 2359304 | tf_op jit(solution)/shard_map/ppermute | solution.py:363
  544.0 85.2 %collective-permute-start.18 = (bf16[1,512,768]{2,1,0:T(8,128)(2,1)S(1)}, bf16[1,512,768]{2,1,0:T(8,128)(2,1)S(1)}, u32[]{:S(2)}, u32[]{:S(2)}) collective-permute-start(bf16[1,512,768]{2,1,0:T(8,128)(2,1)S(1)} %get-tuple-element.81), channel_id=1, source_target_pairs={{0,1},{1,2},{2,3},{3,0},{4,5},{5,6},{6,7},{7,4},{8,9},{9,10},{10,1... | collective-permute-start | bytes 2359304 | tf_op jit(solution)/shard_map/ppermute | solution.py:363
  548.4 83.9 %collective-permute-start.19 = (bf16[1,512,768]{2,1,0:T(8,128)(2,1)S(1)}, bf16[1,512,768]{2,1,0:T(8,128)(2,1)S(1)}, u32[]{:S(2)}, u32[]{:S(2)}) collective-permute-start(bf16[1,512,768]{2,1,0:T(8,128)(2,1)S(1)} %get-tuple-element.80), channel_id=1, source_target_pairs={{0,3},{1,0},{2,1},{3,2},{4,7},{5,4},{6,5},{7,6},{8,11},{9,8},{10,9... | collective-permute-start | bytes 2359304 | tf_op jit(solution)/shard_map/ppermute | solution.py:363
  645.2 48.9 %collective-permute-start.23 = (bf16[128,768]{1,0:T(8,128)(2,1)}, bf16[128,768]{1,0:T(8,128)(2,1)}, u32[]{:S(2)}, u32[]{:S(2)}) collective-permute-start(bf16[128,768]{1,0:T(8,128)(2,1)} %reduce-scatter.16.cloned.1.call-done), channel_id=1, source_target_pairs={{0,1},{1,2},{2,3},{3,0},{4,5},{5,6},{6,7},{7,4},{8,9},{9,10},{10,1... | collective-permute-start | bytes 589832 | tf_op jit(solution)/shard_map/ppermute | solution.py:363
  646.4 48.8 %collective-permute-start.24 = (bf16[128,768]{1,0:T(8,128)(2,1)}, bf16[128,768]{1,0:T(8,128)(2,1)}, u32[]{:S(2)}, u32[]{:S(2)}) collective-permute-start(bf16[128,768]{1,0:T(8,128)(2,1)} %reduce-scatter.16.cloned.1.call-done), channel_id=1, source_target_pairs={{0,2},{1,3},{2,0},{3,1},{4,6},{5,7},{6,4},{7,5},{8,10},{9,11},{10,... | collective-permute-start | bytes 589832 | tf_op jit(solution)/shard_map/ppermute | solution.py:363
  647.5 48.8 %collective-permute-start.25 = (bf16[128,768]{1,0:T(8,128)(2,1)}, bf16[128,768]{1,0:T(8,128)(2,1)S(1)}, u32[]{:S(2)}, u32[]{:S(2)}) collective-permute-start(bf16[128,768]{1,0:T(8,128)(2,1)} %reduce-scatter.16.cloned.1.call-done), channel_id=1, source_target_pairs={{0,3},{1,0},{2,1},{3,2},{4,7},{5,4},{6,5},{7,6},{8,11},{9,8},{10,9... | collective-permute-start | bytes 589832 | tf_op jit(solution)/shard_map/ppermute | solution.py:363
  (84 other events, 1187.2 us)
Sparse Core Ops, SparseCore 0:
  270.0 39.3 reduce-scatter.21
  313.1 41.2 reduce-scatter.27
  357.6 41.2 reduce-scatter.17
  402.5 51.3 reduce-scatter.39
  457.2 71.2 reduce-scatter.31
  532.1 71.2 reduce-scatter.35
  606.7 38.4 reduce-scatter.15
  647.5 21.7 reduce-scatter.23
  671.6 17.7 reduce-scatter.29
  691.5 18.0 reduce-scatter.19
  712.0 20.1 reduce-scatter.25
  734.4 27.3 reduce-scatter.33
  764.1 25.7 reduce-scatter.37

commit v2 on v1

v2 whole, which is shorter than its diff:
```python
import functools

import jax
import jax.numpy as jnp
from jax import lax
from jax.experimental import pallas as pl
from jax.experimental.pallas import tpu as pltpu
from jax.sharding import PartitionSpec as P

HEADS = 16
HEAD_DIM = 64
LANES = 128

norm_eps = 1e-05
masked_score = -1e30


def nt(left, right):
    return lax.dot_general(
        left, right, (((1,), (1,)), ((), ())), preferred_element_type=jnp.float32
    )


def nn(left, right):
    return lax.dot_general(
        left, right, (((1,), (0,)), ((), ())), preferred_element_type=jnp.float32
    )


def tn(left, right):
    return lax.dot_general(
        left, right, (((0,), (0,)), ((), ())), preferred_element_type=jnp.float32
    )


def lane_of(shape):
    return lax.broadcasted_iota(jnp.int32, shape, len(shape) - 1)


def own_lanes(shape, head):
    lane = lane_of(shape)
    return lane < HEAD_DIM if head == 0 else lane >= HEAD_DIM


def spare_lane(shape, head):
    return lane_of(shape) - (HEAD_DIM if head == 0 else 0)


def three_parts(column):
    high = column.astype(jnp.bfloat16)
    rest = column - high.astype(jnp.float32)
    middle = rest.astype(jnp.bfloat16)
    low = (rest - middle.astype(jnp.float32)).astype(jnp.bfloat16)
    return high, middle, low


safe_score = 40.0


def forward_kernel(heads, causal, tq, tk, q_ref, k_ref, v_ref, *rest):
    if causal:
        bias_ref = None
        mixed_ref, qx_ref, kx, vx, totals, tops, reach = rest
    else:
        bias_ref, mixed_ref, qx_ref, kx, vx, totals, tops, reach = rest
    step = pl.program_id(2)
    keys = k_ref.shape[0]
    scale = HEAD_DIM ** (-0.5)

    def longest(rows):
        square = rows.astype(jnp.float32)
        square = (square * square).astype(jnp.bfloat16)
        pick = lax.broadcasted_iota(jnp.int32, (16, LANES), 0)
        own = lax.broadcasted_iota(jnp.int32, (16, LANES), 1) // HEAD_DIM == pick
        lengths = nt(own.astype(jnp.float32).astype(jnp.bfloat16), square)
        return [jnp.max(lengths[h : h + 1]) * 1.05 for h in range(heads)]

    @pl.when(step == 0)
    def _():
        turned = v_ref[...].astype(jnp.float32).T.astype(jnp.bfloat16)
        ones = jnp.ones((16, keys), jnp.bfloat16)
        k = k_ref[...]
        lengths = longest(k)
        for h in range(heads):
            vx[h, :HEAD_DIM] = turned[h * HEAD_DIM : (h + 1) * HEAD_DIM]
            vx[h, HEAD_DIM:] = ones
            filler = jnp.zeros_like(k) if causal else bias_ref[...]
            kx[h] = jnp.where(own_lanes(k.shape, h), k, filler)
            reach[h] = lengths[h]

    q = q_ref[...] * jnp.bfloat16(scale)
    q_heads = []
    for h in range(heads):
        one = (spare_lane(q.shape, h) == 0).astype(jnp.float32).astype(jnp.bfloat16)
        q_heads.append(jnp.where(own_lanes(q.shape, h), q, one))
    lengths = longest(q)
    small = lengths[0] * reach[0] < safe_score * safe_score
    if heads == 2:
        small = jnp.logical_and(small, lengths[1] * reach[1] < safe_score * safe_score)

    def scores_of(h, start, masked):
        scores = nt(kx[h, pl.ds(start, tk), :], q_heads[h])
        if masked:
            key_at = start + lax.broadcasted_iota(jnp.int32, scores.shape, 0)
            query_at = step * tq + lax.broadcasted_iota(jnp.int32, scores.shape, 1)
            scores = jnp.where(key_at <= query_at, scores, masked_score)
        return scores

    def plain_tile(j, carry, masked):
        start = pl.multiple_of(j * tk, tk)
        out = []
        for h in range(heads):
            raised = jnp.exp(scores_of(h, start, masked)).astype(jnp.bfloat16)
            out.append(carry[h] + nn(vx[h, :, pl.ds(start, tk)], raised))
        return tuple(out)

    def careful_tile(j, carry, masked):
        start = pl.multiple_of(j * tk, tk)
        out = []
        for h in range(heads):
            largest, total = carry[h]
            scores = scores_of(h, start, masked)
            new_largest = jnp.maximum(largest, jnp.max(scores, axis=0, keepdims=True))
            raised = jnp.exp(scores - new_largest).astype(jnp.bfloat16)
            part = nn(vx[h, :, pl.ds(start, tk)], raised)
            out.append((new_largest, total * jnp.exp(largest - new_largest) + part))
        return tuple(out)

    def over_tiles(tile, carry):
        if causal:
            full = step * tq // tk
            carry = lax.fori_loop(0, full, lambda j, c: tile(j, c, False), carry)
            for extra in range(max(tq // tk, 1)):
                carry = tile(full + extra, carry, True)
            return carry
        for j in range(keys // tk):
            carry = tile(j, carry, False)
        return carry

    zeros = jnp.zeros((HEAD_DIM + 16, tq), jnp.float32)

    @pl.when(small)
    def _():
        carry = over_tiles(plain_tile, (zeros,) * heads)
        for h in range(heads):
            totals[h] = carry[h]
            tops[h] = jnp.zeros((8, tq), jnp.float32)

    @pl.when(jnp.logical_not(small))
    def _():
        lowest = jnp.full((1, tq), masked_score, jnp.float32)
        carry = over_tiles(careful_tile, ((lowest, zeros),) * heads)
        for h in range(heads):
            totals[h] = carry[h][1]
            tops[h] = jnp.broadcast_to(carry[h][0], (8, tq))

    blended, columns = [], []
    for h in range(heads):
        sums = totals[h, HEAD_DIM : HEAD_DIM + 1]
        blended.append(totals[h, :HEAD_DIM] / sums)
        columns.append(-(tops[h, :1] + jnp.log(sums)))
    if heads == 1:
        blended.append(jnp.zeros_like(blended[0]))
    mixed_ref[...] = jnp.concatenate(blended, 0).T.astype(mixed_ref.dtype)
    for h in range(heads):
        turned = jnp.broadcast_to(columns[h], (LANES, tq)).T
        high, middle, low = three_parts(turned)
        place = spare_lane(q.shape, h)
        qx = jnp.where(own_lanes(q.shape, h), q, jnp.zeros_like(q))
        qx = jnp.where(place == 0, jnp.ones_like(q), qx)
        qx = jnp.where(place == 1, high, qx)
        qx = jnp.where(place == 2, middle, qx)
        qx_ref[:, h * LANES : (h + 1) * LANES] = jnp.where(place == 3, low, qx)


def backward_kernel(heads, causal, tq, tk, parts, place_ref, qx_ref, k_ref, v_ref, o_ref, *rest):
    do_refs, rest = rest[:parts], rest[parts:]
    bias_ref = None
    if causal:
        packed_ref, kx, kt, vx, dx, dqt = rest
    else:
        bias_ref, dq_ref, packed_ref, kx, kt, vx, dx, dqt = rest
    queries, keys = qx_ref.shape[0], k_ref.shape[0]
    scale = HEAD_DIM ** (-0.5)
    first = 1 if causal else 0
    count = packed_ref.shape[0]
    block = keys // count

    def relative(owner):
        return lax.rem(owner - place_ref[0] + count, count) if count > 1 else 0

    k = k_ref[...]
    v = v_ref[...]
    kt[...] = (k.astype(jnp.float32) * scale).T.astype(jnp.bfloat16)
    for h in range(heads):
        own = own_lanes(k.shape, h)
        place = spare_lane(k.shape, h)
        ones = jnp.ones_like(k)
        bias = jnp.zeros_like(k) if causal else bias_ref[...]
        kx[h] = jnp.where(own, k, jnp.where(place == 0, bias, ones))
        vx[h] = jnp.where(own, v, ones)
    for part, do_ref in enumerate(do_refs):
        do = do_ref[...]
        size = do.shape[0]
        source = lax.rem(place_ref[0] - part + parts, parts) if parts > 1 else 0
        rows = pl.ds(pl.multiple_of(source * size, size), size)
        product = do.astype(jnp.float32) * o_ref[rows, :].astype(jnp.float32)
        for h in range(heads):
            own = own_lanes(do.shape, h)
            place = spare_lane(do.shape, h)
            delta = jnp.sum(jnp.where(own, product, 0.0), axis=1, keepdims=True)
            high, middle, low = three_parts(jnp.broadcast_to(-delta, do.shape))
            value = jnp.where(own, do, jnp.zeros_like(do))
            value = jnp.where(place == 0, high, value)
            value = jnp.where(place == 1, middle, value)
            dx[h, rows, :] = jnp.where(place == 2, low, value)

    dqt[...] = jnp.zeros_like(dqt)

    def tile(i, j, masked, sums):
        q_at = pl.multiple_of(i * tq, tq)
        k_at = pl.multiple_of(j * tk, tk)
        out = []
        for h in range(heads):
            qx = qx_ref[pl.ds(q_at, tq), h * LANES : (h + 1) * LANES]
            shares = jnp.exp(nt(kx[h, pl.ds(k_at, tk), :], qx))
            if masked:
                key_at = k_at + lax.broadcasted_iota(jnp.int32, shares.shape, 0)
                query_at = q_at + lax.broadcasted_iota(jnp.int32, shares.shape, 1)
                shares = jnp.where(key_at <= query_at, shares, 0.0)
            grad = dx[h, pl.ds(q_at, tq), :]
            d_shares = nt(vx[h, pl.ds(k_at, tk), :], grad)
            d_scores = (shares * d_shares).astype(jnp.bfloat16)
            dv = nn(shares.astype(jnp.bfloat16), grad)
            dk = nn(d_scores, qx)
            rows = pl.ds(h * HEAD_DIM, HEAD_DIM)
            dqt[rows, pl.ds(q_at, tq)] += nn(kt[rows, pl.ds(k_at, tk)], d_scores)
            if sums is not None:
                dk, dv = sums[h][0] + dk, sums[h][1] + dv
            out.append((dk, dv))
        return tuple(out)

    def finish(j, sums):
        dk, dv = sums[0]
        if heads == 2:
            own = own_lanes(dk.shape, 0)
            dk, dv = jnp.where(own, dk, sums[1][0]), jnp.where(own, dv, sums[1][1])
        dk, dv = dk.astype(packed_ref.dtype), dv.astype(packed_ref.dtype)
        if count == 1:
            k_at = pl.multiple_of(j * tk, tk)
            packed_ref[0, first, pl.ds(k_at, tk), :] = dk
            packed_ref[0, first + 1, pl.ds(k_at, tk), :] = dv
        for part in range(tk // block):
            at = relative(j * (tk // block) + part)
            packed_ref[at, first] = dk[part * block : (part + 1) * block]
            packed_ref[at, first + 1] = dv[part * block : (part + 1) * block]

    if causal:

        @pl.loop(0, keys // tk)
        def _(j):
            sums = tile(j, j, True, None)
            sums = lax.fori_loop(
                j + 1, queries // tq, lambda i, s: tile(i, j, False, s), sums
            )
            finish(j, sums)

        for owner in range(count):
            turned = dqt[:, owner * block : (owner + 1) * block].T
            packed_ref[relative(owner), 0] = turned.astype(packed_ref.dtype)
    else:
        for j in range(keys // tk):
            sums = None
            for i in range(queries // tq):
                sums = tile(i, j, False, sums)
            finish(j, sums)
        dq_ref[...] = dqt[...].T.astype(dq_ref.dtype)


def tile_of(rows, largest):
    return rows if rows < largest else largest


def attend_specs(kv, causal, queries, blocks, at=0):
    keys = kv.shape[-2]
    if causal:
        kind = lambda rows, t, i: pl.BlockSpec(
            (None, None, rows, LANES), lambda p, b, *s: (p, t, s[i] if i is not None else 0, at + b)
        )
        return kind(queries, 0, 0), kind(keys, 1, None), kind(keys, 2, None)
    half = lambda at: pl.BlockSpec((None, keys, LANES), lambda p, b, *s: (p, 0, at + b))
    return None, half(0), half(blocks)


def attend(q, kv, bias, heads, blocks, tq, tk, bias_at=0):
    causal = bias is None
    pages, queries, keys = q.shape[0], q.shape[-2], kv.shape[-2]
    tq, tk = tile_of(queries, tq), tile_of(keys, tk)
    q_spec, k_spec, v_spec = attend_specs(kv, causal, tq, blocks)
    args = [q, kv, kv]
    if causal:
        in_specs = [q_spec, k_spec, v_spec]
    else:
        in_specs = [
            pl.BlockSpec((None, tq, LANES), lambda p, b, i: (p, i, b)),
            k_spec,
            v_spec,
            pl.BlockSpec((None, keys, LANES), lambda p, b, i: (p, 0, bias_at)),
        ]
        args.append(bias)
    elements = pages * blocks * heads * queries * keys // (2 if causal else 1)
    return pl.pallas_call(
        functools.partial(forward_kernel, heads, causal, tq, tk),
        grid=(pages, blocks, queries // tq),
        in_specs=in_specs,
        out_specs=[
            pl.BlockSpec((None, tq, LANES), lambda p, b, i: (p, i, b)),
            pl.BlockSpec((None, tq, heads * LANES), lambda p, b, i: (p, i, b)),
        ],
        out_shape=[
            jax.ShapeDtypeStruct((pages, queries, blocks * LANES), jnp.bfloat16),
            jax.ShapeDtypeStruct((pages, queries, blocks * heads * LANES), jnp.bfloat16),
        ],
        scratch_shapes=[
            pltpu.VMEM((heads, keys, LANES), jnp.bfloat16),
            pltpu.VMEM((heads, HEAD_DIM + 16, keys), jnp.bfloat16),
            pltpu.VMEM((heads, HEAD_DIM + 16, tq), jnp.float32),
            pltpu.VMEM((heads, 8, tq), jnp.float32),
            pltpu.SMEM((2,), jnp.float32),
        ],
        compiler_params=pltpu.CompilerParams(vmem_limit_bytes=40 << 20),
        cost_estimate=pl.CostEstimate(
            flops=elements * 40, bytes_accessed=1 << 18, transcendentals=0
        ),
        name="attend",
    )(*args)


def attend_back(
    place, qx, kv, mixed, d_mixed, bias, heads, blocks, tq, tk, count, bias_at=0, at=0
):
    causal = bias is None
    pages, queries = qx.shape[:2]
    keys = kv.shape[-2]
    tq, tk = tile_of(queries, tq), tile_of(keys, tk)
    _, k_spec, v_spec = attend_specs(kv, causal, tq, blocks, at)
    whole = lambda rows, lanes: pl.BlockSpec((None, rows, lanes), lambda p, b, s: (p, 0, b))
    read = lambda rows, lanes: pl.BlockSpec((None, rows, lanes), lambda p, b, s: (p, 0, at + b))
    in_specs = [read(queries, heads * LANES), k_spec, v_spec, read(queries, LANES)]
    in_specs += [read(part.shape[1], LANES) for part in d_mixed]
    args = [place, qx, kv, kv, mixed, *d_mixed]
    kinds = 3 if causal else 2
    out_specs = [
        pl.BlockSpec((None, count, kinds, keys // count, LANES), lambda p, b, s: (p, 0, 0, 0, b))
    ]
    out_shape = [
        jax.ShapeDtypeStruct((pages, count, kinds, keys // count, blocks * LANES), jnp.bfloat16)
    ]
    if not causal:
        in_specs.append(pl.BlockSpec((None, keys, LANES), lambda p, b, s: (p, 0, bias_at)))
        args.append(bias)
        out_specs.insert(0, whole(queries, LANES))
        out_shape.insert(0, jax.ShapeDtypeStruct((pages, queries, blocks * LANES), jnp.bfloat16))
    elements = pages * blocks * heads * queries * keys // (2 if causal else 1)
    return pl.pallas_call(
        functools.partial(backward_kernel, heads, causal, tq, tk, len(d_mixed)),
        grid_spec=pltpu.PrefetchScalarGridSpec(
            num_scalar_prefetch=1,
            grid=(pages, blocks),
            in_specs=in_specs,
            out_specs=out_specs,
            scratch_shapes=[
                pltpu.VMEM((heads, keys, LANES), jnp.bfloat16),
                pltpu.VMEM((LANES, keys), jnp.bfloat16),
                pltpu.VMEM((heads, keys, LANES), jnp.bfloat16),
                pltpu.VMEM((heads, queries, LANES), jnp.bfloat16),
                pltpu.VMEM((LANES, queries), jnp.float32),
            ],
        ),
        out_shape=out_shape,
        compiler_params=pltpu.CompilerParams(vmem_limit_bytes=40 << 20),
        cost_estimate=pl.CostEstimate(
            flops=elements * 50, bytes_accessed=1 << 18, transcendentals=0
        ),
        name="attend_back",
    )(*args)


def mean(values):
    return jnp.mean(values, axis=-1, keepdims=True)


def norm_of(values):
    center = values - mean(values)
    rstd = lax.rsqrt(mean(center * center) + norm_eps)
    return center * rstd, rstd


def norm_back(values, gain, d_normed):
    xhat, rstd = norm_of(values)
    e = d_normed * gain
    d_values = rstd * (e - mean(e) - xhat * mean(e * xhat))
    return d_values, jnp.sum(d_normed * xhat, axis=0, keepdims=True)


def row_call(kernel, name, grid, args, in_specs, outs, flops, scratch=(), aliases=None, prefetch=0):
    out_shape, out_specs = [], []
    for shape, dtype, spec in outs:
        out_shape.append(jax.ShapeDtypeStruct(shape, dtype))
        out_specs.append(spec)
    moved = sum(a.size * a.dtype.itemsize for a in args)
    return pl.pallas_call(
        kernel,
        grid_spec=pltpu.PrefetchScalarGridSpec(
            num_scalar_prefetch=prefetch,
            grid=grid,
            in_specs=in_specs,
            out_specs=out_specs,
            scratch_shapes=list(scratch),
        ),
        out_shape=out_shape,
        input_output_aliases=aliases or {},
        compiler_params=pltpu.CompilerParams(vmem_limit_bytes=48 << 20),
        cost_estimate=pl.CostEstimate(
            flops=flops // 50, bytes_accessed=moved // 50, transcendentals=0
        ),
        name=name,
    )(*args)


def fixed(*shape):
    return pl.BlockSpec(shape, lambda *_: (0,) * len(shape))


def by_rows(tile, columns):
    return pl.BlockSpec((tile, columns), lambda i, *_: (i, 0))


anywhere = pl.BlockSpec(memory_space=pl.ANY)


def enter_kernel(src_ref, x_ref, gain_ref, w_ref, *rest):
    normed_ref, packed_ref = rest[-2:]
    normed = norm_of(x_ref[...].astype(jnp.float32))[0] * gain_ref[...]
    normed = normed.astype(jnp.bfloat16)
    normed_ref[...] = normed
    packed = nn(normed, w_ref[...]).astype(jnp.bfloat16)
    for kind in range(3):
        size = packed_ref.shape[-1]
        packed_ref[kind] = packed[:, kind * size : (kind + 1) * size]


def enter(piece, source, count, gain, weight, kept):
    pages, rows, width = piece.shape
    wide = weight.shape[1] // 3
    out = [
        (
            (pages, rows * count, width),
            jnp.bfloat16,
            pl.BlockSpec((None, rows, width), lambda p, s: (p, s[0], 0)),
        ),
        (
            (pages, 3, rows * count, wide),
            jnp.bfloat16,
            pl.BlockSpec((None, 3, rows, wide), lambda p, s: (p, 0, s[0], 0)),
        ),
    ]
    args = [source, piece, gain, weight]
    specs = [
        pl.BlockSpec((None, rows, width), lambda p, s: (p, 0, 0)),
        fixed(1, width),
        fixed(width, 3 * wide),
    ]
    aliases = {}
    if kept is not None:
        args += list(kept)
        specs += [anywhere] * 2
        aliases = {4: 0, 5: 1}
    flops = 2 * pages * rows * width * 3 * wide
    return row_call(enter_kernel, "enter", (pages,), args, specs, out, flops, (), aliases, 1)


def between_kernel(parts, tile, place_ref, *refs):
    mixed_refs, refs = refs[:parts], refs[parts:]
    tokens_ref, gain_ref, out_ref, q_ref, resid_ref, normed_ref, query_ref, whole_ref = refs
    for part, mixed_ref in enumerate(mixed_refs):
        size = mixed_ref.shape[1]
        source = lax.rem(place_ref[0] - part + parts, parts) if parts > 1 else 0
        whole_ref[:, pl.ds(pl.multiple_of(source * size, size), size)] = mixed_ref[...]
    resid = tokens_ref[...].astype(jnp.float32) + nn(whole_ref[...], out_ref[...])
    resid_ref[...] = resid
    normed = (norm_of(resid)[0] * gain_ref[...]).astype(jnp.bfloat16)
    normed_ref[...] = normed
    query_ref[...] = nn(normed, q_ref[...]).astype(jnp.bfloat16)


def between(place, mixed, tokens, gain, out_weight, q_weight):
    rows, width = tokens.shape
    tile = tile_of(rows, 256)
    row = by_rows(tile, width)
    square = fixed(width, width)
    return row_call(
        functools.partial(between_kernel, len(mixed), tile),
        "between",
        (rows // tile,),
        [place, *mixed, tokens, gain, out_weight, q_weight],
        [by_rows(tile, part.shape[1]) for part in mixed]
        + [row, fixed(1, width), square, square],
        [
            ((rows, width), jnp.float32, row),
            ((rows, width), jnp.bfloat16, row),
            ((rows, width), jnp.bfloat16, row),
            ((rows, width), jnp.bfloat16, row),
        ],
        4 * rows * width * width,
        prefetch=1,
    )


def expand_kernel(
    mixed_ref, resid_ref, gain_ref, out_ref, grad_ref, up_ref, down_ref,
    resid_two_ref, normed_ref, active_ref, d_upward_ref,
):
    @pl.when(pl.program_id(0) == 0)
    def _():
        resid = resid_ref[...] + nn(mixed_ref[...], out_ref[...])
        resid_two_ref[...] = resid
        normed_ref[...] = (norm_of(resid)[0] * gain_ref[...]).astype(jnp.bfloat16)

    upward = nn(normed_ref[...], up_ref[...])
    d_active = nt(grad_ref[...], down_ref[...])
    share = 0.5 * (1.0 + lax.erf(upward * (0.5**0.5)))
    active_ref[...] = (upward * share).astype(active_ref.dtype)
    density = jnp.exp(-0.5 * upward * upward) * 0.3989422804014327
    d_upward_ref[...] = (d_active * (share + upward * density)).astype(d_upward_ref.dtype)


def expand(mixed, resid, gain, out_weight, grad, w_up, w_down):
    rows, width = grad.shape
    wide = w_up.shape[1]
    step = 512
    all_rows = fixed(rows, width)
    column = pl.BlockSpec((rows, step), lambda f: (0, f))
    return row_call(
        expand_kernel,
        "expand",
        (wide // step,),
        [mixed, resid, gain, out_weight, grad, w_up, w_down],
        [
            all_rows,
            all_rows,
            fixed(1, width),
            fixed(width, width),
            all_rows,
            pl.BlockSpec((width, step), lambda f: (0, f)),
            pl.BlockSpec((step, width), lambda f: (f, 0)),
        ],
        [
            ((rows, width), jnp.float32, all_rows),
            ((rows, width), jnp.bfloat16, all_rows),
            ((rows, wide), jnp.bfloat16, column),
            ((rows, wide), jnp.bfloat16, column),
        ],
        4 * rows * width * wide,
    )


def contract_kernel(
    d_upward_ref, up_ref, resid_ref, grad_ref, gain_ref, out_ref,
    d_resid_ref, branch_ref, d_mixed_ref, d_gain_ref,
):
    step = pl.program_id(0)
    part = nt(d_upward_ref[...], up_ref[...])

    @pl.when(step == 0)
    def _():
        d_resid_ref[...] = part

    @pl.when(step > 0)
    def _():
        d_resid_ref[...] += part

    @pl.when(step == pl.num_programs(0) - 1)
    def _():
        d_values, d_gain_ref[...] = norm_back(resid_ref[...], gain_ref[...], d_resid_ref[...])
        d_resid = grad_ref[...].astype(jnp.float32) + d_values
        d_resid_ref[...] = d_resid
        branch = d_resid.astype(jnp.bfloat16)
        branch_ref[...] = branch
        d_mixed_ref[...] = nt(branch, out_ref[...]).astype(jnp.bfloat16)


def contract(d_upward, w_up, resid, grad, gain, out_weight):
    rows, wide = d_upward.shape
    width = resid.shape[1]
    step = 1024
    all_rows = fixed(rows, width)
    return row_call(
        contract_kernel,
        "contract",
        (wide // step,),
        [d_upward, w_up, resid, grad, gain, out_weight],
        [
            pl.BlockSpec((rows, step), lambda f: (0, f)),
            pl.BlockSpec((width, step), lambda f: (0, f)),
            all_rows,
            all_rows,
            fixed(1, width),
            fixed(width, width),
        ],
        [
            ((rows, width), jnp.float32, all_rows),
            ((rows, width), jnp.bfloat16, all_rows),
            ((rows, width), jnp.bfloat16, all_rows),
            ((1, width), jnp.float32, fixed(1, width)),
        ],
        2 * rows * width * (wide + width),
    )


def between_back_kernel(
    place_ref, d_query_ref, resid_ref, d_resid_ref, gain_ref, q_ref, out_ref,
    d_out_ref, branch_ref, d_mixed_ref, d_gain_ref,
):
    d_values, d_gain = norm_back(
        resid_ref[...], gain_ref[...], nt(d_query_ref[...], q_ref[...])
    )

    @pl.when(pl.program_id(0) == 0)
    def _():
        d_gain_ref[...] = d_gain

    @pl.when(pl.program_id(0) > 0)
    def _():
        d_gain_ref[...] += d_gain

    d_resid = d_resid_ref[...] + d_values
    d_out_ref[...] = d_resid
    branch = d_resid.astype(jnp.bfloat16)
    branch_ref[...] = branch
    count, _, size = d_mixed_ref.shape
    for far in range(count):
        owner = lax.rem(place_ref[0] + far, count)
        weight = out_ref[pl.ds(pl.multiple_of(owner * size, size), size), :]
        d_mixed_ref[far] = nt(branch, weight).astype(jnp.bfloat16)


def between_back(place, d_query, resid, d_resid, gain, q_weight, out_weight, count):
    rows, width = resid.shape
    tile = tile_of(rows, 256)
    row = by_rows(tile, width)
    square = fixed(width, width)
    size = width // count
    return row_call(
        between_back_kernel,
        "between_back",
        (rows // tile,),
        [place, d_query, resid, d_resid, gain, q_weight, out_weight],
        [row, row, row, fixed(1, width), square, square],
        [
            ((rows, width), jnp.float32, row),
            ((rows, width), jnp.bfloat16, row),
            (
                (count, rows, size),
                jnp.bfloat16,
                pl.BlockSpec((count, tile, size), lambda i, s: (0, i, 0)),
            ),
            ((1, width), jnp.float32, fixed(1, width)),
        ],
        4 * rows * width * width,
        prefetch=1,
    )


def leave_kernel(parts, blocks, place_ref, *refs):
    d_packed_refs, refs = refs[: parts * blocks], refs[parts * blocks :]
    w_ref, tokens_ref, d_resid_ref, gain_ref, grad_ref, whole = refs
    kinds = 3
    width = whole.shape[1] // kinds
    for index, d_packed_ref in enumerate(d_packed_refs):
        part, block = index % parts, index // parts
        size = d_packed_ref.shape[-1]
        source = lax.rem(place_ref[0] - part + parts, parts) if parts > 1 else 0
        for kind in range(kinds):
            at = pl.multiple_of(kind * width + (source * blocks + block) * size, size)
            whole[:, pl.ds(at, size)] = d_packed_ref[kind]
    d_normed = nt(whole[...], w_ref[...])
    tokens = tokens_ref[...].astype(jnp.float32)
    grad_ref[...] = d_resid_ref[...] + norm_back(tokens, gain_ref[...], d_normed)[0]


def leave(place, d_packed, blocks, qkv, tokens, d_resid, gain):
    pages, rows, width = tokens.shape
    tile = tile_of(rows, 256)
    row = pl.BlockSpec((None, tile, width), lambda p, i, s: (p, i, 0))
    return row_call(
        functools.partial(leave_kernel, len(d_packed) // blocks, blocks),
        "leave",
        (pages, rows // tile),
        [place, *d_packed, qkv, tokens, d_resid, gain],
        [
            pl.BlockSpec((None, 3, tile, part.shape[-1]), lambda p, i, s: (p, 0, i, 0))
            for part in d_packed
        ]
        + [fixed(width, 3 * width), row, row, fixed(1, width)],
        [((pages, rows, width), jnp.float32, row)],
        6 * pages * rows * width * width,
        [pltpu.VMEM((tile, 3 * width), jnp.bfloat16)],
        prefetch=1,
    )[0]


def turned_rows(me, left, turned, scratch, pages):
    scratch[...] = left.astype(jnp.float32).T.astype(jnp.bfloat16)
    size = scratch.shape[0] // pages
    for place in range(pages):
        odd, upper = place * 2 // pages, place % (pages // 2)
        block = jnp.bitwise_xor(upper * 2 + odd, me)
        at = pl.multiple_of(block * size, size)
        turned[place * size : (place + 1) * size] = scratch[pl.ds(at, size), :]


def grad_kernel(pages, me_ref, left_ref, right_ref, *rest):
    keep_ref, send_ref, turned, scratch = rest[-4:]

    @pl.when(pl.program_id(0) == 0)
    def _():
        turned_rows(me_ref[0], left_ref[...], turned, scratch, pages)

    total = nn(turned[...], right_ref[...]).astype(jnp.bfloat16)
    half = total.shape[0] // 2
    keep_ref[...] = total[:half]
    send_ref[...] = total[half:]


def grad_gain_kernel(pages, blocks, me_ref, left_ref, *rest):
    right_refs, (weight_ref, keep_ref, send_ref, gain_ref, turned, scratch) = (
        rest[:blocks],
        rest[blocks:],
    )

    @pl.when(pl.program_id(0) == 0)
    def _():
        turned_rows(me_ref[0], left_ref[...], turned, scratch, pages)
        gain_ref[...] = jnp.zeros_like(gain_ref)

    count, block, _ = right_refs[0].shape
    total = None
    for far in range(count):
        owner = lax.rem(me_ref[1] + far, count)
        span = pl.ds(pl.multiple_of(owner * block, block), block)
        right = jnp.concatenate([right_ref[far] for right_ref in right_refs], 1)
        part = nn(turned[:, span], right)
        total = part if total is None else total + part
    size = total.shape[0] // pages
    for place in range(pages):
        odd, upper = place * 2 // pages, place % (pages // 2)
        block = jnp.bitwise_xor(upper * 2 + odd, me_ref[0])
        rows = pl.ds(pl.multiple_of(block * size, size), size)
        terms = total[place * size : (place + 1) * size] * weight_ref[rows, :].astype(jnp.float32)
        for lane in range(0, terms.shape[1], LANES):
            gain_ref[rows, :] += terms[:, lane : lane + LANES]
    total = total.astype(jnp.bfloat16)
    half = total.shape[0] // 2
    keep_ref[...] = total[:half]
    send_ref[...] = total[half:]


def grad_with_gain(where, left, rights, weight, pages):
    depth, rows = left.shape
    count, kinds, block, lanes = rights[0].shape
    own = lanes * len(rights)
    half = pl.BlockSpec((rows // 2, own), lambda j, s: (0, j))
    return row_call(
        functools.partial(grad_gain_kernel, pages, len(rights)),
        "grad_gain",
        (kinds,),
        [where, left, *rights, weight],
        [fixed(depth, rows)]
        + [pl.BlockSpec((count, None, block, lanes), lambda j, s: (0, j, 0, 0))] * len(rights)
        + [pl.BlockSpec((rows, own), lambda j, s: (0, j))],
        [
            ((rows // 2, kinds * own), jnp.bfloat16, half),
            ((rows // 2, kinds * own), jnp.bfloat16, half),
            ((rows, LANES), jnp.float32, fixed(rows, LANES)),
        ],
        2 * depth * rows * kinds * own,
        [pltpu.VMEM((rows, depth), jnp.bfloat16)] * 2,
        None,
        1,
    )


def grad_into(kept, columns, where, left, rows, right, right_spec, tiles, tile, pages):
    depth = left.shape[0]
    right_block, right_map, out_map = right_spec
    out = [
        (
            (rows // 2, columns),
            jnp.bfloat16,
            pl.BlockSpec((rows // 2, tile), lambda j, s: (0, out_map(j, s))),
        )
    ] * 2
    args = [where, left, right]
    specs = [fixed(depth, rows), pl.BlockSpec(right_block, right_map)]
    aliases = {}
    if kept is not None:
        args += list(kept)
        specs += [anywhere] * 2
        aliases = {3: 0, 4: 1}
    return row_call(
        functools.partial(grad_kernel, pages),
        "grad",
        (tiles,),
        args,
        specs,
        out,
        2 * depth * rows * tiles * tile,
        [pltpu.VMEM((rows, depth), jnp.bfloat16)] * 2,
        aliases,
        1,
    )


def grad_up_kernel(left_ref, right_ref, out_ref, turned):
    @pl.when(pl.program_id(0) == 0)
    def _():
        turned[...] = left_ref[...].astype(jnp.float32).T.astype(jnp.bfloat16)

    total = nn(turned[...], right_ref[...]).astype(jnp.bfloat16)
    pages, rows, columns = out_ref.shape
    size = total.shape[0] // pages
    for part in range(rows // size):
        piece = total[:, part * columns : (part + 1) * columns]
        out_ref[:, part * size : (part + 1) * size, :] = piece.reshape(pages, size, columns)


def grad_down_kernel(left_ref, right_ref, kept_ref, out_ref):
    turned = left_ref[...].astype(jnp.float32).T.astype(jnp.bfloat16)
    total = nn(turned, right_ref[...]).astype(jnp.bfloat16)
    size = out_ref.shape[-1]
    for place in range(out_ref.shape[0]):
        out_ref[place] = total[:, place * size : (place + 1) * size]


def grad_wide(normed, d_upward, active, grad, count, pages):
    depth, width = normed.shape
    wide = active.shape[1]
    rows, columns = wide // pages, width // count
    subs = wide // count // columns
    shape = (count, pages, 2 * rows, columns)
    (both,) = row_call(
        grad_up_kernel,
        "grad_up",
        (count,),
        [normed, d_upward],
        [fixed(depth, width), pl.BlockSpec((depth, subs * columns), lambda j: (0, j))],
        [
            (
                shape,
                jnp.bfloat16,
                pl.BlockSpec((None, pages, rows, columns), lambda j: (j, 0, 0, 0)),
            )
        ],
        2 * depth * width * wide,
        [pltpu.VMEM((width, depth), jnp.bfloat16)],
    )
    return row_call(
        grad_down_kernel,
        "grad_down",
        (pages,),
        [active, grad, both],
        [pl.BlockSpec((depth, rows), lambda j: (0, j)), fixed(depth, width), anywhere],
        [
            (
                shape,
                jnp.bfloat16,
                pl.BlockSpec((count, None, rows, columns), lambda j: (0, j, 1, 0)),
            )
        ],
        2 * depth * width * wide,
        (),
        {2: 0},
    )[0]


def swapped(value, bit):
    pages = lax.axis_size("page")
    return lax.ppermute(value, "page", [(i, i ^ (1 << bit)) for i in range(pages)])


def added(left, right):
    return (left.astype(jnp.float32) + right.astype(jnp.float32)).astype(jnp.bfloat16)


def halved(keep, send, bit):
    return keep, swapped(send, bit)


def parted(pair, side):
    keep, got = pair
    blocks = 2 if keep.shape[0] % 256 else keep.shape[0] // 128
    shape = (blocks // 2, 2, -1, keep.shape[1]) if side == 1 else (2, blocks // 2, -1, keep.shape[1])
    axis = 1 if side == 1 else 0
    pick = lambda value, half: lax.index_in_dim(
        value.reshape(shape), half, axis, keepdims=False
    ).reshape(-1, keep.shape[1])
    return added(pick(keep, 0), pick(got, 0)), added(pick(keep, 1), pick(got, 1))


def shifted(value, shift):
    count = lax.axis_size("blk")
    return lax.ppermute(value, "blk", [(i, (i + shift) % count) for i in range(count)])


def ring_pieces(value):
    count = lax.axis_size("blk")
    pieces = [(value, 0)]
    right = left = value
    for hop in range(1, (count - 1) // 2 + 1):
        right, left = shifted(right, 1), shifted(left, -1)
        pieces += [(right, -hop), (left, hop)]
    if count % 2 == 0:
        half = value.shape[1] // 2
        if count > 1:
            top, low = shifted(right[:, :half], 1), shifted(left[:, half:], -1)
            pieces.append((jnp.concatenate([top, low], 1), count // 2))
    return pieces


def gathered(pieces, axis):
    count = lax.axis_size("blk")
    place = lax.axis_index("blk")
    size = pieces[0][0].shape[axis]
    shape = list(pieces[0][0].shape)
    shape[axis] = size * count
    whole = jnp.zeros(shape, pieces[0][0].dtype)
    for piece, far in pieces:
        whole = lax.dynamic_update_slice_in_dim(
            whole, piece, (place + far) % count * size, axis
        )
    return whole


def far_first(count):
    return sorted(range(1, count), key=lambda far: -min(far, count - far))


def exchanged(value, split, join):
    count = lax.axis_size("blk")
    place = lax.axis_index("blk")
    size = value.shape[split] // count
    take = lambda far: lax.dynamic_slice_in_dim(
        value, (place + far) % count * size, size, split
    )
    pieces = [(take(0), 0)]
    for far in far_first(count):
        pieces.append((shifted(take(far), far), -far))
    return gathered(pieces, join)


def sent_to_all(value, join):
    count = lax.axis_size("blk")
    pieces = [(value, 0)] + [(shifted(value, far), -far) for far in far_first(count)]
    return gathered(pieces, join)


def together(*values):
    return lax.optimization_barrier(values)


def on_device(
    tokens,
    patches,
    patch_mask,
    gain_one,
    qkv_self,
    out_self,
    gain_two,
    q_cross,
    kv_cross,
    out_cross,
    gain_three,
    w_up,
    w_down,
    cotangent,
):
    pages, token_count, width = tokens.shape
    count = lax.axis_size("blk")
    place = lax.axis_index("blk")
    page_devices = lax.axis_size("page")
    me = lax.axis_index("page")
    rows = pages * token_count
    here = HEADS // count
    heads = 2 if here % 2 == 0 else 1
    blocks = here // heads
    lanes = heads * HEAD_DIM
    own = here * HEAD_DIM
    swift = count == 4 and page_devices == 8 and pages == 1
    where = jnp.stack([me, place]).astype(jnp.int32)
    spot = where[1:]
    gain_one, gain_two, gain_three = (g.reshape(1, width) for g in (gain_one, gain_two, gain_three))

    def cut(value):
        if lanes == LANES:
            return value
        split = value.reshape(value.shape[:-1] + (-1, LANES))[..., :lanes]
        return split.reshape(value.shape[:-1] + (-1,))

    def padded(value):
        if lanes == LANES:
            return value
        split = value.reshape(value.shape[:-1] + (-1, lanes))
        split = jnp.pad(split, [(0, 0)] * (split.ndim - 1) + [(0, LANES - lanes)])
        return split.reshape(value.shape[:-1] + (-1,))

    def received(pieces):
        got = {0: pieces[0]}
        for far in far_first(count):
            got[far] = shifted(pieces[far], far)
        return [got[far] for far in range(count)]

    def ordered(parts, axis):
        if swift:
            return parts
        return [gathered([(part, -far) for far, part in enumerate(parts)], axis)]

    qkv_here = [
        lax.dynamic_slice_in_dim(qkv_self, kind * width + place * own, own, 1) for kind in range(3)
    ]
    qkv_here = padded(jnp.concatenate(qkv_here, 1))

    kept = None
    pieces = ring_pieces(tokens)
    for piece, far in pieces:
        source = ((place + far) % count).astype(jnp.int32).reshape(1)
        kept = enter(piece, source, count, gain_one, qkv_here, kept)
    normed_one, packed = kept
    mixed_here, qx_one = attend(packed, packed, None, heads, blocks, 1024, 512)
    mixed_pieces = [
        lax.dynamic_slice_in_dim(
            cut(mixed_here), (place + far) % count * token_count, token_count, 1
        ).reshape(rows, own)
        for far in range(count)
    ]
    mixed_parts = ordered(received(mixed_pieces), 1)

    dead = jnp.where(patch_mask > 0, 0.0, masked_score).astype(jnp.bfloat16)
    dead = jnp.broadcast_to(dead[:, :, None], dead.shape + (LANES,))
    patches_wide, _ = together(jnp.concatenate([patches, dead], 2), pieces[-1][0])
    patches_all = lax.all_gather(patches_wide, "blk", axis=1, tiled=True)
    bias_at = width // LANES
    page_patches = patches_all.reshape(-1, width + LANES)
    kv_two = nn(page_patches[:, :width], kv_cross).astype(jnp.bfloat16)
    kv_two = kv_two.reshape(pages, -1, 2 * width)

    flat_tokens = tokens.reshape(rows, width)
    resid_one, normed_two, query_two, mixed_one = between(
        spot, mixed_parts, flat_tokens, gain_two, out_self, q_cross
    )
    query_two = query_two.reshape(pages, token_count, width)
    mixed_two, qx_two = attend(
        query_two, kv_two, patches_all, 2, width // LANES, 512, 1024, bias_at
    )
    flat_mixed_two = mixed_two.reshape(rows, width)

    flat_cotangent = cotangent.reshape(rows, width)
    resid_two, normed_three, active, d_upward = expand(
        flat_mixed_two, resid_one, gain_three, out_cross, flat_cotangent, w_up, w_down
    )
    if swift:
        both = grad_wide(normed_three, d_upward, active, flat_cotangent, count, page_devices)
        d_upward, both = together(d_upward, both)
        both = lax.psum_scatter(
            both.reshape(-1, both.shape[-1]), ("blk", "page"), scatter_dimension=0, tiled=True
        ).astype(jnp.float32)

    d_resid_two, branch_two, d_mixed_two, grad_gain_three = contract(
        d_upward, w_up, resid_two, flat_cotangent, gain_three, out_cross
    )
    d_query_two, d_kv_two = attend_back(
        spot,
        qx_two,
        kv_two,
        mixed_two,
        [d_mixed_two.reshape(pages, token_count, width)],
        patches_all,
        2,
        width // LANES,
        512,
        1024,
        1,
        bias_at,
    )
    d_query_two = d_query_two.reshape(rows, width)
    d_resid_one, branch_one, d_mixed_one, grad_gain_two = between_back(
        spot, d_query_two, resid_one, d_resid_two, gain_two, q_cross, out_self, count
    )
    d_mixed_parts = ordered(
        received([d_mixed_one[far].reshape(pages, token_count, own) for far in range(count)]), 1
    )

    if swift:

        def square(at, every, depth):
            return (
                (depth, 256),
                lambda j, s: (0, lax.rem(s[1] + j, count)),
                lambda j, s: j * every + at,
            )

        def key_value(j, s):
            tile = lax.rem(s[1] + j, count)
            return (0, 0, tile // 2, 0, tile % 2)

        depth = page_patches.shape[0]
        first = grad_into(
            None,
            2 * width,
            where,
            page_patches,
            width,
            d_kv_two,
            ((None, None, None, depth, 512), key_value, lambda j, s: j),
            4,
            512,
            page_devices,
        )
        second = None
        for at, (left, right) in enumerate(
            ((flat_mixed_two, branch_two), (normed_two, d_query_two), (mixed_one, branch_one))
        ):
            second = grad_into(
                second, 3 * width, where, left, width, right, square(at, 3, rows), 4, 256, page_devices
            )
        first, second = halved(*first, 0), halved(*second, 0)
        barred = together(*d_mixed_parts, *parted(first, 1), *parted(second, 2))
        d_mixed_parts, barred = list(barred[:count]), barred[count:]
        first, second = halved(*barred[:2], 1), halved(*barred[2:], 2)

    d_packed_here, d_packed = [], []
    for block in range(blocks):
        (grads,) = attend_back(
            spot,
            qx_one,
            packed,
            mixed_here,
            [padded(part) for part in d_mixed_parts],
            None,
            heads,
            1,
            512,
            512,
            count,
            0,
            block,
        )
        grads = cut(grads)
        sent = [grads[:, far] for far in range(count)]
        if swift and block == 1:
            barred = together(grads, *d_packed_here, first[1], second[1], d_kv_two)
            grads, d_packed_here, d_kv_two = barred[0], [barred[1]], barred[4]
            first, second = (first[0], barred[2]), (second[0], barred[3])
            first, second = halved(*parted(first, 1), 2), halved(*parted(second, 1), 1)
            keep, send, gain_rows = grad_with_gain(
                where, normed_one[0], [d_packed_here[0][0], grads[0]], qkv_here, page_devices
            )
            grad_gain_one = jnp.sum(gain_rows, axis=1) / gain_one[0]
            gains = jnp.stack([grad_gain_one, grad_gain_two[0], grad_gain_three[0]])
            third = halved(keep, send, 0)
            gains_got = swapped(gains, 0)
            barred = together(*sent, *d_packed, third[1], gains_got)
            sent, d_packed = list(barred[:count]), list(barred[count : 2 * count])
            third, gains = (third[0], barred[-2]), gains + barred[-1]
        elif swift:
            barred = together(*sent, grads, *d_mixed_parts)
            sent, grads = list(barred[:count]), barred[count]
            d_mixed_parts = list(barred[count + 1 :])
        d_packed_here.append(grads)
        d_packed += ordered(received(sent), 3)
    d_key_two, d_value_two = (d_kv_two[:, 0, kind].reshape(-1, width) for kind in range(2))
    grad_patches = nt(d_key_two, kv_cross[:, :width]) + nt(d_value_two, kv_cross[:, width:])
    grad_patches = grad_patches.astype(jnp.bfloat16).reshape(pages, -1, width)
    if swift:
        grad_patches, both = together(grad_patches, both)
    grad_patches = lax.psum_scatter(grad_patches, "blk", scatter_dimension=1, tiled=True)

    grad_tokens = leave(
        spot, d_packed, blocks, qkv_self, tokens, d_resid_one.reshape(tokens.shape), gain_one
    )

    if swift:
        rows_up = both.shape[0] // 2
        grad_w_up = (
            both[:rows_up]
            .reshape(-1, width // page_devices, both.shape[1])
            .transpose(1, 0, 2)
            .reshape(width // page_devices, -1)
        )
        grad_w_down = both[rows_up:]

        for bit in (1, 2):
            keep, send = parted(third, 1)
            gains, send = together(gains, send)
            third = halved(keep, send, bit)
            gains = gains + swapped(gains, bit)
        qkv_part = added(*third)

        def piece(far):
            kv, rest = slice(far * 512, (far + 1) * 512), slice(far * 768, (far + 1) * 768)
            owner = (place + far) % count
            block = 3 * owner + (place - 3 * owner) % 4
            qkv = lax.dynamic_slice_in_dim(qkv_part, jnp.minimum(block // 4, 2) * 256, 256, 1)
            return [
                added(first[0][:, kv], first[1][:, kv]),
                added(second[0][:, rest], second[1][:, rest]),
                qkv,
            ]

        total = first[0][:, :512].astype(jnp.float32) + first[1][:, :512].astype(jnp.float32)
        rest = second[0][:, :768].astype(jnp.float32) + second[1][:, :768].astype(jnp.float32)
        total = jnp.concatenate([total, rest], 1)
        columns = jnp.zeros((qkv_part.shape[0], 4 * 256), jnp.bfloat16)
        columns = lax.dynamic_update_slice_in_dim(
            columns, piece(0)[2], (place - 3 * place) % 4 * 256, 1
        )
        pieces = together(
            gains, *d_packed[count:], *(jnp.concatenate(piece(far), 1) for far in range(1, count))
        )
        gains, pieces = pieces[0], pieces[1 + count :]
        all_gains = gains
        for far in far_first(count):
            got = shifted(pieces[far - 1], far)
            total += got[:, :1280].astype(jnp.float32)
            columns = lax.dynamic_update_slice_in_dim(
                columns, got[:, 1280:], (place - far - 3 * place) % 4 * 256, 1
            )
            all_gains += shifted(gains, far)
        gains = all_gains
        grad_kv_cross, grad_out_cross = total[:, :512], total[:, 512:768]
        grad_q_cross, grad_out_self = total[:, 768:1024], total[:, 1024:]
        grad_qkv_self = columns[:, :768].astype(jnp.float32)
    else:

        def over_rows(matrix):
            return lax.psum_scatter(
                matrix.astype(jnp.bfloat16), "page", scatter_dimension=0, tiled=True
            )

        def over_both(matrix):
            return lax.psum_scatter(
                over_rows(matrix), "blk", scatter_dimension=1, tiled=True
            ).astype(jnp.float32)

        output_patches = page_patches[:, :width]
        grad_w_up = over_both(tn(normed_three, d_upward))
        grad_w_down = over_both(tn(active, flat_cotangent))
        grad_out_cross = over_both(tn(flat_mixed_two, branch_two))
        grad_kv_cross = over_both(
            jnp.concatenate([tn(output_patches, d_key_two), tn(output_patches, d_value_two)], 1)
        )
        grad_q_cross = over_both(tn(normed_two, d_query_two))
        grad_out_self = over_both(tn(mixed_one, branch_one))
        d_packed_here = jnp.concatenate(d_packed_here, -1)
        columns = gathered([(d_packed_here[:, far], far) for far in range(count)], 2)
        columns = columns.transpose(0, 2, 1, 3).reshape(-1, 3 * own)
        grad_here = tn(normed_one.reshape(-1, width), columns)
        qkv_part = over_rows(grad_here)
        gain_rows = jnp.sum(grad_here * cut(qkv_here).astype(jnp.float32), axis=1)
        grad_gain_one = gain_rows / gain_one[0]
        gains = jnp.stack([grad_gain_one, grad_gain_two[0], grad_gain_three[0]])
        gains = lax.psum(gains, ("page", "blk"))
        qkv_rows = sent_to_all(qkv_part[None], 0)
        qkv_rows = qkv_rows.reshape(count, -1, 3, own).transpose(1, 2, 0, 3).reshape(-1, 3 * width)
        grad_qkv_self = lax.dynamic_slice_in_dim(
            qkv_rows, place * 3 * own, 3 * own, 1
        ).astype(jnp.float32)

    output = (resid_two + nn(active, w_down)).astype(jnp.bfloat16)

    return (
        output.reshape(pages, token_count, width),
        grad_tokens,
        grad_patches.astype(jnp.float32),
        gains[0],
        grad_qkv_self,
        grad_out_self,
        gains[1],
        grad_q_cross,
        grad_kv_cross,
        grad_out_cross,
        gains[2],
        grad_w_up,
        grad_w_down,
    )


def solution(mesh):
    whole = P()
    cut = P("page", "blk", None)
    matrix = P("page", "blk")
    placed = (cut, cut, matrix) + (whole,) * 10 + (cut,)
    return jax.shard_map(
        on_device,
        mesh=mesh,
        in_specs=placed,
        out_specs=(
            cut,
            cut,
            cut,
            whole,
            matrix,
            matrix,
            whole,
            matrix,
            matrix,
            matrix,
            whole,
            matrix,
            matrix,
        ),
        check_vma=False,
    )
```

time: 810 us -> 578 us (0.71); the launches traced: 799 us -> 576 us
  waiting for transfers between devices: 358 us -> 229 us
  Pallas kernels: 123 us -> 207 us
  matrix products: 112 us -> 29.7 us
  local copies, waits for them, and re-layouts: 83.7 us -> 38.6 us
  blocking collectives: 41 us -> 0 us
  other arithmetic: 34.2 us -> 25.7 us
    reduce_scatter x12 -> x2, waiting for transfers between devices: 146 us -> 0.01 us  [the longest x1 0.01 us: on_device(): lax.psum_scatter(both.reshape(-1, both.shape[-1]), ('blk', 'page'), scatt...]
    pallas_call x3 -> x19, Pallas kernels: 76 us -> 167 us  [the longest x16 105 us: row_call(): pl.pallas_call(kernel, grid_spec=pltpu.PrefetchScalarGridSpec(num_scalar_...]
    unnamed x14 -> x3, waiting for transfers between devices: 51.8 us -> 0.05 us
    ppermute x0 -> x12, waiting for transfers between devices: none -> 45.6 us  [swapped(): lax.ppermute(value, 'page', [(i, i ^ 1 << bit) for i in range(pages)])]
    psum x1 -> x0, blocking collectives: 41 us -> none  [on_device(): lax.psum((grad_gain_one, grad_gain_two, grad_gain_three), ('page', 'blk'))]
    dot_general x7 -> x0, matrix products: 40.3 us -> none  [tn(): lax.dot_general(left, right, (((0,), (0,)), ((), ())), preferred_element_...]
    dot_general x6 -> x2, matrix products: 37.8 us -> 11.7 us  [nt(): lax.dot_general(left, right, (((1,), (1,)), ((), ())), preferred_element_...]
    ppermute x26 -> x22, waiting for transfers between devices: 160 us -> 183 us  [shifted(): lax.ppermute(value, 'blk', [(i, (i + shift) % count) for i in range(count)])]
  transfers between devices with their start and end apart: 39 -> 37, of which waited for: 22 -> 15; matrix products, arithmetic and copies ran while one was open for 23% -> 10% of each run, Pallas kernels for 5% -> 27%
where the time goes in v2:
time: 578 us; the launch traced here: 576 us
  waiting for transfers between devices  229 us (40%)
  Pallas kernels  207 us (36%)
  local copies, waits for them, and re-layouts  38.6 us (7%)
  starting transfers between devices  31.1 us (5%)
  matrix products  29.7 us (5%)
  other arithmetic  25.7 us (4%)
  between operations  14.7 us (3%)
    ppermute x22, waiting for transfers between devices, shifted(): lax.ppermute(value, 'blk', [(i, (i + shift) % count) for i in range(count)])  183 us
    pallas_call x16, Pallas kernels, row_call(): pl.pallas_call(kernel, grid_spec=pltpu.PrefetchScalarGridSpec(num_scalar_...  105 us
    pallas_call x3, Pallas kernels, attend_back(): pl.pallas_call(functools.partial(backward_kernel, heads, causal, tq, tk,...  62.3 us
    ppermute x12, waiting for transfers between devices, swapped(): lax.ppermute(value, 'page', [(i, i ^ 1 << bit) for i in range(pages)])  45.6 us
    pallas_call x2, Pallas kernels, attend(): pl.pallas_call(functools.partial(forward_kernel, heads, causal, tq, tk),...  40.3 us
    unnamed x127, local copies, waits for them, and re-layouts  27.9 us
    ppermute x22, starting transfers between devices, shifted(): lax.ppermute(value, 'blk', [(i, (i + shift) % count) for i in range(count)])  24.1 us
    dot_general x2, matrix products, nn(): lax.dot_general(left, right, (((1,), (0,)), ((), ())), preferred_element_...  17.9 us
  transfers between devices with their start and end apart: 37, of which 15 were waited for; matrix products, arithmetic and copies ran while one was open for 10% of the time, Pallas kernels for 27%

profile of v2, /device:TPU:15, one launch (start us, length us, event | category | flops | bytes accessed | tf_op | source)
XLA Modules:
  0.0 575.8 jit_solution(16584520270290065196)
XLA Ops:
  8.8 22.8 %collective-permute-done.x_ref = bf16[1,512,1024]{2,1,0:T(8,128)(2,1)S(1)} collective-permute-done((bf16[1,512,1024]{2,1,0:T(8,128)(2,1)}, bf16[1,512,1024]{2,1,0:T(8,128)(2,1)S(1)}, u32[]{:S(2)}, u32[]{:S(2)}) %collective-permute-start) | collective-permute-done | bytes 1048608 | tf_op jit(solution)/shard_map/ppermute | solution.py:913
  33.0 23.9 %collective-permute-done.2.x_ref = bf16[1,512,1024]{2,1,0:T(8,128)(2,1)S(1)} collective-permute-done((bf16[1,512,1024]{2,1,0:T(8,128)(2,1)}, bf16[1,512,1024]{2,1,0:T(8,128)(2,1)S(1)}, u32[]{:S(2)}, u32[]{:S(2)}) %collective-permute-start.2) | collective-permute-done | bytes 1048608 | tf_op jit(solution)/shard_map/ppermute | solution.py:913
  66.5 12.1 %collective-permute-done.3 = bf16[1,256,1024]{2,1,0:T(8,128)(2,1)} collective-permute-done((bf16[1,256,1024]{2,1,0:T(8,128)(2,1)}, bf16[1,256,1024]{2,1,0:T(8,128)(2,1)}, u32[]{:S(2)}, u32[]{:S(2)}) %collective-permute-start.3) | collective-permute-done | bytes 524320 | tf_op jit(solution)/shard_map/ppermute | solution.py:913
  90.1 19.5 %attend.2 = (bf16[1,2048,256]{2,1,0:T(8,128)(2,1)S(1)}, bf16[1,2048,512]{2,1,0:T(8,128)(2,1)S(1)}) custom-call(bf16[1,3,2048,256]{3,2,1,0:T(8,128)(2,1)S(1)} %get-tuple-element.105.q_ref.k_ref.v_ref, bf16[1,3,2048,256]{3,2,1,0:T(8,128)(2,1)S(1)} %get-tuple-element.105.q_ref.k_ref.v_ref, bf16[1,3,2048,256]{3,2,1,0:T(8,128)(2,1)S(1)} %get-tuple-element.105.q_ref.k_ref.v_ref), custom_call_target="tpu_custom_call" | custom-call | flops 335544320 | bytes 262144 | tf_op jit(solution)/shard_map/attend/pallas_call | solution.py:312
  115.2 17.8 %collective-permute-done.4.refs_1_ = bf16[512,256]{1,0:T(8,128)(2,1)S(1)} collective-permute-done((bf16[512,256]{1,0:T(8,128)(2,1)S(1)}, bf16[512,256]{1,0:T(8,128)(2,1)S(1)}, u32[]{:S(2)}, u32[]{:S(2)}) %collective-permute-start.4) | collective-permute-done | bytes 262176 | tf_op jit(solution)/shard_map/ppermute | solution.py:913
  133.0 17.4 %collective-permute-done.5.refs_2_ = bf16[512,256]{1,0:T(8,128)(2,1)S(1)} collective-permute-done((bf16[512,256]{1,0:T(8,128)(2,1)S(1)}, bf16[512,256]{1,0:T(8,128)(2,1)S(1)}, u32[]{:S(2)}, u32[]{:S(2)}) %collective-permute-start.5) | collective-permute-done | bytes 262176 | tf_op jit(solution)/shard_map/ppermute | solution.py:913
  161.8 7.5 %convert_bitcast_fusion.k_ref.v_ref = bf16[1,1024,2048]{2,1,0:T(8,128)(2,1)S(1)} fusion(bf16[1024,2048]{1,0:T(8,128)(2,1)} %param.22, bf16[1024,1152]{1,0:T(8,128)(2,1)} %bitcast.108), kind=kOutput, calls=%fused_computation.1 | convolution fusion | flops 4297064448 | bytes 10485760 | tf_op jit(solution)/shard_map/dot_general | solution.py:25
  169.3 20.8 %attend.3 = (bf16[1,512,1024]{2,1,0:T(8,128)(2,1)S(1)}, bf16[1,512,2048]{2,1,0:T(8,128)(2,1)S(1)}) custom-call(bf16[1,512,1024]{2,1,0:T(8,128)(2,1)S(1)} %bitcast.122, bf16[1,1024,2048]{2,1,0:T(8,128)(2,1)S(1)} %convert_bitcast_fusion.k_ref.v_ref, bf16[1,1024,2048]{2,1,0:T(8,128)(2,1)S(1)} %convert_bitcast_fusion.k_ref.v_ref, ...), custom_call_target="tpu_custom_call" | custom-call | flops 335544320 | bytes 262144 | tf_op jit(solution)/shard_map/attend/pallas_call | solution.py:312
  191.5 17.9 %expand.1 = (f32[512,1024]{1,0:T(8,128)S(1)}, bf16[512,1024]{1,0:T(8,128)(2,1)S(1)}, bf16[512,4096]{1,0:T(8,128)(2,1)}, bf16[512,4096]{1,0:T(8,128)(2,1)}) custom-call(bf16[512,1024]{1,0:T(8,128)(2,1)S(1)} %bitcast.115, f32[512,1024]{1,0:T(8,128)} %get-tuple-element.110.resid_ref, f32[1,1024]{1,0:T(1,128)S(1)} %bitcast.131, bf16[1024,1024]{1,0:T(8,128)(2,1)} %out_ref.4, ...), custom_call_target="tpu_custom_call" | custom-call | flops 171798688 | bytes 461455 | tf_op jit(solution)/shard_map/expand/pallas_call | solution.py:412
  220.0 8.0 %grad_down.1 = bf16[4,8,1024,256]{3,2,1,0:T(8,128)(2,1)} custom-call(bf16[512,4096]{1,0:T(8,128)(2,1)S(1)} %copy-done.15, bf16[512,1024]{1,0:T(8,128)(2,1)S(1)} %bitcast.113, bf16[4,8,1024,256]{3,2,1,0:T(8,128)(2,1)} %grad_up.1.kept_ref), custom_call_target="tpu_custom_call", output_to_operand_aliasing={{}: (2, {})} | custom-call | flops 85899344 | bytes 440401 | tf_op jit(solution)/shard_map/grad_down/pallas_call | solution.py:412
  229.3 12.8 %contract.1 = (f32[512,1024]{1,0:T(8,128)S(1)}, bf16[512,1024]{1,0:T(8,128)(2,1)S(1)}, bf16[512,1024]{1,0:T(8,128)(2,1)S(1)}, f32[1,1024]{1,0:T(1,128)S(1)}) custom-call(bf16[512,4096]{1,0:T(8,128)(2,1)} %get-tuple-element.117.right_ref.d_upward_ref, bf16[1024,4096]{1,0:T(8,128)(2,1)} %up_ref.3, f32[512,1024]{1,0:T(8,128)} %copy-done.24, ...), custom_call_target="tpu_custom_call" | custom-call | flops 107374184 | bytes 356597 | tf_op jit(solution)/shard_map/contract/pallas_call | solution.py:412
  247.4 26.4 %attend_back.3 = (bf16[1,512,1024]{2,1,0:T(8,128)(2,1)S(1)}, bf16[1,1,2,1024,1024]{4,3,2,1,0:T(8,128)(2,1)S(1)}) custom-call(s32[1]{0:T(128)} %bitcast.place_ref, bf16[1,512,2048]{2,1,0:T(8,128)(2,1)S(1)} %copy-done.28, bf16[1,1024,2048]{2,1,0:T(8,128)(2,1)} %copy-done, bf16[1,1024,2048]{2,1,0:T(8,128)(2,1)} %copy-done, ...), custom_call_target="tpu_custom_call" | custom-call | flops 419430400 | bytes 262144 | tf_op jit(solution)/shard_map/attend_back/pallas_call | solution.py:365
  292.0 8.9 %grad.4 = (bf16[512,2048]{1,0:T(8,128)(2,1)S(1)}, bf16[512,2048]{1,0:T(8,128)(2,1)S(1)}) custom-call(s32[2]{0:T(128)S(1)} %pad_add_fusion.me_ref, bf16[1024,1152]{1,0:T(8,128)(2,1)} %bitcast.109, bf16[1,1,2,1024,1024]{4,3,2,1,0:T(8,128)(2,1)} %copy-done.16), custom_call_target="tpu_custom_call" | custom-call | flops 85899344 | bytes 131072 | tf_op jit(solution)/shard_map/grad/pallas_call | solution.py:412
  312.3 16.7 %collective-permute-done.8.rest_2_ = bf16[1,512,256]{2,1,0:T(8,128)(2,1)S(1)} collective-permute-done((bf16[1,512,256]{2,1,0:T(8,128)(2,1)S(1)}, bf16[1,512,256]{2,1,0:T(8,128)(2,1)S(1)}, u32[]{:S(2)}, u32[]{:S(2)}) %collective-permute-start.8) | collective-permute-done | bytes 262176 | tf_op jit(solution)/shard_map/ppermute | solution.py:913
  329.7 16.1 %collective-permute-done.9.rest_3_ = bf16[1,512,256]{2,1,0:T(8,128)(2,1)S(1)} collective-permute-done((bf16[1,512,256]{2,1,0:T(8,128)(2,1)S(1)}, bf16[1,512,256]{2,1,0:T(8,128)(2,1)S(1)}, u32[]{:S(2)}, u32[]{:S(2)}) %collective-permute-start.9) | collective-permute-done | bytes 262176 | tf_op jit(solution)/shard_map/ppermute | solution.py:913
  352.3 17.8 %attend_back.4 = bf16[1,4,3,512,128]{4,3,2,1,0:T(8,128)(2,1)S(1)} custom-call(s32[1]{0:T(128)} %bitcast.place_ref, bf16[1,2048,512]{2,1,0:T(8,128)(2,1)S(1)} %copy-done.14, bf16[1,3,2048,256]{3,2,1,0:T(8,128)(2,1)S(1)} %get-tuple-element.105.q_ref.k_ref.v_ref, bf16[1,3,2048,256]{3,2,1,0:T(8,128)(2,1)S(1)} %get-tuple-element.105.q_ref.k_ref.v_ref, ...), custom_call_target="tpu_custom_call" | custom-call | flops 209715200 | bytes 262144 | tf_op jit(solution)/shard_map/attend_back/pallas_call | solution.py:365
  372.7 18.2 %attend_back.5 = bf16[1,4,3,512,128]{4,3,2,1,0:T(8,128)(2,1)S(1)} custom-call(s32[1]{0:T(128)} %bitcast.place_ref, bf16[1,2048,512]{2,1,0:T(8,128)(2,1)S(1)} %copy-done.14, bf16[1,3,2048,256]{3,2,1,0:T(8,128)(2,1)S(1)} %get-tuple-element.105.q_ref.k_ref.v_ref, bf16[1,3,2048,256]{3,2,1,0:T(8,128)(2,1)S(1)} %get-tuple-element.105.q_ref.k_ref.v_ref, ...), custom_call_target="tpu_custom_call" | custom-call | flops 209715200 | bytes 262144 | tf_op jit(solution)/shard_map/attend_back/pallas_call | solution.py:365
  396.6 8.9 %grad_gain.1 = (bf16[512,768]{1,0:T(8,128)(2,1)S(1)}, bf16[512,768]{1,0:T(8,128)(2,1)S(1)}, f32[1024,128]{1,0:T(8,128)S(1)}) custom-call(s32[2]{0:T(128)S(1)} %pad_add_fusion.me_ref, bf16[2048,1024]{1,0:T(8,128)(2,1)} %bitcast.136, bf16[4,3,512,128]{3,2,1,0:T(8,128)(2,1)S(1)} %bitcast.110, bf16[4,3,512,128]{3,2,1,0:T(8,128)(2,1)S(1)} %bitcast.111, ...), custom_call_target="tpu_custom_call" | custom-call | flops 64424508 | bytes 178258 | tf_op jit(solution)/shard_map/grad_gain/pallas_call | solution.py:412
  414.8 7.2 %fusion = bf16[1,1024,1024]{2,1,0:T(8,128)(2,1)} fusion(f32[1024,1024]{1,0:T(8,128)} %fusion.2, bf16[1024,2048]{1,0:T(8,128)(2,1)} %param.22, bf16[1,1,2,1024,1024]{4,3,2,1,0:T(8,128)(2,1)} %copy-done.16), kind=kOutput, calls=%fused_computation.4 | convolution fusion | flops 2149580800 | bytes 10485760 | tf_op jit(solution)/shard_map/dot_general | solution.py:19
  433.8 40.0 %collective-permute-done.22 = f32[3,1024]{1,0:T(4,128)S(1)} collective-permute-done((f32[3,1024]{1,0:T(4,128)S(1)}, f32[3,1024]{1,0:T(4,128)S(1)}, u32[]{:S(2)}, u32[]{:S(2)}) %collective-permute-start.22) | collective-permute-done | bytes 12320 | tf_op jit(solution)/shard_map/ppermute | solution.py:889
  490.1 10.5 %fusion.14 = bf16[1,512,1024]{2,1,0:T(8,128)(2,1)} fusion(f32[512,1024]{1,0:T(8,128)S(1)} %copy-done.25, bf16[512,4096]{1,0:T(8,128)(2,1)} %get-tuple-element.112.left_ref, bf16[4096,1024]{1,0:T(8,128)(2,1)} %down_ref.1), kind=kOutput, calls=%fused_computation.20 | convolution fusion | flops 4296015872 | bytes 15728640 | tf_op jit(solution)/shard_map/dot_general | solution.py:25
  500.6 9.4 %leave.1 = f32[1,512,1024]{2,1,0:T(8,128)} custom-call(s32[1]{0:T(128)} %bitcast.place_ref, bf16[1,3,512,128]{3,2,1,0:T(8,128)(2,1)S(1)} %copy-done.30, bf16[1,3,512,128]{3,2,1,0:T(8,128)(2,1)} %collective-permute-done.12.refs_1_, bf16[1,3,512,128]{3,2,1,0:T(8,128)(2,1)} %collective-permute-done.13.refs_2_, ...), custom_call_target="tpu_custom_call" | custom-call | flops 64424508 | bytes 251740 | tf_op jit(solution)/shard_map/leave/pallas_call | solution.py:412
  514.8 29.2 %collective-permute-done.31 = bf16[128,1536]{1,0:T(8,128)(2,1)S(1)} collective-permute-done((bf16[128,1536]{1,0:T(8,128)(2,1)S(1)}, bf16[128,1536]{1,0:T(8,128)(2,1)S(1)}, u32[]{:S(2)}, u32[]{:S(2)}) %collective-permute-start.31) | collective-permute-done | bytes 393248 | tf_op jit(solution)/shard_map/ppermute | solution.py:913
  544.0 16.9 %collective-permute-done.32 = bf16[128,1536]{1,0:T(8,128)(2,1)S(1)} collective-permute-done((bf16[128,1536]{1,0:T(8,128)(2,1)S(1)}, bf16[128,1536]{1,0:T(8,128)(2,1)S(1)}, u32[]{:S(2)}, u32[]{:S(2)}) %collective-permute-start.32) | collective-permute-done | bytes 393248 | tf_op jit(solution)/shard_map/ppermute | solution.py:913
  (251 shorter events, 154.8 us)
Async XLA Ops:
  7.2 154.6 %all-gather.2.cloned.1.call-start = ((), (), s32[]{:S(2)}) async-start(), calls=%async_computation.2 | async-start | bytes 2949120 | tf_op jit(solution)/shard_map/all_gather | solution.py:1051
  8.6 48.3 %collective-permute-start.2 = (bf16[1,512,1024]{2,1,0:T(8,128)(2,1)}, bf16[1,512,1024]{2,1,0:T(8,128)(2,1)S(1)}, u32[]{:S(2)}, u32[]{:S(2)}) collective-permute-start(bf16[1,512,1024]{2,1,0:T(8,128)(2,1)} %refs_9_.1), channel_id=1, source_target_pairs={{0,3},{1,0},{2,1},{3,2},{4,7},{5,4},{6,5},{7,6},{8,11},{9,8},{10,9... | collective-permute-start | bytes 3145736 | tf_op jit(solution)/shard_map/ppermute | solution.py:913
  31.6 33.8 %collective-permute-start.1 = (bf16[1,256,1024]{2,1,0:T(8,128)(2,1)S(1)}, bf16[1,256,1024]{2,1,0:T(8,128)(2,1)}, u32[]{:S(2)}, u32[]{:S(2)}) collective-permute-start(bf16[1,256,1024]{2,1,0:T(8,128)(2,1)S(1)} %slice.304), channel_id=1, source_target_pairs={{0,1},{1,2},{2,3},{3,0},{4,5},{5,6},{6,7},{7,4},{8,9},{9,10},{10,1... | collective-permute-start | bytes 1572872 | tf_op jit(solution)/shard_map/ppermute | solution.py:913
  79.7 402.7 %reduce-scatter.3.cloned.1.call-start = ((), (), s32[]{:S(2)}) async-start(), calls=%async_computation.3 | async-start | bytes 17301504 | tf_op jit(solution)/shard_map/reduce_scatter | solution.py:1074
  112.0 38.4 %collective-permute-start.5 = (bf16[512,256]{1,0:T(8,128)(2,1)S(1)}, bf16[512,256]{1,0:T(8,128)(2,1)S(1)}, u32[]{:S(2)}, u32[]{:S(2)}) collective-permute-start(bf16[512,256]{1,0:T(8,128)(2,1)S(1)} %get-tuple-element.219), channel_id=1, source_target_pairs={{0,2},{1,3},{2,0},{3,1},{4,6},{5,7},{6,4},{7,5},{8,10},{9,11},{10,... | collective-permute-start | bytes 786440 | tf_op jit(solution)/shard_map/ppermute | solution.py:913
  115.2 37.4 %collective-permute-start.6 = (bf16[512,256]{1,0:T(8,128)(2,1)S(1)}, bf16[512,256]{1,0:T(8,128)(2,1)S(1)}, u32[]{:S(2)}, u32[]{:S(2)}) collective-permute-start(bf16[512,256]{1,0:T(8,128)(2,1)S(1)} %get-tuple-element.218), channel_id=1, source_target_pairs={{0,3},{1,0},{2,1},{3,2},{4,7},{5,4},{6,5},{7,6},{8,11},{9,8},{10,9... | collective-permute-start | bytes 786440 | tf_op jit(solution)/shard_map/ppermute | solution.py:913
  228.0 339.0 %reduce-scatter.5.cloned.1.call-start = ((), (), s32[]{:S(2)}) async-start(), calls=%async_computation.4 | async-start | bytes 2621440 | tf_op jit(solution)/shard_map/reduce_scatter | solution.py:1186
  301.6 27.4 %collective-permute-start.8 = (bf16[1,512,256]{2,1,0:T(8,128)(2,1)S(1)}, bf16[1,512,256]{2,1,0:T(8,128)(2,1)S(1)}, u32[]{:S(2)}, u32[]{:S(2)}) collective-permute-start(bf16[1,512,256]{2,1,0:T(8,128)(2,1)S(1)} %get-tuple-element.215), channel_id=1, source_target_pairs={{0,2},{1,3},{2,0},{3,1},{4,6},{5,7},{6,4},{7,5},{8,10},{9,11},{10,... | collective-permute-start | bytes 786440 | tf_op jit(solution)/shard_map/ppermute | solution.py:913
  305.3 40.5 %collective-permute-start.9 = (bf16[1,512,256]{2,1,0:T(8,128)(2,1)S(1)}, bf16[1,512,256]{2,1,0:T(8,128)(2,1)S(1)}, u32[]{:S(2)}, u32[]{:S(2)}) collective-permute-start(bf16[1,512,256]{2,1,0:T(8,128)(2,1)S(1)} %get-tuple-element.214), channel_id=1, source_target_pairs={{0,3},{1,0},{2,1},{3,2},{4,7},{5,4},{6,5},{7,6},{8,11},{9,8},{10,9... | collective-permute-start | bytes 786440 | tf_op jit(solution)/shard_map/ppermute | solution.py:913
  346.5 47.6 %collective-permute-start.16 = (bf16[256,3072]{1,0:T(8,128)(2,1)}, bf16[256,3072]{1,0:T(8,128)(2,1)}, u32[]{:S(2)}, u32[]{:S(2)}) collective-permute-start(bf16[256,3072]{1,0:T(8,128)(2,1)} %get-tuple-element.150), channel_id=1, source_target_pairs={{0,16},{4,20},{8,24},{12,28},{16,0},{20,4},{24,8},{28,12},{1,17},{... | collective-permute-start | bytes 4718600 | tf_op jit(solution)/shard_map/ppermute | solution.py:889
  346.5 47.6 %collective-permute-start.15 = (bf16[256,2048]{1,0:T(8,128)(2,1)}, bf16[256,2048]{1,0:T(8,128)(2,1)}, u32[]{:S(2)}, u32[]{:S(2)}) collective-permute-start(bf16[256,2048]{1,0:T(8,128)(2,1)} %bitcast.25), channel_id=1, source_target_pairs={{0,8},{4,12},{8,0},{12,4},{16,24},{20,28},{24,16},{28,20},{1,9},{5... | collective-permute-start | bytes 3145736 | tf_op jit(solution)/shard_map/ppermute | solution.py:889
  371.2 43.5 %collective-permute-start.12 = (bf16[1,3,512,128]{3,2,1,0:T(8,128)(2,1)}, bf16[1,3,512,128]{3,2,1,0:T(8,128)(2,1)}, u32[]{:S(2)}, u32[]{:S(2)}) collective-permute-start(bf16[1,3,512,128]{3,2,1,0:T(8,128)(2,1)} %get-tuple-element.144), channel_id=1, source_target_pairs={{0,1},{1,2},{2,3},{3,0},{4,5},{5,6},{6,7},{7,4},{8,9},{9,10},{10,1... | collective-permute-start | bytes 1179656 | tf_op jit(solution)/shard_map/ppermute | solution.py:913
  371.2 50.8 %collective-permute-start.13 = (bf16[1,3,512,128]{3,2,1,0:T(8,128)(2,1)}, bf16[1,3,512,128]{3,2,1,0:T(8,128)(2,1)}, u32[]{:S(2)}, u32[]{:S(2)}) collective-permute-start(bf16[1,3,512,128]{3,2,1,0:T(8,128)(2,1)} %get-tuple-element.145), channel_id=1, source_target_pairs={{0,2},{1,3},{2,0},{3,1},{4,6},{5,7},{6,4},{7,5},{8,10},{9,11},{10,... | collective-permute-start | bytes 1179656 | tf_op jit(solution)/shard_map/ppermute | solution.py:913
  371.2 52.6 %collective-permute-start.14 = (bf16[1,3,512,128]{3,2,1,0:T(8,128)(2,1)}, bf16[1,3,512,128]{3,2,1,0:T(8,128)(2,1)}, u32[]{:S(2)}, u32[]{:S(2)}) collective-permute-start(bf16[1,3,512,128]{3,2,1,0:T(8,128)(2,1)} %get-tuple-element.146), channel_id=1, source_target_pairs={{0,3},{1,0},{2,1},{3,2},{4,7},{5,4},{6,5},{7,6},{8,11},{9,8},{10,9... | collective-permute-start | bytes 1179656 | tf_op jit(solution)/shard_map/ppermute | solution.py:913
  396.6 28.5 %collective-permute-start.25 = (bf16[128,2048]{1,0:T(8,128)(2,1)}, bf16[128,2048]{1,0:T(8,128)(2,1)}, u32[]{:S(2)}, u32[]{:S(2)}) collective-permute-start(bf16[128,2048]{1,0:T(8,128)(2,1)} %get-tuple-element.195), channel_id=1, source_target_pairs={{0,16},{4,20},{8,24},{12,28},{16,0},{20,4},{24,8},{28,12},{1,17},{... | collective-permute-start | bytes 1572872 | tf_op jit(solution)/shard_map/ppermute | solution.py:889
  422.0 52.1 %collective-permute-start.26 = (bf16[128,3072]{1,0:T(8,128)(2,1)}, bf16[128,3072]{1,0:T(8,128)(2,1)S(1)}, u32[]{:S(2)}, u32[]{:S(2)}) collective-permute-start(bf16[128,3072]{1,0:T(8,128)(2,1)} %get-tuple-element.193), channel_id=1, source_target_pairs={{0,8},{4,12},{8,0},{12,4},{16,24},{20,28},{24,16},{28,20},{1,9},{5... | collective-permute-start | bytes 2359304 | tf_op jit(solution)/shard_map/ppermute | solution.py:889
  425.0 48.9 %collective-permute-start.23 = (bf16[256,768]{1,0:T(8,128)(2,1)S(1)}, bf16[256,768]{1,0:T(8,128)(2,1)S(1)}, u32[]{:S(2)}, u32[]{:S(2)}) collective-permute-start(bf16[256,768]{1,0:T(8,128)(2,1)S(1)} %bitcast.144), channel_id=1, source_target_pairs={{0,8},{4,12},{8,0},{12,4},{16,24},{20,28},{24,16},{28,20},{1,9},{5... | collective-permute-start | bytes 1179656 | tf_op jit(solution)/shard_map/ppermute | solution.py:889
  427.1 46.7 %collective-permute-start.22 = (f32[3,1024]{1,0:T(4,128)S(1)}, f32[3,1024]{1,0:T(4,128)S(1)}, u32[]{:S(2)}, u32[]{:S(2)}) collective-permute-start(f32[3,1024]{1,0:T(4,128)S(1)} %fusion.27), channel_id=1, source_target_pairs={{0,8},{4,12},{8,0},{12,4},{16,24},{20,28},{24,16},{28,20},{1,9},{5... | collective-permute-start | bytes 36872 | tf_op jit(solution)/shard_map/ppermute | solution.py:889
  429.6 56.1 %collective-permute-start.19 = (bf16[1,3,512,128]{3,2,1,0:T(8,128)(2,1)}, bf16[1,3,512,128]{3,2,1,0:T(8,128)(2,1)S(1)}, u32[]{:S(2)}, u32[]{:S(2)}) collective-permute-start(bf16[1,3,512,128]{3,2,1,0:T(8,128)(2,1)} %get-tuple-element.162), channel_id=1, source_target_pairs={{0,1},{1,2},{2,3},{3,0},{4,5},{5,6},{6,7},{7,4},{8,9},{9,10},{10,1... | collective-permute-start | bytes 1179656 | tf_op jit(solution)/shard_map/ppermute | solution.py:913
  430.8 55.7 %collective-permute-start.20 = (bf16[1,3,512,128]{3,2,1,0:T(8,128)(2,1)}, bf16[1,3,512,128]{3,2,1,0:T(8,128)(2,1)S(1)}, u32[]{:S(2)}, u32[]{:S(2)}) collective-permute-start(bf16[1,3,512,128]{3,2,1,0:T(8,128)(2,1)} %get-tuple-element.163), channel_id=1, source_target_pairs={{0,2},{1,3},{2,0},{3,1},{4,6},{5,7},{6,4},{7,5},{8,10},{9,11},{10,... | collective-permute-start | bytes 1179656 | tf_op jit(solution)/shard_map/ppermute | solution.py:913
  487.2 26.9 %collective-permute-start.28 = (f32[3,1024]{1,0:T(4,128)}, f32[3,1024]{1,0:T(4,128)S(1)}, u32[]{:S(2)}, u32[]{:S(2)}) collective-permute-start(f32[3,1024]{1,0:T(4,128)} %add.284), channel_id=1, source_target_pairs={{0,2},{1,3},{2,0},{3,1},{4,6},{5,7},{6,4},{7,5},{8,10},{9,11},{10,... | collective-permute-start | bytes 36872 | tf_op jit(solution)/shard_map/ppermute | solution.py:913
  510.0 34.0 %collective-permute-start.31 = (bf16[128,1536]{1,0:T(8,128)(2,1)S(1)}, bf16[128,1536]{1,0:T(8,128)(2,1)S(1)}, u32[]{:S(2)}, u32[]{:S(2)}) collective-permute-start(bf16[128,1536]{1,0:T(8,128)(2,1)S(1)} %copy-done.60), channel_id=1, source_target_pairs={{0,2},{1,3},{2,0},{3,1},{4,6},{5,7},{6,4},{7,5},{8,10},{9,11},{10,... | collective-permute-start | bytes 1179656 | tf_op jit(solution)/shard_map/ppermute | solution.py:913
  511.5 49.4 %collective-permute-start.32 = (bf16[128,1536]{1,0:T(8,128)(2,1)S(1)}, bf16[128,1536]{1,0:T(8,128)(2,1)S(1)}, u32[]{:S(2)}, u32[]{:S(2)}) collective-permute-start(bf16[128,1536]{1,0:T(8,128)(2,1)S(1)} %copy-done.59), channel_id=1, source_target_pairs={{0,1},{1,2},{2,3},{3,0},{4,5},{5,6},{6,7},{7,4},{8,9},{9,10},{10,1... | collective-permute-start | bytes 1179656 | tf_op jit(solution)/shard_map/ppermute | solution.py:913
  514.1 48.6 %collective-permute-start.33 = (bf16[128,1536]{1,0:T(8,128)(2,1)S(1)}, bf16[128,1536]{1,0:T(8,128)(2,1)S(1)}, u32[]{:S(2)}, u32[]{:S(2)}) collective-permute-start(bf16[128,1536]{1,0:T(8,128)(2,1)S(1)} %pad_maximum_fusion.4), channel_id=1, source_target_pairs={{0,3},{1,0},{2,1},{3,2},{4,7},{5,4},{6,5},{7,6},{8,11},{9,8},{10,9... | collective-permute-start | bytes 1179656 | tf_op jit(solution)/shard_map/ppermute | solution.py:913
  (76 other events, 981.6 us)
Sparse Core Ops, SparseCore 0:
  79.8 67.3 all-gather.1
  228.1 245.9 reduce-scatter.2
  484.7 69.0 reduce-scatter.4

commit v3 on v2

--- a/solution.py
+++ b/solution.py
@@ -162,9 +162,10 @@
     if heads == 1:
         blended.append(jnp.zeros_like(blended[0]))
     mixed_ref[...] = jnp.concatenate(blended, 0).T.astype(mixed_ref.dtype)
+    row = lax.broadcasted_iota(jnp.int32, (LANES, tq), 0)
+    turned = jnp.where(row >= HEAD_DIM, columns[0], columns[heads - 1]).T
+    high, middle, low = three_parts(turned)
     for h in range(heads):
-        turned = jnp.broadcast_to(columns[h], (LANES, tq)).T
-        high, middle, low = three_parts(turned)
         place = spare_lane(q.shape, h)
         qx = jnp.where(own_lanes(q.shape, h), q, jnp.zeros_like(q))
         qx = jnp.where(place == 0, jnp.ones_like(q), qx)
@@ -480,6 +481,36 @@
     return row_call(enter_kernel, "enter", (pages,), args, specs, out, flops, (), aliases, 1)
 
 
+def enter_cross_kernel(src_ref, x_ref, w_ref, *rest):
+    whole_ref, pair_ref = rest[-2:]
+    whole_ref[...] = x_ref[...]
+    pair_ref[...] = nn(x_ref[:, : w_ref.shape[0]], w_ref[...]).astype(jnp.bfloat16)
+
+
+def enter_cross(piece, source, count, weight, kept):
+    pages, rows, wide = piece.shape
+    width, both = weight.shape
+    out = [
+        (
+            (pages, rows * count, columns),
+            jnp.bfloat16,
+            pl.BlockSpec((None, rows, columns), lambda p, s: (p, s[0], 0)),
+        )
+        for columns in (wide, both)
+    ]
+    args = [source, piece, weight]
+    specs = [pl.BlockSpec((None, rows, wide), lambda p, s: (p, 0, 0)), fixed(width, both)]
+    aliases = {}
+    if kept is not None:
+        args += list(kept)
+        specs += [anywhere] * 2
+        aliases = {3: 0, 4: 1}
+    flops = 2 * pages * rows * width * both
+    return row_call(
+        enter_cross_kernel, "enter_cross", (pages,), args, specs, out, flops, (), aliases, 1
+    )
+
+
 def between_kernel(parts, tile, place_ref, *refs):
     mixed_refs, refs = refs[:parts], refs[parts:]
     tokens_ref, gain_ref, out_ref, q_ref, resid_ref, normed_ref, query_ref, whole_ref = refs
@@ -897,6 +928,18 @@
     return keep, swapped(send, bit)
 
 
+def halved_with(keep, send, gains, bit):
+    rows, columns = send.shape
+    high = gains.astype(jnp.bfloat16)
+    low = (gains - high.astype(jnp.float32)).astype(jnp.bfloat16)
+    below = jnp.stack([high, low]).reshape(-1, columns)
+    count = below.shape[0]
+    below = jnp.pad(below, [(0, -count % 16), (0, 0)])
+    keep, got = halved(keep, jnp.concatenate([send, below], 0), bit)
+    parts = got[rows : rows + count].astype(jnp.float32).reshape(2, *gains.shape)
+    return (keep, got[:rows]), high.astype(jnp.float32) + low.astype(jnp.float32) + parts[0] + parts[1]
+
+
 def parted(pair, side):
     keep, got = pair
     blocks = 2 if keep.shape[0] % 256 else keep.shape[0] // 128
@@ -913,7 +956,7 @@
     return lax.ppermute(value, "blk", [(i, (i + shift) % count) for i in range(count)])
 
 
-def ring_pieces(value):
+def ring_pieces(value, before_last=None):
     count = lax.axis_size("blk")
     pieces = [(value, 0)]
     right = left = value
@@ -923,7 +966,10 @@
     if count % 2 == 0:
         half = value.shape[1] // 2
         if count > 1:
-            top, low = shifted(right[:, :half], 1), shifted(left[:, half:], -1)
+            top, low = right[:, :half], left[:, half:]
+            if before_last is not None:
+                top, low, _ = lax.optimization_barrier((top, low, before_last))
+            top, low = shifted(top, 1), shifted(low, -1)
             pieces.append((jnp.concatenate([top, low], 1), count // 2))
     return pieces
 
@@ -1048,11 +1094,15 @@
     dead = jnp.where(patch_mask > 0, 0.0, masked_score).astype(jnp.bfloat16)
     dead = jnp.broadcast_to(dead[:, :, None], dead.shape + (LANES,))
     patches_wide, _ = together(jnp.concatenate([patches, dead], 2), pieces[-1][0])
-    patches_all = lax.all_gather(patches_wide, "blk", axis=1, tiled=True)
+    kept = None
+    for piece, far in ring_pieces(patches_wide, mixed_here if swift else None):
+        source = ((place + far) % count).astype(jnp.int32).reshape(1)
+        kept = enter_cross(piece, source, count, kv_cross, kept)
+    patches_all, kv_two = kept
     bias_at = width // LANES
     page_patches = patches_all.reshape(-1, width + LANES)
-    kv_two = nn(page_patches[:, :width], kv_cross).astype(jnp.bfloat16)
-    kv_two = kv_two.reshape(pages, -1, 2 * width)
+    if swift:
+        kv_two, *mixed_parts = together(kv_two, *mixed_parts)
 
     flat_tokens = tokens.reshape(rows, width)
     resid_one, normed_two, query_two, mixed_one = between(
@@ -1133,10 +1183,10 @@
             second = grad_into(
                 second, 3 * width, where, left, width, right, square(at, 3, rows), 4, 256, page_devices
             )
-        first, second = halved(*first, 0), halved(*second, 0)
-        barred = together(*d_mixed_parts, *parted(first, 1), *parted(second, 2))
+        output = (resid_two + nn(active, w_down)).astype(jnp.bfloat16)
+        barred = together(*d_mixed_parts, *first, *second, output)
         d_mixed_parts, barred = list(barred[:count]), barred[count:]
-        first, second = halved(*barred[:2], 1), halved(*barred[2:], 2)
+        first, second, output = halved(*barred[:2], 0), halved(*barred[2:4], 0), barred[4]
 
     d_packed_here, d_packed = [], []
     for block in range(blocks):
@@ -1167,15 +1217,15 @@
             )
             grad_gain_one = jnp.sum(gain_rows, axis=1) / gain_one[0]
             gains = jnp.stack([grad_gain_one, grad_gain_two[0], grad_gain_three[0]])
-            third = halved(keep, send, 0)
-            gains_got = swapped(gains, 0)
-            barred = together(*sent, *d_packed, third[1], gains_got)
-            sent, d_packed = list(barred[:count]), list(barred[count : 2 * count])
-            third, gains = (third[0], barred[-2]), gains + barred[-1]
+            third, gains = halved_with(keep, send, gains, 0)
+            barred = together(*sent, *d_packed)
+            sent, d_packed = list(barred[:count]), list(barred[count:])
         elif swift:
-            barred = together(*sent, grads, *d_mixed_parts)
+            barred = together(*sent, grads, *d_mixed_parts, first[1], second[1])
             sent, grads = list(barred[:count]), barred[count]
-            d_mixed_parts = list(barred[count + 1 :])
+            d_mixed_parts = list(barred[count + 1 : 2 * count + 1])
+            first, second = (first[0], barred[-2]), (second[0], barred[-1])
+            first, second = halved(*parted(first, 1), 1), halved(*parted(second, 2), 2)
         d_packed_here.append(grads)
         d_packed += ordered(received(sent), 3)
     d_key_two, d_value_two = (d_kv_two[:, 0, kind].reshape(-1, width) for kind in range(2))
@@ -1184,10 +1234,6 @@
     if swift:
         grad_patches, both = together(grad_patches, both)
     grad_patches = lax.psum_scatter(grad_patches, "blk", scatter_dimension=1, tiled=True)
-
-    grad_tokens = leave(
-        spot, d_packed, blocks, qkv_self, tokens, d_resid_one.reshape(tokens.shape), gain_one
-    )
 
     if swift:
         rows_up = both.shape[0] // 2
@@ -1201,9 +1247,13 @@
 
         for bit in (1, 2):
             keep, send = parted(third, 1)
-            gains, send = together(gains, send)
-            third = halved(keep, send, bit)
-            gains = gains + swapped(gains, bit)
+            if bit == 2:
+                barred = together(send, *d_packed)
+                send, d_packed = barred[0], list(barred[1:])
+            third, gains = halved_with(keep, send, gains, bit)
+        grad_tokens = leave(
+            spot, d_packed, blocks, qkv_self, tokens, d_resid_one.reshape(tokens.shape), gain_one
+        )
         qkv_part = added(*third)
 
         def piece(far):
@@ -1225,9 +1275,9 @@
             columns, piece(0)[2], (place - 3 * place) % 4 * 256, 1
         )
         pieces = together(
-            gains, *d_packed[count:], *(jnp.concatenate(piece(far), 1) for far in range(1, count))
+            gains, *(jnp.concatenate(piece(far), 1) for far in range(1, count))
         )
-        gains, pieces = pieces[0], pieces[1 + count :]
+        gains, pieces = pieces[0], pieces[1:]
         all_gains = gains
         for far in far_first(count):
             got = shifted(pieces[far - 1], far)
@@ -1252,6 +1302,10 @@
                 over_rows(matrix), "blk", scatter_dimension=1, tiled=True
             ).astype(jnp.float32)
 
+        grad_tokens = leave(
+            spot, d_packed, blocks, qkv_self, tokens, d_resid_one.reshape(tokens.shape), gain_one
+        )
+        output = (resid_two + nn(active, w_down)).astype(jnp.bfloat16)
         output_patches = page_patches[:, :width]
         grad_w_up = over_both(tn(normed_three, d_upward))
         grad_w_down = over_both(tn(active, flat_cotangent))
@@ -1275,8 +1329,6 @@
         grad_qkv_self = lax.dynamic_slice_in_dim(
             qkv_rows, place * 3 * own, 3 * own, 1
         ).astype(jnp.float32)
-
-    output = (resid_two + nn(active, w_down)).astype(jnp.bfloat16)
 
     return (
         output.reshape(pages, token_count, width),

time: 578 us -> 565 us (0.978)
  waiting for transfers between devices: 229 us -> 197 us
  Pallas kernels: 207 us -> 225 us
  matrix products: 29.7 us -> 16.2 us
  other arithmetic: 25.7 us -> 37.9 us
    pallas_call x16 -> x20, Pallas kernels: 105 us -> 125 us  [row_call(): pl.pallas_call(kernel, grid_spec=pltpu.PrefetchScalarGridSpec(num_scalar_...]
    ppermute x22 -> x26, waiting for transfers between devices: 183 us -> 165 us  [shifted(): lax.ppermute(value, 'blk', [(i, (i + shift) % count) for i in range(count)])]
    ppermute x12 -> x9, waiting for transfers between devices: 45.6 us -> 31.2 us  [swapped(): lax.ppermute(value, 'page', [(i, i ^ 1 << bit) for i in range(pages)])]
    dot_general x2 -> x1, matrix products: 17.9 us -> 8.32 us  [nn(): lax.dot_general(left, right, (((1,), (0,)), ((), ())), preferred_element_...]
    unnamed x127 -> x163, local copies, waits for them, and re-layouts: 27.9 us -> 21.8 us
    convert_element_type x8 -> x9, other arithmetic: 12.8 us -> 14.2 us  [added(): (left.astype(jnp.float32) + right.astype(jnp.float32)).astype(jnp.bfloat16)]
    ppermute x22 -> x26, starting transfers between devices: 24.1 us -> 24.3 us  [shifted(): lax.ppermute(value, 'blk', [(i, (i + shift) % count) for i in range(count)])]
  transfers between devices with their start and end apart: 37 -> 37, of which waited for: 15 -> 14; matrix products, arithmetic and copies ran while one was open for 10% -> 12% of each run, Pallas kernels for 27% -> 30%
where the time goes in v3:
time: 565 us; the launch traced here: 558 us
  Pallas kernels  225 us (40%)
  waiting for transfers between devices  197 us (35%)
  local copies, waits for them, and re-layouts  40.9 us (7%)
  other arithmetic  37.9 us (7%)
  starting transfers between devices  26.7 us (5%)
  matrix products  16.2 us (3%)
  between operations  15.5 us (3%)
    ppermute x26, waiting for transfers between devices, shifted(): lax.ppermute(value, 'blk', [(i, (i + shift) % count) for i in range(count)])  165 us
    pallas_call x20, Pallas kernels, row_call(): pl.pallas_call(kernel, grid_spec=pltpu.PrefetchScalarGridSpec(num_scalar_...  125 us
    pallas_call x3, Pallas kernels, attend_back(): pl.pallas_call(functools.partial(backward_kernel, heads, causal, tq, tk,...  64.5 us
    pallas_call x2, Pallas kernels, attend(): pl.pallas_call(functools.partial(forward_kernel, heads, causal, tq, tk),...  35.6 us
    ppermute x9, waiting for transfers between devices, swapped(): lax.ppermute(value, 'page', [(i, i ^ 1 << bit) for i in range(pages)])  31.2 us
    ppermute x26, starting transfers between devices, shifted(): lax.ppermute(value, 'blk', [(i, (i + shift) % count) for i in range(count)])  24.3 us
    unnamed x163, local copies, waits for them, and re-layouts  21.8 us
    convert_element_type x9, other arithmetic, added(): (left.astype(jnp.float32) + right.astype(jnp.float32)).astype(jnp.bfloat16)  14.2 us
  transfers between devices with their start and end apart: 37, of which 14 were waited for; matrix products, arithmetic and copies ran while one was open for 12% of the time, Pallas kernels for 30%

profile of v3, /device:TPU:15, one launch (start us, length us, event | category | flops | bytes accessed | tf_op | source)
XLA Modules:
  0.0 558.4 jit_solution(13253433273537188839)
XLA Ops:
  8.8 22.8 %collective-permute-done.x_ref = bf16[1,512,1024]{2,1,0:T(8,128)(2,1)S(1)} collective-permute-done((bf16[1,512,1024]{2,1,0:T(8,128)(2,1)}, bf16[1,512,1024]{2,1,0:T(8,128)(2,1)S(1)}, u32[]{:S(2)}, u32[]{:S(2)}) %collective-permute-start) | collective-permute-done | bytes 1048608 | tf_op jit(solution)/shard_map/ppermute | solution.py:956
  33.0 23.8 %collective-permute-done.2.x_ref = bf16[1,512,1024]{2,1,0:T(8,128)(2,1)S(1)} collective-permute-done((bf16[1,512,1024]{2,1,0:T(8,128)(2,1)}, bf16[1,512,1024]{2,1,0:T(8,128)(2,1)S(1)}, u32[]{:S(2)}, u32[]{:S(2)}) %collective-permute-start.2) | collective-permute-done | bytes 1048608 | tf_op jit(solution)/shard_map/ppermute | solution.py:956
  58.0 7.3 %collective-permute-done.1 = bf16[1,256,1024]{2,1,0:T(8,128)(2,1)S(1)} collective-permute-done((bf16[1,256,1024]{2,1,0:T(8,128)(2,1)S(1)}, bf16[1,256,1024]{2,1,0:T(8,128)(2,1)S(1)}, u32[]{:S(2)}, u32[]{:S(2)}) %collective-permute-start.1) | collective-permute-done | bytes 524320 | tf_op jit(solution)/shard_map/ppermute | solution.py:956
  65.3 13.1 %collective-permute-done.3 = bf16[1,256,1024]{2,1,0:T(8,128)(2,1)S(1)} collective-permute-done((bf16[1,256,1024]{2,1,0:T(8,128)(2,1)S(1)}, bf16[1,256,1024]{2,1,0:T(8,128)(2,1)S(1)}, u32[]{:S(2)}, u32[]{:S(2)}) %collective-permute-start.3) | collective-permute-done | bytes 524320 | tf_op jit(solution)/shard_map/ppermute | solution.py:956
  90.2 19.0 %attend.2 = (bf16[1,2048,256]{2,1,0:T(8,128)(2,1)S(1)}, bf16[1,2048,512]{2,1,0:T(8,128)(2,1)S(1)}) custom-call(bf16[1,3,2048,256]{3,2,1,0:T(8,128)(2,1)S(1)} %get-tuple-element.127.q_ref.k_ref.v_ref, bf16[1,3,2048,256]{3,2,1,0:T(8,128)(2,1)S(1)} %get-tuple-element.127.q_ref.k_ref.v_ref, bf16[1,3,2048,256]{3,2,1,0:T(8,128)(2,1)S(1)} %get-tuple-element.127.q_ref.k_ref.v_ref), custom_call_target="tpu_custom_call" | custom-call | flops 335544320 | bytes 262144 | tf_op jit(solution)/shard_map/attend/pallas_call | solution.py:313
  141.9 10.7 %collective-permute-done.9.refs_2_ = bf16[512,256]{1,0:T(8,128)(2,1)S(1)} collective-permute-done((bf16[512,256]{1,0:T(8,128)(2,1)S(1)}, bf16[512,256]{1,0:T(8,128)(2,1)S(1)}, u32[]{:S(2)}, u32[]{:S(2)}) %collective-permute-start.9) | collective-permute-done | bytes 262176 | tf_op jit(solution)/shard_map/ppermute | solution.py:956
  159.5 16.7 %attend.3 = (bf16[1,512,1024]{2,1,0:T(8,128)(2,1)S(1)}, bf16[1,512,2048]{2,1,0:T(8,128)(2,1)S(1)}) custom-call(bf16[1,512,1024]{2,1,0:T(8,128)(2,1)S(1)} %bitcast.129, bf16[1,1024,2048]{2,1,0:T(8,128)(2,1)S(1)} %copy-done, bf16[1,1024,2048]{2,1,0:T(8,128)(2,1)S(1)} %copy-done, bf16[1,1024,1152]{2,1,0:T(8,128)(2,1)S(1)} %get-tuple-element.144.rest_0_.rest_1_), custom_call_target="tpu_custom_call" | custom-call | flops 335544320 | bytes 262144 | tf_op jit(solution)/shard_map/attend/pallas_call | solution.py:313
  177.5 18.0 %expand.1 = (f32[512,1024]{1,0:T(8,128)S(1)}, bf16[512,1024]{1,0:T(8,128)(2,1)S(1)}, bf16[512,4096]{1,0:T(8,128)(2,1)}, bf16[512,4096]{1,0:T(8,128)(2,1)}) custom-call(bf16[512,1024]{1,0:T(8,128)(2,1)S(1)} %bitcast.121, f32[512,1024]{1,0:T(8,128)} %get-tuple-element.147.resid_ref, f32[1,1024]{1,0:T(1,128)S(1)} %bitcast.144, bf16[1024,1024]{1,0:T(8,128)(2,1)} %out_ref.4, ...), custom_call_target="tpu_custom_call" | custom-call | flops 171798688 | bytes 461455 | tf_op jit(solution)/shard_map/expand/pallas_call | solution.py:413
  206.0 8.0 %grad_down.1 = bf16[4,8,1024,256]{3,2,1,0:T(8,128)(2,1)} custom-call(bf16[512,4096]{1,0:T(8,128)(2,1)S(1)} %copy-done.20, bf16[512,1024]{1,0:T(8,128)(2,1)S(1)} %bitcast.119, bf16[4,8,1024,256]{3,2,1,0:T(8,128)(2,1)} %grad_up.1.kept_ref), custom_call_target="tpu_custom_call", output_to_operand_aliasing={{}: (2, {})} | custom-call | flops 85899344 | bytes 440401 | tf_op jit(solution)/shard_map/grad_down/pallas_call | solution.py:413
  215.4 13.0 %contract.1 = (f32[512,1024]{1,0:T(8,128)S(1)}, bf16[512,1024]{1,0:T(8,128)(2,1)S(1)}, bf16[512,1024]{1,0:T(8,128)(2,1)S(1)}, f32[1,1024]{1,0:T(1,128)S(1)}) custom-call(bf16[512,4096]{1,0:T(8,128)(2,1)} %get-tuple-element.151.right_ref.d_upward_ref, bf16[1024,4096]{1,0:T(8,128)(2,1)} %up_ref.3, f32[512,1024]{1,0:T(8,128)} %copy-done.32, ...), custom_call_target="tpu_custom_call" | custom-call | flops 107374184 | bytes 356597 | tf_op jit(solution)/shard_map/contract/pallas_call | solution.py:413
  229.8 26.6 %attend_back.3 = (bf16[1,512,1024]{2,1,0:T(8,128)(2,1)S(1)}, bf16[1,1,2,1024,1024]{4,3,2,1,0:T(8,128)(2,1)S(1)}) custom-call(s32[1]{0:T(128)} %bitcast.place_ref, bf16[1,512,2048]{2,1,0:T(8,128)(2,1)S(1)} %copy-done.35, bf16[1,1024,2048]{2,1,0:T(8,128)(2,1)} %get-tuple-element.143.k_ref.v_ref, bf16[1,1024,2048]{2,1,0:T(8,128)(2,1)} %get-tuple-element.143.k_ref.v_ref, ...), custom_call_target="tpu_custom_call" | custom-call | flops 419430400 | bytes 262144 | tf_op jit(solution)/shard_map/attend_back/pallas_call | solution.py:366
  269.9 8.3 %add_convert_fusion.5 = bf16[512,1024]{1,0:T(8,128)(2,1)} fusion(f32[512,1024]{1,0:T(8,128)S(1)} %copy-done.33, bf16[512,4096]{1,0:T(8,128)(2,1)S(1)} %copy-done.21, bf16[4096,1024]{1,0:T(8,128)(2,1)} %down_ref.1), kind=kOutput, calls=%fused_computation.14 | convolution fusion | flops 4296015872 | bytes 15728640 | tf_op jit(solution)/shard_map/dot_general | solution.py:25
  291.6 9.7 %grad.4 = (bf16[512,2048]{1,0:T(8,128)(2,1)S(1)}, bf16[512,2048]{1,0:T(8,128)(2,1)}) custom-call(s32[2]{0:T(128)S(1)} %pad_add_fusion.me_ref, bf16[1024,1152]{1,0:T(8,128)(2,1)} %bitcast.115, bf16[1,1,2,1024,1024]{4,3,2,1,0:T(8,128)(2,1)} %copy-done.22), custom_call_target="tpu_custom_call" | custom-call | flops 85899344 | bytes 131072 | tf_op jit(solution)/shard_map/grad/pallas_call | solution.py:413
  301.4 7.2 %collective-permute-done.13.rest_3_ = bf16[1,512,256]{2,1,0:T(8,128)(2,1)} collective-permute-done((bf16[1,512,256]{2,1,0:T(8,128)(2,1)}, bf16[1,512,256]{2,1,0:T(8,128)(2,1)}, u32[]{:S(2)}, u32[]{:S(2)}) %collective-permute-start.13) | collective-permute-done | bytes 262176 | tf_op jit(solution)/shard_map/ppermute | solution.py:956
  309.1 19.0 %attend_back.4 = bf16[1,4,3,512,128]{4,3,2,1,0:T(8,128)(2,1)S(1)} custom-call(s32[1]{0:T(128)} %bitcast.place_ref, bf16[1,2048,512]{2,1,0:T(8,128)(2,1)S(1)} %copy-done.18, bf16[1,3,2048,256]{3,2,1,0:T(8,128)(2,1)S(1)} %get-tuple-element.127.q_ref.k_ref.v_ref, bf16[1,3,2048,256]{3,2,1,0:T(8,128)(2,1)S(1)} %get-tuple-element.127.q_ref.k_ref.v_ref, ...), custom_call_target="tpu_custom_call" | custom-call | flops 209715200 | bytes 262144 | tf_op jit(solution)/shard_map/attend_back/pallas_call | solution.py:366
  340.0 18.8 %attend_back.5 = bf16[1,4,3,512,128]{4,3,2,1,0:T(8,128)(2,1)S(1)} custom-call(s32[1]{0:T(128)} %bitcast.place_ref, bf16[1,2048,512]{2,1,0:T(8,128)(2,1)S(1)} %copy-done.19, bf16[1,3,2048,256]{3,2,1,0:T(8,128)(2,1)S(1)} %get-tuple-element.127.q_ref.k_ref.v_ref, bf16[1,3,2048,256]{3,2,1,0:T(8,128)(2,1)S(1)} %get-tuple-element.127.q_ref.k_ref.v_ref, ...), custom_call_target="tpu_custom_call" | custom-call | flops 209715200 | bytes 262144 | tf_op jit(solution)/shard_map/attend_back/pallas_call | solution.py:366
  360.7 13.4 %collective-permute-done.21.refs_2_ = bf16[1,3,512,128]{3,2,1,0:T(8,128)(2,1)S(1)} collective-permute-done((bf16[1,3,512,128]{3,2,1,0:T(8,128)(2,1)}, bf16[1,3,512,128]{3,2,1,0:T(8,128)(2,1)S(1)}, u32[]{:S(2)}, u32[]{:S(2)}) %collective-permute-start.21) | collective-permute-done | bytes 393248 | tf_op jit(solution)/shard_map/ppermute | solution.py:956
  374.8 19.7 %collective-permute-done.22.refs_3_ = bf16[1,3,512,128]{3,2,1,0:T(8,128)(2,1)S(1)} collective-permute-done((bf16[1,3,512,128]{3,2,1,0:T(8,128)(2,1)}, bf16[1,3,512,128]{3,2,1,0:T(8,128)(2,1)S(1)}, u32[]{:S(2)}, u32[]{:S(2)}) %collective-permute-start.22) | collective-permute-done | bytes 393248 | tf_op jit(solution)/shard_map/ppermute | solution.py:956
  396.7 8.8 %grad_gain.1 = (bf16[512,768]{1,0:T(8,128)(2,1)S(1)}, bf16[512,768]{1,0:T(8,128)(2,1)S(1)}, f32[1024,128]{1,0:T(8,128)S(1)}) custom-call(s32[2]{0:T(128)S(1)} %pad_add_fusion.me_ref, bf16[2048,1024]{1,0:T(8,128)(2,1)} %bitcast.149, bf16[4,3,512,128]{3,2,1,0:T(8,128)(2,1)S(1)} %bitcast.116, bf16[4,3,512,128]{3,2,1,0:T(8,128)(2,1)S(1)} %bitcast.117, ...), custom_call_target="tpu_custom_call" | custom-call | flops 64424508 | bytes 178258 | tf_op jit(solution)/shard_map/grad_gain/pallas_call | solution.py:413
  431.0 21.8 %collective-permute-done.27 = bf16[128,2048]{1,0:T(8,128)(2,1)} collective-permute-done((bf16[128,2048]{1,0:T(8,128)(2,1)}, bf16[128,2048]{1,0:T(8,128)(2,1)}, u32[]{:S(2)}, u32[]{:S(2)}) %collective-permute-start.27) | collective-permute-done | bytes 524320 | tf_op jit(solution)/shard_map/ppermute | solution.py:920
  454.9 8.7 %collective-permute-done.19 = bf16[272,768]{1,0:T(8,128)(2,1)S(1)} collective-permute-done((bf16[272,768]{1,0:T(8,128)(2,1)S(1)}, bf16[272,768]{1,0:T(8,128)(2,1)S(1)}, u32[]{:S(2)}, u32[]{:S(2)}) %collective-permute-start.19) | collective-permute-done | bytes 417824 | tf_op jit(solution)/shard_map/ppermute | solution.py:920
  483.7 9.7 %leave.1 = f32[1,512,1024]{2,1,0:T(8,128)} custom-call(s32[1]{0:T(128)} %bitcast.place_ref, bf16[1,3,512,128]{3,2,1,0:T(8,128)(2,1)S(1)} %copy-done.37, bf16[1,3,512,128]{3,2,1,0:T(8,128)(2,1)S(1)} %copy-done.50, bf16[1,3,512,128]{3,2,1,0:T(8,128)(2,1)S(1)} %copy-done.52, bf16[1,3,512,128]{3,2,1,0:T(8,128)(2,1)S(1)} %copy-done.54, ...), custom_call_target="tpu_custom_call" | custom-call | flops 64424508 | bytes 251740 | tf_op jit(solution)/shard_map/leave/pallas_call | solution.py:413
  497.4 28.5 %collective-permute-done.32 = bf16[128,1536]{1,0:T(8,128)(2,1)S(1)} collective-permute-done((bf16[128,1536]{1,0:T(8,128)(2,1)S(1)}, bf16[128,1536]{1,0:T(8,128)(2,1)S(1)}, u32[]{:S(2)}, u32[]{:S(2)}) %collective-permute-start.32) | collective-permute-done | bytes 393248 | tf_op jit(solution)/shard_map/ppermute | solution.py:956
  525.9 16.6 %collective-permute-done.33 = bf16[128,1536]{1,0:T(8,128)(2,1)S(1)} collective-permute-done((bf16[128,1536]{1,0:T(8,128)(2,1)S(1)}, bf16[128,1536]{1,0:T(8,128)(2,1)S(1)}, u32[]{:S(2)}, u32[]{:S(2)}) %collective-permute-start.33) | collective-permute-done | bytes 393248 | tf_op jit(solution)/shard_map/ppermute | solution.py:956
  (322 shorter events, 173.7 us)
Async XLA Ops:
  7.2 456.7 %reduce-scatter.3.cloned.1.call-start = ((), (), s32[]{:S(2)}) async-start(), calls=%async_computation.2 | async-start | bytes 17301504 | tf_op jit(solution)/shard_map/reduce_scatter | solution.py:1124
  8.6 48.2 %collective-permute-start.2 = (bf16[1,512,1024]{2,1,0:T(8,128)(2,1)}, bf16[1,512,1024]{2,1,0:T(8,128)(2,1)S(1)}, u32[]{:S(2)}, u32[]{:S(2)}) collective-permute-start(bf16[1,512,1024]{2,1,0:T(8,128)(2,1)} %refs_9_.1), channel_id=1, source_target_pairs={{0,3},{1,0},{2,1},{3,2},{4,7},{5,4},{6,5},{7,6},{8,11},{9,8},{10,9... | collective-permute-start | bytes 3145736 | tf_op jit(solution)/shard_map/ppermute | solution.py:956
  31.6 33.7 %collective-permute-start.1 = (bf16[1,256,1024]{2,1,0:T(8,128)(2,1)S(1)}, bf16[1,256,1024]{2,1,0:T(8,128)(2,1)S(1)}, u32[]{:S(2)}, u32[]{:S(2)}) collective-permute-start(bf16[1,256,1024]{2,1,0:T(8,128)(2,1)S(1)} %slice.362), channel_id=1, source_target_pairs={{0,1},{1,2},{2,3},{3,0},{4,5},{5,6},{6,7},{7,4},{8,9},{9,10},{10,1... | collective-permute-start | bytes 1572872 | tf_op jit(solution)/shard_map/ppermute | solution.py:956
  78.5 33.0 %collective-permute-start.4 = (bf16[1,256,1152]{2,1,0:T(8,128)(2,1)}, bf16[1,256,1152]{2,1,0:T(8,128)(2,1)}, u32[]{:S(2)}, u32[]{:S(2)}) collective-permute-start(bf16[1,256,1152]{2,1,0:T(8,128)(2,1)} %pad_maximum_fusion.1.x_ref), channel_id=1, source_target_pairs={{0,1},{1,2},{2,3},{3,0},{4,5},{5,6},{6,7},{7,4},{8,9},{9,10},{10,1... | collective-permute-start | bytes 1769480 | tf_op jit(solution)/shard_map/ppermute | solution.py:956
  78.6 34.0 %collective-permute-start.5 = (bf16[1,256,1152]{2,1,0:T(8,128)(2,1)}, bf16[1,256,1152]{2,1,0:T(8,128)(2,1)}, u32[]{:S(2)}, u32[]{:S(2)}) collective-permute-start(bf16[1,256,1152]{2,1,0:T(8,128)(2,1)} %pad_maximum_fusion.1.x_ref), channel_id=1, source_target_pairs={{0,3},{1,0},{2,1},{3,2},{4,7},{5,4},{6,5},{7,6},{8,11},{9,8},{10,9... | collective-permute-start | bytes 1769480 | tf_op jit(solution)/shard_map/ppermute | solution.py:956
  118.5 34.1 %collective-permute-start.9 = (bf16[512,256]{1,0:T(8,128)(2,1)S(1)}, bf16[512,256]{1,0:T(8,128)(2,1)S(1)}, u32[]{:S(2)}, u32[]{:S(2)}) collective-permute-start(bf16[512,256]{1,0:T(8,128)(2,1)S(1)} %get-tuple-element.261), channel_id=1, source_target_pairs={{0,2},{1,3},{2,0},{3,1},{4,6},{5,7},{6,4},{7,5},{8,10},{9,11},{10,... | collective-permute-start | bytes 786440 | tf_op jit(solution)/shard_map/ppermute | solution.py:956
  122.1 30.6 %collective-permute-start.10 = (bf16[512,256]{1,0:T(8,128)(2,1)S(1)}, bf16[512,256]{1,0:T(8,128)(2,1)S(1)}, u32[]{:S(2)}, u32[]{:S(2)}) collective-permute-start(bf16[512,256]{1,0:T(8,128)(2,1)S(1)} %get-tuple-element.260), channel_id=1, source_target_pairs={{0,3},{1,0},{2,1},{3,2},{4,7},{5,4},{6,5},{7,6},{8,11},{9,8},{10,9... | collective-permute-start | bytes 786440 | tf_op jit(solution)/shard_map/ppermute | solution.py:956
  214.1 334.9 %reduce-scatter.5.cloned.1.call-start = ((), (), s32[]{:S(2)}) async-start(), calls=%async_computation.3 | async-start | bytes 2621440 | tf_op jit(solution)/shard_map/reduce_scatter | solution.py:1236
  266.2 35.1 %collective-permute-start.11 = (bf16[1,512,256]{2,1,0:T(8,128)(2,1)}, bf16[1,512,256]{2,1,0:T(8,128)(2,1)S(1)}, u32[]{:S(2)}, u32[]{:S(2)}) collective-permute-start(bf16[1,512,256]{2,1,0:T(8,128)(2,1)} %get-tuple-element.258), channel_id=1, source_target_pairs={{0,1},{1,2},{2,3},{3,0},{4,5},{5,6},{6,7},{7,4},{8,9},{9,10},{10,1... | collective-permute-start | bytes 786440 | tf_op jit(solution)/shard_map/ppermute | solution.py:956
  266.2 35.1 %collective-permute-start.12 = (bf16[1,512,256]{2,1,0:T(8,128)(2,1)}, bf16[1,512,256]{2,1,0:T(8,128)(2,1)S(1)}, u32[]{:S(2)}, u32[]{:S(2)}) collective-permute-start(bf16[1,512,256]{2,1,0:T(8,128)(2,1)} %get-tuple-element.257), channel_id=1, source_target_pairs={{0,2},{1,3},{2,0},{3,1},{4,6},{5,7},{6,4},{7,5},{8,10},{9,11},{10,... | collective-permute-start | bytes 786440 | tf_op jit(solution)/shard_map/ppermute | solution.py:956
  268.4 40.1 %collective-permute-start.13 = (bf16[1,512,256]{2,1,0:T(8,128)(2,1)}, bf16[1,512,256]{2,1,0:T(8,128)(2,1)}, u32[]{:S(2)}, u32[]{:S(2)}) collective-permute-start(bf16[1,512,256]{2,1,0:T(8,128)(2,1)} %get-tuple-element.256), channel_id=1, source_target_pairs={{0,3},{1,0},{2,1},{3,2},{4,7},{5,4},{6,5},{7,6},{8,11},{9,8},{10,9... | collective-permute-start | bytes 786440 | tf_op jit(solution)/shard_map/ppermute | solution.py:956
  332.3 64.4 %collective-permute-start.17 = (bf16[256,3072]{1,0:T(8,128)(2,1)}, bf16[256,3072]{1,0:T(8,128)(2,1)}, u32[]{:S(2)}, u32[]{:S(2)}) collective-permute-start(bf16[256,3072]{1,0:T(8,128)(2,1)} %get-tuple-element.230), channel_id=1, source_target_pairs={{0,16},{4,20},{8,24},{12,28},{16,0},{20,4},{24,8},{28,12},{1,17},{... | collective-permute-start | bytes 4718600 | tf_op jit(solution)/shard_map/ppermute | solution.py:920
  333.7 63.0 %collective-permute-start.16 = (bf16[256,2048]{1,0:T(8,128)(2,1)}, bf16[256,2048]{1,0:T(8,128)(2,1)}, u32[]{:S(2)}, u32[]{:S(2)}) collective-permute-start(bf16[256,2048]{1,0:T(8,128)(2,1)} %bitcast.28), channel_id=1, source_target_pairs={{0,8},{4,12},{8,0},{12,4},{16,24},{20,28},{24,16},{28,20},{1,9},{5... | collective-permute-start | bytes 3145736 | tf_op jit(solution)/shard_map/ppermute | solution.py:920
  333.7 26.2 %collective-permute-start.20 = (bf16[1,3,512,128]{3,2,1,0:T(8,128)(2,1)}, bf16[1,3,512,128]{3,2,1,0:T(8,128)(2,1)S(1)}, u32[]{:S(2)}, u32[]{:S(2)}) collective-permute-start(bf16[1,3,512,128]{3,2,1,0:T(8,128)(2,1)} %get-tuple-element.196), channel_id=1, source_target_pairs={{0,1},{1,2},{2,3},{3,0},{4,5},{5,6},{6,7},{7,4},{8,9},{9,10},{10,1... | collective-permute-start | bytes 1179656 | tf_op jit(solution)/shard_map/ppermute | solution.py:956
  333.7 40.3 %collective-permute-start.21 = (bf16[1,3,512,128]{3,2,1,0:T(8,128)(2,1)}, bf16[1,3,512,128]{3,2,1,0:T(8,128)(2,1)S(1)}, u32[]{:S(2)}, u32[]{:S(2)}) collective-permute-start(bf16[1,3,512,128]{3,2,1,0:T(8,128)(2,1)} %get-tuple-element.197), channel_id=1, source_target_pairs={{0,2},{1,3},{2,0},{3,1},{4,6},{5,7},{6,4},{7,5},{8,10},{9,11},{10,... | collective-permute-start | bytes 1179656 | tf_op jit(solution)/shard_map/ppermute | solution.py:956
  333.8 60.7 %collective-permute-start.22 = (bf16[1,3,512,128]{3,2,1,0:T(8,128)(2,1)}, bf16[1,3,512,128]{3,2,1,0:T(8,128)(2,1)S(1)}, u32[]{:S(2)}, u32[]{:S(2)}) collective-permute-start(bf16[1,3,512,128]{3,2,1,0:T(8,128)(2,1)} %get-tuple-element.198), channel_id=1, source_target_pairs={{0,3},{1,0},{2,1},{3,2},{4,7},{5,4},{6,5},{7,6},{8,11},{9,8},{10,9... | collective-permute-start | bytes 1179656 | tf_op jit(solution)/shard_map/ppermute | solution.py:956
  395.2 68.5 %collective-permute-start.23 = (bf16[1,3,512,128]{3,2,1,0:T(8,128)(2,1)}, bf16[1,3,512,128]{3,2,1,0:T(8,128)(2,1)}, u32[]{:S(2)}, u32[]{:S(2)}) collective-permute-start(bf16[1,3,512,128]{3,2,1,0:T(8,128)(2,1)} %get-tuple-element.204), channel_id=1, source_target_pairs={{0,1},{1,2},{2,3},{3,0},{4,5},{5,6},{6,7},{7,4},{8,9},{9,10},{10,1... | collective-permute-start | bytes 1179656 | tf_op jit(solution)/shard_map/ppermute | solution.py:956
  395.2 68.5 %collective-permute-start.24 = (bf16[1,3,512,128]{3,2,1,0:T(8,128)(2,1)}, bf16[1,3,512,128]{3,2,1,0:T(8,128)(2,1)}, u32[]{:S(2)}, u32[]{:S(2)}) collective-permute-start(bf16[1,3,512,128]{3,2,1,0:T(8,128)(2,1)} %get-tuple-element.205), channel_id=1, source_target_pairs={{0,2},{1,3},{2,0},{3,1},{4,6},{5,7},{6,4},{7,5},{8,10},{9,11},{10,... | collective-permute-start | bytes 1179656 | tf_op jit(solution)/shard_map/ppermute | solution.py:956
  395.2 68.5 %collective-permute-start.25 = (bf16[1,3,512,128]{3,2,1,0:T(8,128)(2,1)}, bf16[1,3,512,128]{3,2,1,0:T(8,128)(2,1)}, u32[]{:S(2)}, u32[]{:S(2)}) collective-permute-start(bf16[1,3,512,128]{3,2,1,0:T(8,128)(2,1)} %get-tuple-element.206), channel_id=1, source_target_pairs={{0,3},{1,0},{2,1},{3,2},{4,7},{5,4},{6,5},{7,6},{8,11},{9,8},{10,9... | collective-permute-start | bytes 1179656 | tf_op jit(solution)/shard_map/ppermute | solution.py:956
  417.3 48.8 %collective-permute-start.28 = (bf16[128,3072]{1,0:T(8,128)(2,1)}, bf16[128,3072]{1,0:T(8,128)(2,1)}, u32[]{:S(2)}, u32[]{:S(2)}) collective-permute-start(bf16[128,3072]{1,0:T(8,128)(2,1)} %get-tuple-element.235), channel_id=1, source_target_pairs={{0,8},{4,12},{8,0},{12,4},{16,24},{20,28},{24,16},{28,20},{1,9},{5... | collective-permute-start | bytes 2359304 | tf_op jit(solution)/shard_map/ppermute | solution.py:920
  427.7 25.1 %collective-permute-start.27 = (bf16[128,2048]{1,0:T(8,128)(2,1)}, bf16[128,2048]{1,0:T(8,128)(2,1)}, u32[]{:S(2)}, u32[]{:S(2)}) collective-permute-start(bf16[128,2048]{1,0:T(8,128)(2,1)} %get-tuple-element.237), channel_id=1, source_target_pairs={{0,16},{4,20},{8,24},{12,28},{16,0},{20,4},{24,8},{28,12},{1,17},{... | collective-permute-start | bytes 1572872 | tf_op jit(solution)/shard_map/ppermute | solution.py:920
  493.3 32.6 %collective-permute-start.32 = (bf16[128,1536]{1,0:T(8,128)(2,1)S(1)}, bf16[128,1536]{1,0:T(8,128)(2,1)S(1)}, u32[]{:S(2)}, u32[]{:S(2)}) collective-permute-start(bf16[128,1536]{1,0:T(8,128)(2,1)S(1)} %copy-done.72), channel_id=1, source_target_pairs={{0,2},{1,3},{2,0},{3,1},{4,6},{5,7},{6,4},{7,5},{8,10},{9,11},{10,... | collective-permute-start | bytes 1179656 | tf_op jit(solution)/shard_map/ppermute | solution.py:956
  494.6 48.0 %collective-permute-start.33 = (bf16[128,1536]{1,0:T(8,128)(2,1)S(1)}, bf16[128,1536]{1,0:T(8,128)(2,1)S(1)}, u32[]{:S(2)}, u32[]{:S(2)}) collective-permute-start(bf16[128,1536]{1,0:T(8,128)(2,1)S(1)} %copy-done.71), channel_id=1, source_target_pairs={{0,1},{1,2},{2,3},{3,0},{4,5},{5,6},{6,7},{7,4},{8,9},{9,10},{10,1... | collective-permute-start | bytes 1179656 | tf_op jit(solution)/shard_map/ppermute | solution.py:956
  496.1 48.7 %collective-permute-start.34 = (bf16[128,1536]{1,0:T(8,128)(2,1)S(1)}, bf16[128,1536]{1,0:T(8,128)(2,1)S(1)}, u32[]{:S(2)}, u32[]{:S(2)}) collective-permute-start(bf16[128,1536]{1,0:T(8,128)(2,1)S(1)} %copy-done.70), channel_id=1, source_target_pairs={{0,3},{1,0},{2,1},{3,2},{4,7},{5,4},{6,5},{7,6},{8,11},{9,8},{10,9... | collective-permute-start | bytes 1179656 | tf_op jit(solution)/shard_map/ppermute | solution.py:956
  (94 other events, 1161.7 us)
Sparse Core Ops, SparseCore 0:
  214.2 239.5 reduce-scatter.2
  466.2 69.1 reduce-scatter.4

commit v4 on v3

--- a/solution.py
+++ b/solution.py
@@ -98,32 +98,39 @@
     if heads == 2:
         small = jnp.logical_and(small, lengths[1] * reach[1] < safe_score * safe_score)
 
-    def scores_of(h, start, masked):
-        scores = nt(kx[h, pl.ds(start, tk), :], q_heads[h])
+    def scores_of(h, start, masked, skip):
+        scores = nt(kx[h, pl.ds(start, tk), :], q_heads[h][skip:])
         if masked:
             key_at = start + lax.broadcasted_iota(jnp.int32, scores.shape, 0)
-            query_at = step * tq + lax.broadcasted_iota(jnp.int32, scores.shape, 1)
+            query_at = step * tq + skip + lax.broadcasted_iota(jnp.int32, scores.shape, 1)
             scores = jnp.where(key_at <= query_at, scores, masked_score)
         return scores
 
-    def plain_tile(j, carry, masked):
+    def behind(whole, part, skip):
+        return jnp.concatenate([whole[:, :skip], part], 1) if skip else part
+
+    def plain_tile(j, carry, masked, skip=0):
         start = pl.multiple_of(j * tk, tk)
         out = []
         for h in range(heads):
-            raised = jnp.exp(scores_of(h, start, masked)).astype(jnp.bfloat16)
-            out.append(carry[h] + nn(vx[h, :, pl.ds(start, tk)], raised))
+            raised = jnp.exp(scores_of(h, start, masked, skip)).astype(jnp.bfloat16)
+            part = carry[h][:, skip:] + nn(vx[h, :, pl.ds(start, tk)], raised)
+            out.append(behind(carry[h], part, skip))
         return tuple(out)
 
-    def careful_tile(j, carry, masked):
+    def careful_tile(j, carry, masked, skip=0):
         start = pl.multiple_of(j * tk, tk)
         out = []
         for h in range(heads):
-            largest, total = carry[h]
-            scores = scores_of(h, start, masked)
+            largest, total = carry[h][0][:, skip:], carry[h][1][:, skip:]
+            scores = scores_of(h, start, masked, skip)
             new_largest = jnp.maximum(largest, jnp.max(scores, axis=0, keepdims=True))
             raised = jnp.exp(scores - new_largest).astype(jnp.bfloat16)
             part = nn(vx[h, :, pl.ds(start, tk)], raised)
-            out.append((new_largest, total * jnp.exp(largest - new_largest) + part))
+            total = total * jnp.exp(largest - new_largest) + part
+            out.append(
+                (behind(carry[h][0], new_largest, skip), behind(carry[h][1], total, skip))
+            )
         return tuple(out)
 
     def over_tiles(tile, carry):
@@ -131,7 +138,7 @@
             full = step * tq // tk
             carry = lax.fori_loop(0, full, lambda j, c: tile(j, c, False), carry)
             for extra in range(max(tq // tk, 1)):
-                carry = tile(full + extra, carry, True)
+                carry = tile(full + extra, carry, True, extra * tk)
             return carry
         for j in range(keys // tk):
             carry = tile(j, carry, False)
@@ -218,9 +225,7 @@
 
     dqt[...] = jnp.zeros_like(dqt)
 
-    def tile(i, j, masked, sums):
-        q_at = pl.multiple_of(i * tq, tq)
-        k_at = pl.multiple_of(j * tk, tk)
+    def tile_at(q_at, tq, k_at, tk, masked):
         out = []
         for h in range(heads):
             qx = qx_ref[pl.ds(q_at, tq), h * LANES : (h + 1) * LANES]
@@ -236,9 +241,24 @@
             dk = nn(d_scores, qx)
             rows = pl.ds(h * HEAD_DIM, HEAD_DIM)
             dqt[rows, pl.ds(q_at, tq)] += nn(kt[rows, pl.ds(k_at, tk)], d_scores)
-            if sums is not None:
-                dk, dv = sums[h][0] + dk, sums[h][1] + dv
             out.append((dk, dv))
+        return out
+
+    def tile(i, j, masked, sums):
+        q_at = pl.multiple_of(i * tq, tq)
+        k_at = pl.multiple_of(j * tk, tk)
+        if masked and tq == tk and tk % (4 * LANES) == 0:
+            half = tk // 2
+            upper = tile_at(q_at, tq, k_at, half, True)
+            lower = tile_at(
+                pl.multiple_of(q_at + half, half), half, pl.multiple_of(k_at + half, half), half, True
+            )
+            return tuple(
+                tuple(jnp.concatenate(pair, 0) for pair in zip(*both)) for both in zip(upper, lower)
+            )
+        out = tile_at(q_at, tq, k_at, tk, masked)
+        if sums is not None:
+            out = [(old[0] + new[0], old[1] + new[1]) for old, new in zip(sums, out)]
         return tuple(out)
 
     def finish(j, sums):
@@ -1082,7 +1102,7 @@
         source = ((place + far) % count).astype(jnp.int32).reshape(1)
         kept = enter(piece, source, count, gain_one, qkv_here, kept)
     normed_one, packed = kept
-    mixed_here, qx_one = attend(packed, packed, None, heads, blocks, 1024, 512)
+    mixed_here, qx_one = attend(packed, packed, None, heads, blocks, 2048, 512)
     mixed_pieces = [
         lax.dynamic_slice_in_dim(
             cut(mixed_here), (place + far) % count * token_count, token_count, 1

time: 565 us -> 559 us (0.989)
  Pallas kernels: 225 us -> 217 us
    pallas_call x2, Pallas kernels: 35.6 us -> 29.1 us  [attend(): pl.pallas_call(functools.partial(forward_kernel, heads, causal, tq, tk),...]
  transfers between devices with their start and end apart: 37 -> 37, of which waited for: 14 -> 14; matrix products, arithmetic and copies ran while one was open for 12% -> 13% of each run, Pallas kernels for 30% -> 29%
where the time goes in v4:
time: 559 us; the launch traced here: 553 us
  Pallas kernels  217 us (39%)
  waiting for transfers between devices  200 us (36%)
  local copies, waits for them, and re-layouts  40.9 us (7%)
  other arithmetic  37.9 us (7%)
  starting transfers between devices  25.7 us (5%)
  matrix products  16.2 us (3%)
  between operations  15.5 us (3%)
    ppermute x26, waiting for transfers between devices, shifted(): lax.ppermute(value, 'blk', [(i, (i + shift) % count) for i in range(count)])  166 us
    pallas_call x20, Pallas kernels, row_call(): pl.pallas_call(kernel, grid_spec=pltpu.PrefetchScalarGridSpec(num_scalar_...  124 us
    pallas_call x3, Pallas kernels, attend_back(): pl.pallas_call(functools.partial(backward_kernel, heads, causal, tq, tk,...  63.3 us
    ppermute x9, waiting for transfers between devices, swapped(): lax.ppermute(value, 'page', [(i, i ^ 1 << bit) for i in range(pages)])  33.9 us
    pallas_call x2, Pallas kernels, attend(): pl.pallas_call(functools.partial(forward_kernel, heads, causal, tq, tk),...  29.1 us
    ppermute x26, starting transfers between devices, shifted(): lax.ppermute(value, 'blk', [(i, (i + shift) % count) for i in range(count)])  24.1 us
    unnamed x163, local copies, waits for them, and re-layouts  21.8 us
    convert_element_type x9, other arithmetic, added(): (left.astype(jnp.float32) + right.astype(jnp.float32)).astype(jnp.bfloat16)  14.2 us
  transfers between devices with their start and end apart: 37, of which 14 were waited for; matrix products, arithmetic and copies ran while one was open for 13% of the time, Pallas kernels for 29%

profile of v4, /device:TPU:15, one launch (start us, length us, event | category | flops | bytes accessed | tf_op | source)
XLA Modules:
  0.0 552.7 jit_solution(14202623315574478282)
XLA Ops:
  8.8 22.8 %collective-permute-done.x_ref = bf16[1,512,1024]{2,1,0:T(8,128)(2,1)S(1)} collective-permute-done((bf16[1,512,1024]{2,1,0:T(8,128)(2,1)}, bf16[1,512,1024]{2,1,0:T(8,128)(2,1)S(1)}, u32[]{:S(2)}, u32[]{:S(2)}) %collective-permute-start) | collective-permute-done | bytes 1048608 | tf_op jit(solution)/shard_map/ppermute | solution.py:976
  33.0 23.8 %collective-permute-done.2.x_ref = bf16[1,512,1024]{2,1,0:T(8,128)(2,1)S(1)} collective-permute-done((bf16[1,512,1024]{2,1,0:T(8,128)(2,1)}, bf16[1,512,1024]{2,1,0:T(8,128)(2,1)S(1)}, u32[]{:S(2)}, u32[]{:S(2)}) %collective-permute-start.2) | collective-permute-done | bytes 1048608 | tf_op jit(solution)/shard_map/ppermute | solution.py:976
  58.0 7.3 %collective-permute-done.1 = bf16[1,256,1024]{2,1,0:T(8,128)(2,1)S(1)} collective-permute-done((bf16[1,256,1024]{2,1,0:T(8,128)(2,1)S(1)}, bf16[1,256,1024]{2,1,0:T(8,128)(2,1)S(1)}, u32[]{:S(2)}, u32[]{:S(2)}) %collective-permute-start.1) | collective-permute-done | bytes 524320 | tf_op jit(solution)/shard_map/ppermute | solution.py:976
  65.3 13.1 %collective-permute-done.3 = bf16[1,256,1024]{2,1,0:T(8,128)(2,1)S(1)} collective-permute-done((bf16[1,256,1024]{2,1,0:T(8,128)(2,1)S(1)}, bf16[1,256,1024]{2,1,0:T(8,128)(2,1)S(1)}, u32[]{:S(2)}, u32[]{:S(2)}) %collective-permute-start.3) | collective-permute-done | bytes 524320 | tf_op jit(solution)/shard_map/ppermute | solution.py:976
  90.2 13.4 %attend.2 = (bf16[1,2048,256]{2,1,0:T(8,128)(2,1)S(1)}, bf16[1,2048,512]{2,1,0:T(8,128)(2,1)S(1)}) custom-call(bf16[1,3,2048,256]{3,2,1,0:T(8,128)(2,1)S(1)} %get-tuple-element.127.q_ref.k_ref.v_ref, bf16[1,3,2048,256]{3,2,1,0:T(8,128)(2,1)S(1)} %get-tuple-element.127.q_ref.k_ref.v_ref, bf16[1,3,2048,256]{3,2,1,0:T(8,128)(2,1)S(1)} %get-tuple-element.127.q_ref.k_ref.v_ref), custom_call_target="tpu_custom_call" | custom-call | flops 335544320 | bytes 262144 | tf_op jit(solution)/shard_map/attend/pallas_call | solution.py:333
  136.1 10.9 %collective-permute-done.9.refs_2_ = bf16[512,256]{1,0:T(8,128)(2,1)S(1)} collective-permute-done((bf16[512,256]{1,0:T(8,128)(2,1)S(1)}, bf16[512,256]{1,0:T(8,128)(2,1)S(1)}, u32[]{:S(2)}, u32[]{:S(2)}) %collective-permute-start.9) | collective-permute-done | bytes 262176 | tf_op jit(solution)/shard_map/ppermute | solution.py:976
  153.9 15.7 %attend.3 = (bf16[1,512,1024]{2,1,0:T(8,128)(2,1)S(1)}, bf16[1,512,2048]{2,1,0:T(8,128)(2,1)S(1)}) custom-call(bf16[1,512,1024]{2,1,0:T(8,128)(2,1)S(1)} %bitcast.129, bf16[1,1024,2048]{2,1,0:T(8,128)(2,1)S(1)} %copy-done, bf16[1,1024,2048]{2,1,0:T(8,128)(2,1)S(1)} %copy-done, bf16[1,1024,1152]{2,1,0:T(8,128)(2,1)S(1)} %get-tuple-element.144.rest_0_.rest_1_), custom_call_target="tpu_custom_call" | custom-call | flops 335544320 | bytes 262144 | tf_op jit(solution)/shard_map/attend/pallas_call | solution.py:333
  171.0 18.0 %expand.1 = (f32[512,1024]{1,0:T(8,128)S(1)}, bf16[512,1024]{1,0:T(8,128)(2,1)S(1)}, bf16[512,4096]{1,0:T(8,128)(2,1)}, bf16[512,4096]{1,0:T(8,128)(2,1)}) custom-call(bf16[512,1024]{1,0:T(8,128)(2,1)S(1)} %bitcast.121, f32[512,1024]{1,0:T(8,128)} %get-tuple-element.147.resid_ref, f32[1,1024]{1,0:T(1,128)S(1)} %bitcast.144, bf16[1024,1024]{1,0:T(8,128)(2,1)} %out_ref.4, ...), custom_call_target="tpu_custom_call" | custom-call | flops 171798688 | bytes 461455 | tf_op jit(solution)/shard_map/expand/pallas_call | solution.py:433
  199.5 8.0 %grad_down.1 = bf16[4,8,1024,256]{3,2,1,0:T(8,128)(2,1)} custom-call(bf16[512,4096]{1,0:T(8,128)(2,1)S(1)} %copy-done.20, bf16[512,1024]{1,0:T(8,128)(2,1)S(1)} %bitcast.119, bf16[4,8,1024,256]{3,2,1,0:T(8,128)(2,1)} %grad_up.1.kept_ref), custom_call_target="tpu_custom_call", output_to_operand_aliasing={{}: (2, {})} | custom-call | flops 85899344 | bytes 440401 | tf_op jit(solution)/shard_map/grad_down/pallas_call | solution.py:433
  208.9 12.9 %contract.1 = (f32[512,1024]{1,0:T(8,128)S(1)}, bf16[512,1024]{1,0:T(8,128)(2,1)S(1)}, bf16[512,1024]{1,0:T(8,128)(2,1)S(1)}, f32[1,1024]{1,0:T(1,128)S(1)}) custom-call(bf16[512,4096]{1,0:T(8,128)(2,1)} %get-tuple-element.151.right_ref.d_upward_ref, bf16[1024,4096]{1,0:T(8,128)(2,1)} %up_ref.3, f32[512,1024]{1,0:T(8,128)} %copy-done.32, ...), custom_call_target="tpu_custom_call" | custom-call | flops 107374184 | bytes 356597 | tf_op jit(solution)/shard_map/contract/pallas_call | solution.py:433
  223.1 26.6 %attend_back.3 = (bf16[1,512,1024]{2,1,0:T(8,128)(2,1)S(1)}, bf16[1,1,2,1024,1024]{4,3,2,1,0:T(8,128)(2,1)S(1)}) custom-call(s32[1]{0:T(128)} %bitcast.place_ref, bf16[1,512,2048]{2,1,0:T(8,128)(2,1)S(1)} %copy-done.35, bf16[1,1024,2048]{2,1,0:T(8,128)(2,1)} %get-tuple-element.143.k_ref.v_ref, bf16[1,1024,2048]{2,1,0:T(8,128)(2,1)} %get-tuple-element.143.k_ref.v_ref, ...), custom_call_target="tpu_custom_call" | custom-call | flops 419430400 | bytes 262144 | tf_op jit(solution)/shard_map/attend_back/pallas_call | solution.py:386
  264.3 8.3 %add_convert_fusion.5 = bf16[512,1024]{1,0:T(8,128)(2,1)} fusion(f32[512,1024]{1,0:T(8,128)S(1)} %copy-done.33, bf16[512,4096]{1,0:T(8,128)(2,1)S(1)} %copy-done.21, bf16[4096,1024]{1,0:T(8,128)(2,1)} %down_ref.1), kind=kOutput, calls=%fused_computation.14 | convolution fusion | flops 4296015872 | bytes 15728640 | tf_op jit(solution)/shard_map/dot_general | solution.py:25
  286.0 9.7 %grad.4 = (bf16[512,2048]{1,0:T(8,128)(2,1)S(1)}, bf16[512,2048]{1,0:T(8,128)(2,1)}) custom-call(s32[2]{0:T(128)S(1)} %pad_add_fusion.me_ref, bf16[1024,1152]{1,0:T(8,128)(2,1)} %bitcast.115, bf16[1,1,2,1024,1024]{4,3,2,1,0:T(8,128)(2,1)} %copy-done.22), custom_call_target="tpu_custom_call" | custom-call | flops 85899344 | bytes 131072 | tf_op jit(solution)/shard_map/grad/pallas_call | solution.py:433
  295.7 7.2 %collective-permute-done.13.rest_3_ = bf16[1,512,256]{2,1,0:T(8,128)(2,1)} collective-permute-done((bf16[1,512,256]{2,1,0:T(8,128)(2,1)}, bf16[1,512,256]{2,1,0:T(8,128)(2,1)}, u32[]{:S(2)}, u32[]{:S(2)}) %collective-permute-start.13) | collective-permute-done | bytes 262176 | tf_op jit(solution)/shard_map/ppermute | solution.py:976
  303.4 18.5 %attend_back.4 = bf16[1,4,3,512,128]{4,3,2,1,0:T(8,128)(2,1)S(1)} custom-call(s32[1]{0:T(128)} %bitcast.place_ref, bf16[1,2048,512]{2,1,0:T(8,128)(2,1)S(1)} %copy-done.18, bf16[1,3,2048,256]{3,2,1,0:T(8,128)(2,1)S(1)} %get-tuple-element.127.q_ref.k_ref.v_ref, bf16[1,3,2048,256]{3,2,1,0:T(8,128)(2,1)S(1)} %get-tuple-element.127.q_ref.k_ref.v_ref, ...), custom_call_target="tpu_custom_call" | custom-call | flops 209715200 | bytes 262144 | tf_op jit(solution)/shard_map/attend_back/pallas_call | solution.py:386
  333.8 18.2 %attend_back.5 = bf16[1,4,3,512,128]{4,3,2,1,0:T(8,128)(2,1)S(1)} custom-call(s32[1]{0:T(128)} %bitcast.place_ref, bf16[1,2048,512]{2,1,0:T(8,128)(2,1)S(1)} %copy-done.19, bf16[1,3,2048,256]{3,2,1,0:T(8,128)(2,1)S(1)} %get-tuple-element.127.q_ref.k_ref.v_ref, bf16[1,3,2048,256]{3,2,1,0:T(8,128)(2,1)S(1)} %get-tuple-element.127.q_ref.k_ref.v_ref, ...), custom_call_target="tpu_custom_call" | custom-call | flops 209715200 | bytes 262144 | tf_op jit(solution)/shard_map/attend_back/pallas_call | solution.py:386
  353.9 13.6 %collective-permute-done.21.refs_2_ = bf16[1,3,512,128]{3,2,1,0:T(8,128)(2,1)S(1)} collective-permute-done((bf16[1,3,512,128]{3,2,1,0:T(8,128)(2,1)}, bf16[1,3,512,128]{3,2,1,0:T(8,128)(2,1)S(1)}, u32[]{:S(2)}, u32[]{:S(2)}) %collective-permute-start.21) | collective-permute-done | bytes 393248 | tf_op jit(solution)/shard_map/ppermute | solution.py:976
  368.2 20.7 %collective-permute-done.22.refs_3_ = bf16[1,3,512,128]{3,2,1,0:T(8,128)(2,1)S(1)} collective-permute-done((bf16[1,3,512,128]{3,2,1,0:T(8,128)(2,1)}, bf16[1,3,512,128]{3,2,1,0:T(8,128)(2,1)S(1)}, u32[]{:S(2)}, u32[]{:S(2)}) %collective-permute-start.22) | collective-permute-done | bytes 393248 | tf_op jit(solution)/shard_map/ppermute | solution.py:976
  391.2 8.8 %grad_gain.1 = (bf16[512,768]{1,0:T(8,128)(2,1)S(1)}, bf16[512,768]{1,0:T(8,128)(2,1)S(1)}, f32[1024,128]{1,0:T(8,128)S(1)}) custom-call(s32[2]{0:T(128)S(1)} %pad_add_fusion.me_ref, bf16[2048,1024]{1,0:T(8,128)(2,1)} %bitcast.149, bf16[4,3,512,128]{3,2,1,0:T(8,128)(2,1)S(1)} %bitcast.116, bf16[4,3,512,128]{3,2,1,0:T(8,128)(2,1)S(1)} %bitcast.117, ...), custom_call_target="tpu_custom_call" | custom-call | flops 64424508 | bytes 178258 | tf_op jit(solution)/shard_map/grad_gain/pallas_call | solution.py:433
  424.7 17.5 %collective-permute-done.27 = bf16[128,2048]{1,0:T(8,128)(2,1)} collective-permute-done((bf16[128,2048]{1,0:T(8,128)(2,1)}, bf16[128,2048]{1,0:T(8,128)(2,1)}, u32[]{:S(2)}, u32[]{:S(2)}) %collective-permute-start.27) | collective-permute-done | bytes 524320 | tf_op jit(solution)/shard_map/ppermute | solution.py:940
  444.3 14.6 %collective-permute-done.19 = bf16[272,768]{1,0:T(8,128)(2,1)S(1)} collective-permute-done((bf16[272,768]{1,0:T(8,128)(2,1)S(1)}, bf16[272,768]{1,0:T(8,128)(2,1)S(1)}, u32[]{:S(2)}, u32[]{:S(2)}) %collective-permute-start.19) | collective-permute-done | bytes 417824 | tf_op jit(solution)/shard_map/ppermute | solution.py:940
  478.0 9.7 %leave.1 = f32[1,512,1024]{2,1,0:T(8,128)} custom-call(s32[1]{0:T(128)} %bitcast.place_ref, bf16[1,3,512,128]{3,2,1,0:T(8,128)(2,1)S(1)} %copy-done.37, bf16[1,3,512,128]{3,2,1,0:T(8,128)(2,1)S(1)} %copy-done.50, bf16[1,3,512,128]{3,2,1,0:T(8,128)(2,1)S(1)} %copy-done.52, bf16[1,3,512,128]{3,2,1,0:T(8,128)(2,1)S(1)} %copy-done.54, ...), custom_call_target="tpu_custom_call" | custom-call | flops 64424508 | bytes 251740 | tf_op jit(solution)/shard_map/leave/pallas_call | solution.py:433
  492.7 28.0 %collective-permute-done.32 = bf16[128,1536]{1,0:T(8,128)(2,1)S(1)} collective-permute-done((bf16[128,1536]{1,0:T(8,128)(2,1)S(1)}, bf16[128,1536]{1,0:T(8,128)(2,1)S(1)}, u32[]{:S(2)}, u32[]{:S(2)}) %collective-permute-start.32) | collective-permute-done | bytes 393248 | tf_op jit(solution)/shard_map/ppermute | solution.py:976
  520.7 16.5 %collective-permute-done.33 = bf16[128,1536]{1,0:T(8,128)(2,1)S(1)} collective-permute-done((bf16[128,1536]{1,0:T(8,128)(2,1)S(1)}, bf16[128,1536]{1,0:T(8,128)(2,1)S(1)}, u32[]{:S(2)}, u32[]{:S(2)}) %collective-permute-start.33) | collective-permute-done | bytes 393248 | tf_op jit(solution)/shard_map/ppermute | solution.py:976
  (322 shorter events, 173.5 us)
Async XLA Ops:
  7.2 452.0 %reduce-scatter.3.cloned.1.call-start = ((), (), s32[]{:S(2)}) async-start(), calls=%async_computation.2 | async-start | bytes 17301504 | tf_op jit(solution)/shard_map/reduce_scatter | solution.py:1144
  7.2 24.3 %collective-permute-start = (bf16[1,512,1024]{2,1,0:T(8,128)(2,1)}, bf16[1,512,1024]{2,1,0:T(8,128)(2,1)S(1)}, u32[]{:S(2)}, u32[]{:S(2)}) collective-permute-start(bf16[1,512,1024]{2,1,0:T(8,128)(2,1)} %refs_9_.1), channel_id=1, source_target_pairs={{0,1},{1,2},{2,3},{3,0},{4,5},{5,6},{6,7},{7,4},{8,9},{9,10},{10,1... | collective-permute-start | bytes 3145736 | tf_op jit(solution)/shard_map/ppermute | solution.py:976
  8.6 48.2 %collective-permute-start.2 = (bf16[1,512,1024]{2,1,0:T(8,128)(2,1)}, bf16[1,512,1024]{2,1,0:T(8,128)(2,1)S(1)}, u32[]{:S(2)}, u32[]{:S(2)}) collective-permute-start(bf16[1,512,1024]{2,1,0:T(8,128)(2,1)} %refs_9_.1), channel_id=1, source_target_pairs={{0,3},{1,0},{2,1},{3,2},{4,7},{5,4},{6,5},{7,6},{8,11},{9,8},{10,9... | collective-permute-start | bytes 3145736 | tf_op jit(solution)/shard_map/ppermute | solution.py:976
  31.6 33.7 %collective-permute-start.1 = (bf16[1,256,1024]{2,1,0:T(8,128)(2,1)S(1)}, bf16[1,256,1024]{2,1,0:T(8,128)(2,1)S(1)}, u32[]{:S(2)}, u32[]{:S(2)}) collective-permute-start(bf16[1,256,1024]{2,1,0:T(8,128)(2,1)S(1)} %slice.362), channel_id=1, source_target_pairs={{0,1},{1,2},{2,3},{3,0},{4,5},{5,6},{6,7},{7,4},{8,9},{9,10},{10,1... | collective-permute-start | bytes 1572872 | tf_op jit(solution)/shard_map/ppermute | solution.py:976
  78.5 27.4 %collective-permute-start.4 = (bf16[1,256,1152]{2,1,0:T(8,128)(2,1)}, bf16[1,256,1152]{2,1,0:T(8,128)(2,1)}, u32[]{:S(2)}, u32[]{:S(2)}) collective-permute-start(bf16[1,256,1152]{2,1,0:T(8,128)(2,1)} %pad_maximum_fusion.1.x_ref), channel_id=1, source_target_pairs={{0,1},{1,2},{2,3},{3,0},{4,5},{5,6},{6,7},{7,4},{8,9},{9,10},{10,1... | collective-permute-start | bytes 1769480 | tf_op jit(solution)/shard_map/ppermute | solution.py:976
  78.6 28.4 %collective-permute-start.5 = (bf16[1,256,1152]{2,1,0:T(8,128)(2,1)}, bf16[1,256,1152]{2,1,0:T(8,128)(2,1)}, u32[]{:S(2)}, u32[]{:S(2)}) collective-permute-start(bf16[1,256,1152]{2,1,0:T(8,128)(2,1)} %pad_maximum_fusion.1.x_ref), channel_id=1, source_target_pairs={{0,3},{1,0},{2,1},{3,2},{4,7},{5,4},{6,5},{7,6},{8,11},{9,8},{10,9... | collective-permute-start | bytes 1769480 | tf_op jit(solution)/shard_map/ppermute | solution.py:976
  112.9 34.1 %collective-permute-start.9 = (bf16[512,256]{1,0:T(8,128)(2,1)S(1)}, bf16[512,256]{1,0:T(8,128)(2,1)S(1)}, u32[]{:S(2)}, u32[]{:S(2)}) collective-permute-start(bf16[512,256]{1,0:T(8,128)(2,1)S(1)} %get-tuple-element.261), channel_id=1, source_target_pairs={{0,2},{1,3},{2,0},{3,1},{4,6},{5,7},{6,4},{7,5},{8,10},{9,11},{10,... | collective-permute-start | bytes 786440 | tf_op jit(solution)/shard_map/ppermute | solution.py:976
  116.5 30.6 %collective-permute-start.10 = (bf16[512,256]{1,0:T(8,128)(2,1)S(1)}, bf16[512,256]{1,0:T(8,128)(2,1)S(1)}, u32[]{:S(2)}, u32[]{:S(2)}) collective-permute-start(bf16[512,256]{1,0:T(8,128)(2,1)S(1)} %get-tuple-element.260), channel_id=1, source_target_pairs={{0,3},{1,0},{2,1},{3,2},{4,7},{5,4},{6,5},{7,6},{8,11},{9,8},{10,9... | collective-permute-start | bytes 786440 | tf_op jit(solution)/shard_map/ppermute | solution.py:976
  207.5 335.7 %reduce-scatter.5.cloned.1.call-start = ((), (), s32[]{:S(2)}) async-start(), calls=%async_computation.3 | async-start | bytes 2621440 | tf_op jit(solution)/shard_map/reduce_scatter | solution.py:1256
  259.6 36.1 %collective-permute-start.11 = (bf16[1,512,256]{2,1,0:T(8,128)(2,1)}, bf16[1,512,256]{2,1,0:T(8,128)(2,1)S(1)}, u32[]{:S(2)}, u32[]{:S(2)}) collective-permute-start(bf16[1,512,256]{2,1,0:T(8,128)(2,1)} %get-tuple-element.258), channel_id=1, source_target_pairs={{0,1},{1,2},{2,3},{3,0},{4,5},{5,6},{6,7},{7,4},{8,9},{9,10},{10,1... | collective-permute-start | bytes 786440 | tf_op jit(solution)/shard_map/ppermute | solution.py:976
  259.6 36.1 %collective-permute-start.12 = (bf16[1,512,256]{2,1,0:T(8,128)(2,1)}, bf16[1,512,256]{2,1,0:T(8,128)(2,1)S(1)}, u32[]{:S(2)}, u32[]{:S(2)}) collective-permute-start(bf16[1,512,256]{2,1,0:T(8,128)(2,1)} %get-tuple-element.257), channel_id=1, source_target_pairs={{0,2},{1,3},{2,0},{3,1},{4,6},{5,7},{6,4},{7,5},{8,10},{9,11},{10,... | collective-permute-start | bytes 786440 | tf_op jit(solution)/shard_map/ppermute | solution.py:976
  262.8 40.1 %collective-permute-start.13 = (bf16[1,512,256]{2,1,0:T(8,128)(2,1)}, bf16[1,512,256]{2,1,0:T(8,128)(2,1)}, u32[]{:S(2)}, u32[]{:S(2)}) collective-permute-start(bf16[1,512,256]{2,1,0:T(8,128)(2,1)} %get-tuple-element.256), channel_id=1, source_target_pairs={{0,3},{1,0},{2,1},{3,2},{4,7},{5,4},{6,5},{7,6},{8,11},{9,8},{10,9... | collective-permute-start | bytes 786440 | tf_op jit(solution)/shard_map/ppermute | solution.py:976
  326.1 65.1 %collective-permute-start.17 = (bf16[256,3072]{1,0:T(8,128)(2,1)}, bf16[256,3072]{1,0:T(8,128)(2,1)}, u32[]{:S(2)}, u32[]{:S(2)}) collective-permute-start(bf16[256,3072]{1,0:T(8,128)(2,1)} %get-tuple-element.230), channel_id=1, source_target_pairs={{0,16},{4,20},{8,24},{12,28},{16,0},{20,4},{24,8},{28,12},{1,17},{... | collective-permute-start | bytes 4718600 | tf_op jit(solution)/shard_map/ppermute | solution.py:940
  327.5 63.7 %collective-permute-start.16 = (bf16[256,2048]{1,0:T(8,128)(2,1)}, bf16[256,2048]{1,0:T(8,128)(2,1)}, u32[]{:S(2)}, u32[]{:S(2)}) collective-permute-start(bf16[256,2048]{1,0:T(8,128)(2,1)} %bitcast.28), channel_id=1, source_target_pairs={{0,8},{4,12},{8,0},{12,4},{16,24},{20,28},{24,16},{28,20},{1,9},{5... | collective-permute-start | bytes 3145736 | tf_op jit(solution)/shard_map/ppermute | solution.py:940
  327.5 25.6 %collective-permute-start.20 = (bf16[1,3,512,128]{3,2,1,0:T(8,128)(2,1)}, bf16[1,3,512,128]{3,2,1,0:T(8,128)(2,1)S(1)}, u32[]{:S(2)}, u32[]{:S(2)}) collective-permute-start(bf16[1,3,512,128]{3,2,1,0:T(8,128)(2,1)} %get-tuple-element.196), channel_id=1, source_target_pairs={{0,1},{1,2},{2,3},{3,0},{4,5},{5,6},{6,7},{7,4},{8,9},{9,10},{10,1... | collective-permute-start | bytes 1179656 | tf_op jit(solution)/shard_map/ppermute | solution.py:976
  327.5 40.0 %collective-permute-start.21 = (bf16[1,3,512,128]{3,2,1,0:T(8,128)(2,1)}, bf16[1,3,512,128]{3,2,1,0:T(8,128)(2,1)S(1)}, u32[]{:S(2)}, u32[]{:S(2)}) collective-permute-start(bf16[1,3,512,128]{3,2,1,0:T(8,128)(2,1)} %get-tuple-element.197), channel_id=1, source_target_pairs={{0,2},{1,3},{2,0},{3,1},{4,6},{5,7},{6,4},{7,5},{8,10},{9,11},{10,... | collective-permute-start | bytes 1179656 | tf_op jit(solution)/shard_map/ppermute | solution.py:976
  327.6 61.4 %collective-permute-start.22 = (bf16[1,3,512,128]{3,2,1,0:T(8,128)(2,1)}, bf16[1,3,512,128]{3,2,1,0:T(8,128)(2,1)S(1)}, u32[]{:S(2)}, u32[]{:S(2)}) collective-permute-start(bf16[1,3,512,128]{3,2,1,0:T(8,128)(2,1)} %get-tuple-element.198), channel_id=1, source_target_pairs={{0,3},{1,0},{2,1},{3,2},{4,7},{5,4},{6,5},{7,6},{8,11},{9,8},{10,9... | collective-permute-start | bytes 1179656 | tf_op jit(solution)/shard_map/ppermute | solution.py:976
  389.7 69.3 %collective-permute-start.23 = (bf16[1,3,512,128]{3,2,1,0:T(8,128)(2,1)}, bf16[1,3,512,128]{3,2,1,0:T(8,128)(2,1)}, u32[]{:S(2)}, u32[]{:S(2)}) collective-permute-start(bf16[1,3,512,128]{3,2,1,0:T(8,128)(2,1)} %get-tuple-element.204), channel_id=1, source_target_pairs={{0,1},{1,2},{2,3},{3,0},{4,5},{5,6},{6,7},{7,4},{8,9},{9,10},{10,1... | collective-permute-start | bytes 1179656 | tf_op jit(solution)/shard_map/ppermute | solution.py:976
  389.7 69.3 %collective-permute-start.24 = (bf16[1,3,512,128]{3,2,1,0:T(8,128)(2,1)}, bf16[1,3,512,128]{3,2,1,0:T(8,128)(2,1)}, u32[]{:S(2)}, u32[]{:S(2)}) collective-permute-start(bf16[1,3,512,128]{3,2,1,0:T(8,128)(2,1)} %get-tuple-element.205), channel_id=1, source_target_pairs={{0,2},{1,3},{2,0},{3,1},{4,6},{5,7},{6,4},{7,5},{8,10},{9,11},{10,... | collective-permute-start | bytes 1179656 | tf_op jit(solution)/shard_map/ppermute | solution.py:976
  389.7 69.3 %collective-permute-start.25 = (bf16[1,3,512,128]{3,2,1,0:T(8,128)(2,1)}, bf16[1,3,512,128]{3,2,1,0:T(8,128)(2,1)}, u32[]{:S(2)}, u32[]{:S(2)}) collective-permute-start(bf16[1,3,512,128]{3,2,1,0:T(8,128)(2,1)} %get-tuple-element.206), channel_id=1, source_target_pairs={{0,3},{1,0},{2,1},{3,2},{4,7},{5,4},{6,5},{7,6},{8,11},{9,8},{10,9... | collective-permute-start | bytes 1179656 | tf_op jit(solution)/shard_map/ppermute | solution.py:976
  411.1 50.4 %collective-permute-start.28 = (bf16[128,3072]{1,0:T(8,128)(2,1)}, bf16[128,3072]{1,0:T(8,128)(2,1)}, u32[]{:S(2)}, u32[]{:S(2)}) collective-permute-start(bf16[128,3072]{1,0:T(8,128)(2,1)} %get-tuple-element.235), channel_id=1, source_target_pairs={{0,8},{4,12},{8,0},{12,4},{16,24},{20,28},{24,16},{28,20},{1,9},{5... | collective-permute-start | bytes 2359304 | tf_op jit(solution)/shard_map/ppermute | solution.py:940
  487.7 33.1 %collective-permute-start.32 = (bf16[128,1536]{1,0:T(8,128)(2,1)S(1)}, bf16[128,1536]{1,0:T(8,128)(2,1)S(1)}, u32[]{:S(2)}, u32[]{:S(2)}) collective-permute-start(bf16[128,1536]{1,0:T(8,128)(2,1)S(1)} %copy-done.72), channel_id=1, source_target_pairs={{0,2},{1,3},{2,0},{3,1},{4,6},{5,7},{6,4},{7,5},{8,10},{9,11},{10,... | collective-permute-start | bytes 1179656 | tf_op jit(solution)/shard_map/ppermute | solution.py:976
  489.9 47.3 %collective-permute-start.33 = (bf16[128,1536]{1,0:T(8,128)(2,1)S(1)}, bf16[128,1536]{1,0:T(8,128)(2,1)S(1)}, u32[]{:S(2)}, u32[]{:S(2)}) collective-permute-start(bf16[128,1536]{1,0:T(8,128)(2,1)S(1)} %copy-done.71), channel_id=1, source_target_pairs={{0,1},{1,2},{2,3},{3,0},{4,5},{5,6},{6,7},{7,4},{8,9},{9,10},{10,1... | collective-permute-start | bytes 1179656 | tf_op jit(solution)/shard_map/ppermute | solution.py:976
  490.4 48.7 %collective-permute-start.34 = (bf16[128,1536]{1,0:T(8,128)(2,1)S(1)}, bf16[128,1536]{1,0:T(8,128)(2,1)S(1)}, u32[]{:S(2)}, u32[]{:S(2)}) collective-permute-start(bf16[128,1536]{1,0:T(8,128)(2,1)S(1)} %copy-done.70), channel_id=1, source_target_pairs={{0,3},{1,0},{2,1},{3,2},{4,7},{5,4},{6,5},{7,6},{8,11},{9,8},{10,9... | collective-permute-start | bytes 1179656 | tf_op jit(solution)/shard_map/ppermute | solution.py:976
  (94 other events, 1159.5 us)
Sparse Core Ops, SparseCore 0:
  207.7 243.4 reduce-scatter.2
  461.4 68.1 reduce-scatter.4
